TPU v7x, 256 devices: a whole 4x4x8 slice. The times are simulated.
256 devices in a mesh: seq: 32 (over z, x), head: 8 (over y, core).
Axes of the slice: x: 4, y: 4, z: 8, core: 2. Of those that a mesh axis runs over, the one named last changes fastest.
Arguments:
- queries: bfloat16 [32768, 4096], P('seq', 'head'), may hold values from -6 to 6
- key_rows: bfloat16 [32768, 4096], P('seq', 'head'), may hold values from -6 to 6
- value_rows: bfloat16 [32768, 4096], P('seq', 'head'), may hold values from -6 to 6
- out_grad: bfloat16 [32768, 4096], P('seq', 'head'), may hold values from -6 to 6
- cache_states: bfloat16 [32, 32, 128, 128], P('seq', 'head'), may hold values from -96 to 96
- session_start: int32 [32], P('seq'), may hold values from 0 to 1024, as said below
- cache_owner: int32 [32], replicated, may hold values from 0 to 31, as said below
- probe_gate: float32 [32768], P('seq'), may hold values from 0.1 to 4.5
- steer_vector: bfloat16 [32, 128], P('head'), may hold values from -0.09375 to 0.09375
Outputs:
- grad_queries: bfloat16 [32768, 4096], P('seq', 'head')
- grad_keys: bfloat16 [32768, 4096], P('seq', 'head')
- grad_values: bfloat16 [32768, 4096], P('seq', 'head')
- grad_cache: bfloat16 [32, 32, 128, 128], P('seq', 'head')
- grad_steer: float32 [32, 128], P('head')
- grad_gate: float32 [32768], P('seq')
Inputs may be any that keep to these rules, and one draw needn't show every extreme that they name: session_start[b] is the position of the session beginning in block b, or 1024 where none does; it is 512 for every b with b % 4 == 3, so no session reaches across more than 5 blocks. `cache_owner`: a permutation of the slots.
All inputs are finite; a program needn't handle non-finite values.
Results may differ from a plain program's by a relative error of at most 0.007.
Values may be sent and summed in bfloat16 or wider, within the bound.
No kernel may reach another device: no remote copies, remote signals or barrier semaphores. Data moves between devices by JAX's collectives and lax.ppermute only.
A program may use at most 128 MiB of HBM per device.

v0:
```python
import math

import jax
import jax.numpy as jnp
from jax import lax
from jax.sharding import PartitionSpec as P

DK = 128
DV = 128


def prefix(part, axis, combine, identity, reverse):
    count = lax.axis_size(axis)
    place = lax.axis_index(axis)
    ahead = count - 1 - place if reverse else place
    gathered = jax.tree.map(lambda a: lax.all_gather(a, axis), part)
    state = jax.tree.map(lambda a, e: jnp.zeros_like(a) + jnp.asarray(e, a.dtype), part, identity)

    def one(turn, state):
        source = count - 1 - turn if reverse else turn
        return combine(
            state, jax.tree.map(lambda a: lax.dynamic_index_in_dim(a, source, 0, False), gathered)
        )

    return lax.fori_loop(0, ahead, one, state)


def pairwise_dot(left_rows, right_rows):
    return lax.dot_general(
        left_rows, right_rows, (((1,), (1,)), ((), ())), preferred_element_type=jnp.float32
    )


def leading_dot(left_rows, right_rows):
    return lax.dot_general(
        left_rows, right_rows, (((0,), (0,)), ((), ())), preferred_element_type=jnp.float32
    )


def combine_states(earlier_item, later_item):
    return (
        jnp.maximum(earlier_item[0], later_item[0]),
        jnp.where(later_item[0] > 0, later_item[1], earlier_item[1] + later_item[1]),
    )


def shards(
    queries,
    key_rows,
    value_rows,
    out_grad,
    cache_states,
    session_start,
    cache_owner,
    probe_gate,
    steer_vector,
):
    length = queries.shape[0]
    heads_here = steer_vector.shape[0]
    scaling = 1.0 / DK
    blocks_total = lax.axis_size("seq")
    block_index = lax.axis_index("seq")
    start_pos = session_start[0]
    reset_flag = (start_pos < length).astype(jnp.float32)
    positions = jnp.arange(length)
    before_start = positions < start_pos
    after_start = positions >= start_pos
    final_part = after_start | (start_pos >= length)
    causal = (positions[None, :] <= positions[:, None]) & (
        after_start[:, None] == after_start[None, :]
    )
    target = cache_owner[block_index]
    zero_state = jnp.zeros((heads_here, DK, DV), jnp.float32)
    shard_piece = lax.all_gather(cache_states, "seq", axis=0, tiled=True)
    slot_ids = jnp.arange(shard_piece.shape[0])
    weights = (slot_ids == target).astype(jnp.bfloat16)
    owned_state = lax.dot_general(
        weights, shard_piece, (((0,), (0,)), ((), ())), preferred_element_type=jnp.float32
    ).astype(jnp.bfloat16)
    query_heads = queries.reshape(length, heads_here, DK)
    key_heads = key_rows.reshape(length, heads_here, DK)
    value_heads = value_rows.reshape(length, heads_here, DV)
    grad_heads = out_grad.reshape(length, heads_here, DV)
    before_mask = before_start.astype(jnp.bfloat16)[:, None]
    after_mask = after_start.astype(jnp.bfloat16)[:, None]
    final_mask = final_part.astype(jnp.bfloat16)[:, None]
    kv_final = jnp.einsum(
        "thd,the->hde",
        key_heads * final_mask[:, :, None],
        value_heads,
        preferred_element_type=jnp.float32,
    )
    tail_state = jnp.where(reset_flag > 0, owned_state.astype(jnp.float32) + kv_final, kv_final)
    head_state = scaling * jnp.einsum(
        "thd,the->hde",
        query_heads * before_mask[:, :, None],
        grad_heads,
        preferred_element_type=jnp.float32,
    )
    start_state = scaling * jnp.einsum(
        "thd,the->hde",
        query_heads * after_mask[:, :, None],
        grad_heads,
        preferred_element_type=jnp.float32,
    )
    identity = (jnp.zeros((), jnp.float32), zero_state)
    entering = prefix((reset_flag, tail_state), "seq", combine_states, identity, False)[1]
    leaving = prefix((reset_flag, head_state), "seq", combine_states, identity, True)[1]
    start_grad = jnp.where(reset_flag > 0, start_state + leaving, 0.0).astype(jnp.bfloat16)
    slot_ids = jnp.arange(lax.axis_size("seq") * 1)
    weights = (slot_ids == target).astype(jnp.float32)
    grad_cache = lax.psum_scatter(
        (weights[:, None, None, None] * start_grad.astype(jnp.float32)[None]).astype(jnp.bfloat16),
        "seq",
        scatter_dimension=0,
        tiled=True,
    )
    entering_low = entering.astype(jnp.bfloat16)
    leaving_low = leaving.astype(jnp.bfloat16)
    query_grads = []
    key_grads = []
    value_grads = []
    for head_index in range(heads_here):
        query_head = queries[:, head_index * DK : (head_index + 1) * DK]
        key_head = key_rows[:, head_index * DK : (head_index + 1) * DK]
        value_head = value_rows[:, head_index * DV : (head_index + 1) * DV]
        grad_head = out_grad[:, head_index * DV : (head_index + 1) * DV]
        grad_scores = jnp.where(causal, scaling * pairwise_dot(grad_head, value_head), 0.0).astype(
            jnp.bfloat16
        )
        key_scores = jnp.where(causal, scaling * pairwise_dot(query_head, key_head), 0.0).astype(
            jnp.bfloat16
        )
        inter_query = pairwise_dot(grad_head * before_mask, entering_low[head_index])
        inter_query = inter_query + pairwise_dot(grad_head * after_mask, owned_state[head_index])
        grad_query = (
            jnp.dot(grad_scores, key_head, preferred_element_type=jnp.float32)
            + scaling * inter_query
        )
        grad_key = leading_dot(grad_scores, query_head) + pairwise_dot(
            value_head * final_mask, leaving_low[head_index]
        )
        grad_value = leading_dot(key_scores, grad_head) + jnp.dot(
            key_head * final_mask, leaving_low[head_index], preferred_element_type=jnp.float32
        )
        query_grads.append(grad_query.astype(jnp.bfloat16))
        key_grads.append(grad_key.astype(jnp.bfloat16))
        value_grads.append(grad_value.astype(jnp.bfloat16))
    grad_queries = jnp.concatenate(query_grads, axis=1)
    grad_keys = jnp.concatenate(key_grads, axis=1)
    grad_values = jnp.concatenate(value_grads, axis=1)
    steer_part = jnp.einsum("t,tc->c", probe_gate, out_grad, preferred_element_type=jnp.float32)
    grad_steer = lax.psum(steer_part, "seq").reshape(heads_here, DV) / math.sqrt(
        length * blocks_total
    )
    gate_part = jnp.dot(out_grad, steer_vector.reshape(-1), preferred_element_type=jnp.float32)
    grad_gate = lax.psum(gate_part, "head")
    return (grad_queries, grad_keys, grad_values, grad_cache, grad_steer, grad_gate)


def solution(mesh):
    in_specs = (
        P("seq", "head"),
        P("seq", "head"),
        P("seq", "head"),
        P("seq", "head"),
        P("seq", "head", None, None),
        P("seq"),
        P(),
        P("seq"),
        P("head", None),
    )
    out_specs = (
        P("seq", "head"),
        P("seq", "head"),
        P("seq", "head"),
        P("seq", "head", None, None),
        P("head", None),
        P("seq"),
    )
    return jax.shard_map(shards, mesh=mesh, in_specs=in_specs, out_specs=out_specs, check_vma=False)
```

profile of v0, /device:TPU:8, one launch (start us, length us, event | category | flops | bytes accessed | tf_op | source)
XLA Modules:
  0.0 521.7 jit_solution(7952977365945046856)
XLA Ops:
  8.6 1.5 copy.37
  10.1 2.8 convolution_multiply_fusion.1
  14.2 81.1 %all-gather.6.cloned.1.call-done = bf16[32,4,128,128]{3,2,1,0:T(8,128)(2,1)} async-done(((bf16[1,4,128,128]{3,2,1,0:T(8,128)(2,1)}), bf16[32,4,128,128]{3,2,1,0:T(8,128)(2,1)}) %all-gather.6.cloned.1.call-update) | async-done | bytes 4194320 | tf_op jit(solution)/shard_map/all_gather | solution.py:74
  95.3 5.4 %fusion = f32[1,4,128,128]{3,0,2,1:T(1,128)S(1)} fusion(bf16[32,4,128,128]{3,2,1,0:T(8,128)(2,1)} %all-gather.6.cloned.1.call-done, s32[]{:T(128)} %bitcast.7), kind=kOutput, calls=%fused_computation.3 | convolution fusion | flops 4194336 | bytes 4456452 | tf_op jit(solution)/shard_map/dot_general | solution.py:77
  100.8 1.1 add_select_fusion.2
  103.7 73.2 %all-reduce.1 = (f32[32]{0:T(128)S(1)}, f32[512]{0:T(512)S(1)}) all-reduce(f32[32]{0:T(128)S(1)} %dynamic-update-slice, f32[512]{0:T(512)S(1)} %bitcast.121), channel_id=1, replica_groups=mesh['seq'=32,'head'=8] {'seq'}, use_global_device_ids=true, to_apply=%add | all-reduce | flops 544 | bytes 4352
  177.2 11.4 %psum.15 = f32[1024]{0:T(1024)} all-reduce(f32[1024]{0:T(1024)S(1)} %bitcast.120), channel_id=1, replica_groups=mesh['seq'=32,'head'=8] {'head'}, use_global_device_ids=true, to_apply=%region_6.7 | all-reduce | flops 1024 | bytes 8192 | tf_op jit(solution)/shard_map/psum | solution.py:157
  189.3 1.8 select_convert_fusion.4
  191.2 1.3 copy-done.6
  192.5 2.2 fusion.66
  195.6 1.3 copy-done.4
  196.9 1.3 fusion.74
  199.0 1.3 copy-done.2
  200.4 1.3 fusion.78
  202.5 72.2 %while.27 = (s32[]{:T(128)}, f32[4,128,128]{2,1,0:T(8,128)S(1)}, s32[]{:T(128)}, f32[32]{0:T(128)S(1)}, f32[32,4,128,128]{3,2,1,0:T(8,128)}, /*index=5*/s32[]{:T(128)}, s32[]{:T(128)}, s32[]{:T(128)}, s32[]{:T(128)}, f32[1]{0:T(128)}) while((s32[]{:T(128)}, f32[4,128,128]{2,1,0:T(8,128)S(1)}, s32[]{:T(128)}, f32[32]{0:T(128)S(1)}, ...), condition=%wide.region_3.4_spmd, body=%wide.region_2.3_spmd.sunk | while | flops 131079 | bytes 786613 | solution.py:25
  203.8 1.1 add_select_fusion.6
  206.1 1.1 add_select_fusion.6
  213.1 1.1 add_select_fusion.6
  217.7 1.1 add_select_fusion.6
  224.7 1.1 add_select_fusion.6
  231.7 1.1 add_select_fusion.6
  245.6 1.1 add_select_fusion.6
  252.5 1.1 add_select_fusion.6
  254.9 1.1 add_select_fusion.6
  257.2 1.1 add_select_fusion.6
  266.5 1.1 add_select_fusion.6
  268.8 1.1 add_select_fusion.6
  271.1 1.1 add_select_fusion.6
  273.5 1.1 add_select_fusion.6
  274.7 1.7 fusion.26
  276.4 3.1 multiply_convert_fusion
  280.1 2.3 fusion.70
  282.4 3.0 fusion.3
  285.5 3.0 fusion.4
  288.5 3.0 fusion.5
  291.5 3.0 fusion.6
  294.6 1.6 fusion.18
  296.2 1.5 fusion.17
  297.7 1.5 fusion.16
  299.3 1.5 fusion.15
  301.9 2.3 copy.32
  304.1 1.5 fusion.14
  305.7 1.5 fusion.12
  307.2 1.5 fusion.11
  308.7 1.5 fusion.13
  311.3 2.3 copy.31
  320.5 1.3 copy.30
  321.8 193.4 %reduce-scatter.2.cloned.1.call-done = bf16[1,4,128,128]{3,2,1,0:T(8,128)(2,1)} async-done(((bf16[32,4,128,128]{3,2,1,0:T(8,128)(2,1)}), bf16[1,4,128,128]{3,2,1,0:T(8,128)(2,1)}) %reduce-scatter.2.cloned.1.call-update) | async-done | bytes 131088 | tf_op jit(solution)/shard_map/reduce_scatter | solution.py:112
  (132 shorter events, 52.9 us)
Async XLA Ops:
  7.2 96.2 %copy-start = (f32[1024]{0:T(1024)S(1)}, f32[1024]{0:T(1024)}, u32[]{:S(2)}) copy-start(f32[1024]{0:T(1024)} %param.20) | copy-start | bytes 12292
  7.2 5.8 %copy-start.8 = (bf16[1024,512]{1,0:T(8,128)(2,1)S(1)}, bf16[1024,512]{1,0:T(8,128)(2,1)}, u32[]{:S(2)}) copy-start(bf16[1024,512]{1,0:T(8,128)(2,1)} %param.14) | copy-start | bytes 3145732
  7.2 6.4 %copy-start.17 = (s32[32]{0:T(128)S(1)}, s32[32]{0:T(128)}, u32[]{:S(2)}) copy-start(s32[32]{0:T(128)} %param.19) | copy-start | bytes 388
  7.2 88.1 %all-gather.6.cloned.1.call-start = ((), (), s32[]{:S(2)}) async-start(), calls=%async_computation.1 | async-start | bytes 4325376 | tf_op jit(solution)/shard_map/all_gather | solution.py:74
  7.9 194.6 %all-gather.10.cloned.1.call-start = ((), (), s32[]{:S(2)}) async-start(), calls=%async_computation.4 | async-start | bytes 8650752 | tf_op jit(solution)/shard_map/all_gather | solution.py:16
  10.1 85.2 %copy-start.11 = (bf16[1024,512]{0,1:T(8,128)(2,1)}, bf16[1024,512]{0,1:T(8,128)(2,1)S(1)}, u32[]{:S(2)}) copy-start(bf16[1024,512]{0,1:T(8,128)(2,1)S(1)} %copy.37) | copy-start | bytes 3145732
  12.9 300.6 %all-gather.8.cloned.1.call-start = ((), (), s32[]{:S(2)}) async-start(), calls=%async_computation.3 | async-start | bytes 8650752 | tf_op jit(solution)/shard_map/all_gather | solution.py:16
  95.3 5.5 %copy-start.12 = (bf16[1024,512]{1,0:T(8,128)(2,1)S(1)}, bf16[1024,512]{1,0:T(8,128)(2,1)}, u32[]{:S(2)}) copy-start(bf16[1024,512]{1,0:T(8,128)(2,1)} %param.15) | copy-start | bytes 3145732
  95.3 6.7 %copy-start.16 = (bf16[4,128]{1,0:T(4,128)(2,1)S(1)}, bf16[4,128]{1,0:T(4,128)(2,1)}, u32[]{:S(2)}) copy-start(bf16[4,128]{1,0:T(4,128)(2,1)} %param.21) | copy-start | bytes 3076
  95.3 6.7 %copy-start.19 = (u32[256]{0:T(256)S(1)}, u32[256]{0:T(256)}, u32[]{:S(2)}) copy-start(u32[256]{0:T(256)} %constant.87) | copy-start | bytes 3076
  95.3 8.1 %copy-start.1 = (bf16[1024,512]{1,0:T(8,128)(2,1)S(1)}, bf16[1024,512]{1,0:T(8,128)(2,1)}, u32[]{:S(2)}) copy-start(bf16[1024,512]{1,0:T(8,128)(2,1)} %param.16) | copy-start | bytes 3145732
  100.8 88.5 %copy-start.14 = (bf16[4,128,128]{2,1,0:T(8,128)(2,1)}, bf16[4,128,128]{2,1,0:T(8,128)(2,1)S(1)}, u32[]{:S(2)}) copy-start(bf16[4,128,128]{2,1,0:T(8,128)(2,1)S(1)} %convert_element_type.128) | copy-start | bytes 393220
  102.0 413.2 %reduce-scatter.2.cloned.1.call-start = ((), (), s32[]{:S(2)}) async-start(), calls=%async_computation.2 | async-start | bytes 4325376 | tf_op jit(solution)/shard_map/reduce_scatter | solution.py:112
  189.3 5.4 %copy-start.13 = (bf16[1024,512]{1,0:T(8,128)(2,1)S(1)}, bf16[1024,512]{1,0:T(8,128)(2,1)}, u32[]{:S(2)}) copy-start(bf16[1024,512]{1,0:T(8,128)(2,1)} %param.15) | copy-start | bytes 3145732
  191.2 1.3 copy-start.6
  194.8 2.1 copy-start.10
  195.6 1.3 copy-start.4
  199.0 1.4 copy-start.2
  274.7 4.9 copy-start.18
  313.6 1.9 copy-start.15
  313.8 3.2 copy-start.7
  313.9 3.2 copy-start.9
  315.4 2.4 copy-start.5
  316.2 2.5 copy-start.3
Sparse Core Ops, SparseCore 0:
  10.6 84.6 all-gather.5
  98.5 95.9 all-gather.9
  197.0 95.3 all-gather.7
  296.8 218.3 reduce-scatter.1
where the time goes:
time: 524 us; the launch traced here: 522 us
  waiting for transfers between devices  275 us (52%)
  blocking collectives  84.6 us (16%)
  matrix products  53.9 us (10%)
  other arithmetic  39.3 us (7%)
  local copies, waits for them, and re-layouts  32.3 us (6%)
  loops' own time  21.4 us (4%)
  between operations  14.9 us (3%)
    reduce_scatter x1, waiting for transfers between devices, shards(): lax.psum_scatter((weights[:, None, None, None] * start_grad.astype(jnp.fl...  193 us
    all_gather x1, waiting for transfers between devices, shards(): shard_piece = lax.all_gather(cache_states, 'seq', axis=0, tiled=True)  81.1 us
    unnamed x1, blocking collectives  73.2 us
    select_n x31, other arithmetic, combine_states(): jnp.where(later_item[0] > 0, later_item[1], earlier_item[1] + later_item[1])  32.7 us
    another operation x2, loops' own time, prefix(): return lax.fori_loop(0, ahead, one, state)  21.4 us
    dot_general x8, matrix products, leading_dot(): lax.dot_general(left_rows, right_rows, (((0,), (0,)), ((), ())), preferre...  19.3 us
    dynamic_slice x31, local copies, waits for them, and re-layouts, one(): lax.dynamic_index_in_dim(a, source, 0, False)  18.3 us
    dot_general x16, matrix products, pairwise_dot(): lax.dot_general(left_rows, right_rows, (((1,), (1,)), ((), ())), preferre...  13.4 us
  transfers between devices with their start and end apart: 4, of which 2 were waited for; matrix products, arithmetic and copies ran while one was open for 23% of the time, Pallas kernels for 0%

commit v1 on v0

v1 whole, which is shorter than its diff:
```python
import functools
import math

import jax
import jax.numpy as jnp
from jax import lax
from jax.experimental import pallas as pl
from jax.experimental.pallas import tpu as pltpu
from jax.sharding import PartitionSpec as P

D = 128
PIECE = 16
STRIP = 256
F32 = jnp.float32
BF16 = jnp.bfloat16


def nt(a, b):
    return lax.dot_general(a, b, (((1,), (1,)), ((), ())), preferred_element_type=F32)


def nn(a, b):
    return lax.dot_general(a, b, (((1,), (0,)), ((), ())), preferred_element_type=F32)


def tn(a, b):
    return lax.dot_general(a, b, (((0,), (0,)), ((), ())), preferred_element_type=F32)


def row_masks(start, length):
    rows = lax.broadcasted_iota(jnp.int32, (length, D), 0)
    after = (rows >= start).astype(F32)
    before = 1.0 - after
    whole = jnp.where(start >= length, 1.0, 0.0).astype(F32)
    final = jnp.maximum(after, whole)
    return before.astype(BF16), after.astype(BF16), final.astype(BF16)


def sums_kernel(start_ref, q_ref, k_ref, v_ref, g_ref, c_ref, probe_ref, steer_ref, u_ref, gate_ref, acc_ref):
    head = pl.program_id(0)
    length = q_ref.shape[0]
    start = start_ref[0]
    before, after, final = row_masks(start, length)
    g = g_ref[...]
    kv = tn(k_ref[...], v_ref[...] * final)
    both = tn(q_ref[...], jnp.concatenate([g * before, g * after], axis=1))
    pieces = D // PIECE
    here = pl.ds(head * pieces, pieces)
    u_ref[here, 0:16, :] = kv.astype(BF16).reshape(pieces, PIECE, D)
    u_ref[here, 16:32, :] = both[:, :D].astype(BF16).reshape(pieces, PIECE, D)
    u_ref[here, 32:48, :] = both[:, D:].astype(BF16).reshape(pieces, PIECE, D)
    u_ref[here, 48:64, :] = c_ref[0, 0].reshape(pieces, PIECE, D)

    probe = probe_ref[...]
    high = probe.astype(BF16)
    low = (probe - high.astype(F32)).astype(BF16)
    steer_sum = nn(high, g) + nn(low, g)
    which = lax.broadcasted_iota(jnp.int32, (8, D), 0) == head
    steer_rows = jnp.where(which, jnp.broadcast_to(steer_sum, (8, D)), 0.0)
    vector = jnp.where(which, steer_ref[...], 0.0).astype(BF16)
    gate_rows = nt(vector, g)
    gate_sum = jnp.sum(gate_rows, axis=0, keepdims=True)

    @pl.when(head == 0)
    def _():
        acc_ref[...] = steer_rows
        gate_ref[...] = gate_sum

    @pl.when(head > 0)
    def _():
        acc_ref[...] += steer_rows
        gate_ref[...] += gate_sum

    @pl.when(head == pl.num_programs(0) - 1)
    def _():
        total = acc_ref[...]
        total_high = total.astype(BF16).astype(F32)
        total_low = total - total_high
        rows = lax.broadcasted_iota(jnp.int32, (8, D), 0)
        spread = jnp.where(rows < 4, total_high, pltpu.roll(total_low, 4, 0))
        flag = jnp.where(start < length, 1.0, 0.0).astype(F32)
        tile = jnp.concatenate([spread, jnp.full((8, D), flag)], axis=0).astype(BF16)
        u_ref[:, 64:80, :] = jnp.broadcast_to(tile[None], (u_ref.shape[0], PIECE, D))


def block_sums(queries, key_rows, value_rows, out_grad, cache_states, session_start, probe_gate, steer_vector):
    length, width = queries.shape
    heads = width // D
    total = heads * D // PIECE
    steer_rows = jnp.zeros((8, D), F32).at[:heads].set(steer_vector.astype(F32))
    column = pl.BlockSpec((length, D), lambda h: (0, h))
    return pl.pallas_call(
        sums_kernel,
        grid=(heads,),
        in_specs=[
            pl.BlockSpec(memory_space=pltpu.SMEM),
            column,
            column,
            column,
            column,
            pl.BlockSpec((1, 1, D, D), lambda h: (0, h, 0, 0)),
            pl.BlockSpec((1, length), lambda h: (0, 0)),
            pl.BlockSpec((8, D), lambda h: (0, 0)),
        ],
        out_specs=[
            pl.BlockSpec((total, 80, D), lambda h: (0, 0, 0)),
            pl.BlockSpec((1, length), lambda h: (0, 0)),
        ],
        out_shape=[
            jax.ShapeDtypeStruct((total, 80, D), BF16),
            jax.ShapeDtypeStruct((1, length), F32),
        ],
        scratch_shapes=[pltpu.VMEM((8, D), F32)],
        compiler_params=pltpu.CompilerParams(vmem_limit_bytes=32 << 20),
        cost_estimate=pl.CostEstimate(
            flops=8 * heads * length * D * D, bytes_accessed=8 * length * width, transcendentals=0
        ),
        name="block_sums",
    )(
        session_start,
        queries,
        key_rows,
        value_rows,
        out_grad,
        cache_states,
        probe_gate.reshape(1, length),
        steer_rows,
    )


def scan_kernel(owner_ref, v_ref, w_ref, steer_ref):
    blocks = v_ref.shape[0]

    def flag_of(b):
        rows = v_ref[b, 64:80, :].astype(F32)[8:16]
        return jnp.concatenate([rows, rows], axis=0) > 0.5

    state = jnp.zeros((PIECE, D), F32)
    steer = jnp.zeros((8, D), F32)
    for b in range(blocks):
        cached = v_ref[owner_ref[b], 48:64, :]
        w_ref[b, 32:48, :] = cached
        w_ref[b, 0:16, :] = state.astype(BF16)
        added = v_ref[b, 0:16, :].astype(F32)
        state = added + jnp.where(flag_of(b), cached.astype(F32), state)
        steer = steer + v_ref[b, 64:80, :].astype(F32)[0:8]
    state = jnp.zeros((PIECE, D), F32)
    for b in reversed(range(blocks)):
        flag = flag_of(b)
        w_ref[b, 16:32, :] = state.astype(BF16)
        begun = (v_ref[b, 32:48, :].astype(F32) + state) * (1.0 / D)
        w_ref[owner_ref[b], 48:64, :] = jnp.where(flag, begun, 0.0).astype(BF16)
        state = v_ref[b, 16:32, :].astype(F32) + jnp.where(flag, 0.0, state)
    tokens = blocks * 1024
    steer_ref[...] = (steer + pltpu.roll(steer, 4, 0)) * (1.0 / math.sqrt(tokens))


def scan_blocks(owner, pieces):
    blocks = pieces.shape[0]
    vmem = pl.BlockSpec(memory_space=pltpu.VMEM)
    return pl.pallas_call(
        scan_kernel,
        in_specs=[pl.BlockSpec(memory_space=pltpu.SMEM), vmem],
        out_specs=[vmem, vmem],
        out_shape=[
            jax.ShapeDtypeStruct((blocks, 64, D), BF16),
            jax.ShapeDtypeStruct((8, D), F32),
        ],
        compiler_params=pltpu.CompilerParams(vmem_limit_bytes=32 << 20),
        name="scan_blocks",
    )(owner, pieces)


def grads_kernel(start_ref, q_ref, k_ref, v_ref, g_ref, w_ref, dq_ref, dk_ref, dv_ref, dc_ref):
    length = q_ref.shape[0]
    start = start_ref[0]
    before, after, final = row_masks(start, length)
    state = w_ref[...]
    enter = state[:, 0:16, :].reshape(D, D)
    leave = state[:, 16:32, :].reshape(D, D)
    cached = state[:, 32:48, :].reshape(D, D)
    dc_ref[0, 0] = state[:, 48:64, :].reshape(D, D)
    enter_cached = jnp.concatenate([enter, cached], axis=1)
    scale = 1.0 / D
    for i in range(length // STRIP):
        lo, hi = i * STRIP, (i + 1) * STRIP
        g = g_ref[lo:hi, :]
        s = lo + lax.broadcasted_iota(jnp.int32, (STRIP, hi), 0)
        t = lax.broadcasted_iota(jnp.int32, (STRIP, hi), 1)
        keep = (t <= s) & (t >= jnp.where(s >= start, start, 0))
        y = jnp.where(keep, nt(g, v_ref[0:hi, :]), 0.0).astype(BF16)
        inter = jnp.concatenate([g * before[lo:hi], g * after[lo:hi]], axis=1)
        dq = nn(y, k_ref[0:hi, :]) + nt(inter, enter_cached)
        dq_ref[lo:hi, :] = (dq * scale).astype(BF16)
    for j in range(length // STRIP):
        lo, hi = j * STRIP, (j + 1) * STRIP
        rest = length - lo
        k = k_ref[lo:hi, :]
        v = v_ref[lo:hi, :]
        t = lo + lax.broadcasted_iota(jnp.int32, (STRIP, rest), 0)
        s = lo + lax.broadcasted_iota(jnp.int32, (STRIP, rest), 1)
        keep = (t <= s) & (s < jnp.where(t < start, start, length))
        yt = jnp.where(keep, nt(v, g_ref[lo:length, :]), 0.0).astype(BF16)
        xt = jnp.where(keep, nt(k, q_ref[lo:length, :]), 0.0).astype(BF16)
        dk = nn(yt, q_ref[lo:length, :]) + nt(v * final[lo:hi], leave)
        dv = nn(xt, g_ref[lo:length, :]) + nn(k * final[lo:hi], leave)
        dk_ref[lo:hi, :] = (dk * scale).astype(BF16)
        dv_ref[lo:hi, :] = (dv * scale).astype(BF16)


def block_grads(queries, key_rows, value_rows, out_grad, session_start, states):
    length, width = queries.shape
    heads = width // D
    pieces = D // PIECE
    column = pl.BlockSpec((length, D), lambda h: (0, h))
    wide = jax.ShapeDtypeStruct((length, width), BF16)
    return pl.pallas_call(
        grads_kernel,
        grid=(heads,),
        in_specs=[
            pl.BlockSpec(memory_space=pltpu.SMEM),
            column,
            column,
            column,
            column,
            pl.BlockSpec((pieces, 64, D), lambda h: (h, 0, 0)),
        ],
        out_specs=[column, column, column, pl.BlockSpec((1, 1, D, D), lambda h: (0, h, 0, 0))],
        out_shape=[wide, wide, wide, jax.ShapeDtypeStruct((1, heads, D, D), BF16)],
        compiler_params=pltpu.CompilerParams(vmem_limit_bytes=48 << 20),
        cost_estimate=pl.CostEstimate(
            flops=10 * heads * length * length * D, bytes_accessed=14 * length * width, transcendentals=0
        ),
        name="block_grads",
    )(session_start, queries, key_rows, value_rows, out_grad, states)


def shards(
    queries,
    key_rows,
    value_rows,
    out_grad,
    cache_states,
    session_start,
    cache_owner,
    probe_gate,
    steer_vector,
):
    heads = steer_vector.shape[0]
    sent, gate = block_sums(
        queries, key_rows, value_rows, out_grad, cache_states, session_start, probe_gate, steer_vector
    )
    pieces = lax.all_to_all(sent, "seq", 0, 0, tiled=True)
    scanned, steer = scan_blocks(cache_owner, pieces)
    states = lax.all_to_all(scanned, "seq", 0, 0, tiled=True)
    grad_queries, grad_keys, grad_values, grad_cache = block_grads(
        queries, key_rows, value_rows, out_grad, session_start, states
    )
    grad_steer = steer[:heads]
    count = lax.axis_size("head")
    step = 1
    while step < count:
        gate = gate + lax.ppermute(gate, "head", [(i, i ^ step) for i in range(count)])
        step *= 2
    return (grad_queries, grad_keys, grad_values, grad_cache, grad_steer, gate.reshape(-1))


def solution(mesh):
    in_specs = (
        P("seq", "head"),
        P("seq", "head"),
        P("seq", "head"),
        P("seq", "head"),
        P("seq", "head", None, None),
        P("seq"),
        P(),
        P("seq"),
        P("head", None),
    )
    out_specs = (
        P("seq", "head"),
        P("seq", "head"),
        P("seq", "head"),
        P("seq", "head", None, None),
        P("head", None),
        P("seq"),
    )
    return jax.shard_map(shards, mesh=mesh, in_specs=in_specs, out_specs=out_specs, check_vma=False)
```

time: 524 us -> 79.7 us (0.15)
  waiting for transfers between devices: 275 us -> 12.8 us
  matrix products: 53.9 us -> 0 us
  blocking collectives: 84.6 us -> 31.4 us
  other arithmetic: 39.3 us -> 0.61 us
  local copies, waits for them, and re-layouts: 32.3 us -> 8.41 us
  loops' own time: 21.4 us -> 0 us
  Pallas kernels: 0 us -> 16.5 us
  between operations: 14.9 us -> 1.42 us
  starting transfers between devices: 0.16 us -> 7.97 us
    reduce_scatter x1 -> x0, waiting for transfers between devices: 193 us -> none  [shards(): lax.psum_scatter((weights[:, None, None, None] * start_grad.astype(jnp.fl...]
    all_gather x3 -> x0, waiting for transfers between devices: 81.1 us -> none  [the longest x1 81.1 us: shards(): shard_piece = lax.all_gather(cache_states, 'seq', axis=0, tiled=True)]
    unnamed x1 -> x0, blocking collectives: 73.2 us -> none
    dot_general x38 -> x0, matrix products: 53.9 us -> none  [the longest x8 19.3 us: leading_dot(): lax.dot_general(left_rows, right_rows, (((0,), (0,)), ((), ())), preferre...]
    select_n x31 -> x0, other arithmetic: 32.7 us -> none  [combine_states(): jnp.where(later_item[0] > 0, later_item[1], earlier_item[1] + later_item[1])]
    all_to_all x0 -> x1, blocking collectives: none -> 31.4 us  [shards(): pieces = lax.all_to_all(sent, 'seq', 0, 0, tiled=True)]
    another operation x2 -> x0, loops' own time: 21.4 us -> none  [prefix(): return lax.fori_loop(0, ahead, one, state)]
    dynamic_slice x32 -> x0, local copies, waits for them, and re-layouts: 18.9 us -> none  [the longest x31 18.3 us: one(): lax.dynamic_index_in_dim(a, source, 0, False)]
  transfers between devices with their start and end apart: 4 -> 4, of which waited for: 2 -> 4; matrix products, arithmetic and copies ran while one was open for 23% -> 1% of each run, Pallas kernels for 0% -> 0%
where the time goes in v1:
time: 79.7 us; the launch traced here: 79.2 us
  blocking collectives  31.4 us (39%)
  Pallas kernels  16.5 us (21%)
  waiting for transfers between devices  12.8 us (16%)
  local copies, waits for them, and re-layouts  8.41 us (11%)
  starting transfers between devices  7.97 us (10%)
  between operations  1.42 us (2%)
    all_to_all x1, blocking collectives, shards(): pieces = lax.all_to_all(sent, 'seq', 0, 0, tiled=True)  31.4 us
    pallas_call x1, Pallas kernels, block_grads(): pl.pallas_call(grads_kernel, grid=(heads,), in_specs=[pl.BlockSpec(memory...  13 us
    unnamed x26, local copies, waits for them, and re-layouts  7.83 us
    ppermute x3, waiting for transfers between devices, shards(): lax.ppermute(gate, 'head', [(i, i ^ step) for i in range(count)])  7.13 us
    all_to_all x1, waiting for transfers between devices, shards(): states = lax.all_to_all(scanned, 'seq', 0, 0, tiled=True)  5.68 us
    all_to_all x1, starting transfers between devices, shards(): states = lax.all_to_all(scanned, 'seq', 0, 0, tiled=True)  5.14 us
    pallas_call x1, Pallas kernels, block_sums(): pl.pallas_call(sums_kernel, grid=(heads,), in_specs=[pl.BlockSpec(memory_...  2.86 us
    ppermute x3, starting transfers between devices, shards(): lax.ppermute(gate, 'head', [(i, i ^ step) for i in range(count)])  2.84 us
  transfers between devices with their start and end apart: 4, of which 4 were waited for; matrix products, arithmetic and copies ran while one was open for 1% of the time, Pallas kernels for 0%

profile of v1, /device:TPU:8, one launch (start us, length us, event | category | flops | bytes accessed | tf_op | source)
XLA Modules:
  0.0 79.2 jit_solution(17950952043281749424)
XLA Ops:
  0.6 0.0 copy-start.12
  0.6 0.0 copy-start.10
  1.3 0.0 copy-done.12
  1.3 0.0 copy-done.10
  1.3 0.0 copy-start
  1.4 1.2 %copy-done = bf16[1024,512]{1,0:T(8,128)(2,1)S(1)} copy-done((bf16[1024,512]{1,0:T(8,128)(2,1)S(1)}, bf16[1024,512]{1,0:T(8,128)(2,1)}, u32[]{:S(2)}) %copy-start) | copy-done | bytes 1048600
  2.6 0.0 copy-start.2
  2.6 1.2 %copy-done.2 = bf16[1024,512]{1,0:T(8,128)(2,1)S(1)} copy-done((bf16[1024,512]{1,0:T(8,128)(2,1)S(1)}, bf16[1024,512]{1,0:T(8,128)(2,1)}, u32[]{:S(2)}) %copy-start.2) | copy-done | bytes 1048600
  3.8 0.0 copy-start.4
  3.8 1.2 %copy-done.4 = bf16[1024,512]{1,0:T(8,128)(2,1)S(1)} copy-done((bf16[1024,512]{1,0:T(8,128)(2,1)S(1)}, bf16[1024,512]{1,0:T(8,128)(2,1)}, u32[]{:S(2)}) %copy-start.4) | copy-done | bytes 1048600
  5.0 0.0 copy-start.6
  5.0 1.2 %copy-done.6 = bf16[1024,512]{1,0:T(8,128)(2,1)S(1)} copy-done((bf16[1024,512]{1,0:T(8,128)(2,1)S(1)}, bf16[1024,512]{1,0:T(8,128)(2,1)}, u32[]{:S(2)}) %copy-start.6) | copy-done | bytes 1048600
  6.3 0.0 copy-start.9
  6.3 0.9 %copy-done.9 = bf16[1,4,128,128]{3,2,1,0:T(8,128)(2,1)S(1)} copy-done((bf16[1,4,128,128]{3,2,1,0:T(8,128)(2,1)S(1)}, bf16[1,4,128,128]{3,2,1,0:T(8,128)(2,1)}, u32[]{:S(2)}) %copy-start.9) | copy-done | bytes 131096
  7.2 0.0 copy-start.5
  7.2 2.9 %block_sums.1 = (bf16[32,80,128]{2,1,0:T(8,128)(2,1)S(1)}, f32[1,1024]{1,0:T(1,128)S(1)}) custom-call(s32[1]{0:T(128)S(6)} %copy.15.start_ref, bf16[1024,512]{1,0:T(8,128)(2,1)S(1)} %copy-done, bf16[1024,512]{1,0:T(8,128)(2,1)S(1)} %copy-done.2, bf16[1024,512]{1,0:T(8,128)(2,1)S(1)} %copy-done.4, bf16[1024,512]{1,0:T(8,128)(2,1)S(1)} %copy-done.6, ...), custom_call_target="tpu_custom_call" | custom-call | flops 536870912 | bytes 4194304 | tf_op jit(solution)/shard_map/block_sums/pallas_call | solution.py:92
  10.0 0.0 copy-start.11
  10.0 0.0 copy-start.3
  10.1 31.4 %all_to_all.10.v_ref = bf16[32,80,128]{2,1,0:T(8,128)(2,1)S(1)} all-to-all(bf16[32,80,128]{2,1,0:T(8,128)(2,1)S(1)} %get-tuple-element.26), channel_id=1, replica_groups=mesh['seq'=32,'head'=8] {'seq'}, dimensions={0} | all-to-all | bytes 1310720 | tf_op jit(solution)/shard_map/all_to_all | solution.py:253
  41.5 0.0 copy-done.11
  41.5 0.0 copy-start.1
  41.5 0.7 scan_blocks.1
  42.2 0.0 copy-start.8
  42.2 0.8 copy-done.8
  43.0 5.1 %all-to-all-start.1 = ((bf16[32,64,128]{2,1,0:T(8,128)(2,1)}), bf16[32,64,128]{2,1,0:T(8,128)(2,1)}, u32[]{:S(2)}, u32[]{:S(2)}) async-start(bf16[32,64,128]{2,1,0:T(8,128)(2,1)} %copy-done.8), calls=%async_computation.1 | async-start | bytes 1048576 | tf_op jit(solution)/shard_map/all_to_all | solution.py:255
  48.1 0.1 collective-permute-start
  48.2 1.2 %collective-permute-done = f32[1,1024]{1,0:T(1,128)S(1)} collective-permute-done((f32[1,1024]{1,0:T(1,128)S(1)}, f32[1,1024]{1,0:T(1,128)S(1)}, u32[]{:S(2)}, u32[]{:S(2)}) %collective-permute-start) | collective-permute-done | bytes 4128 | tf_op jit(solution)/shard_map/ppermute | solution.py:263
  49.4 0.4 collective-permute-start.1
  49.9 3.2 %collective-permute-done.1 = f32[1,1024]{1,0:T(1,128)S(1)} collective-permute-done((f32[1,1024]{1,0:T(1,128)S(1)}, f32[1,1024]{1,0:T(1,128)S(1)}, u32[]{:S(2)}, u32[]{:S(2)}) %collective-permute-start.1) | collective-permute-done | bytes 4128 | tf_op jit(solution)/shard_map/ppermute | solution.py:263
  53.0 2.3 %collective-permute-start.2 = (f32[1,1024]{1,0:T(1,128)S(1)}, f32[1,1024]{1,0:T(1,128)S(1)}, u32[]{:S(2)}, u32[]{:S(2)}) collective-permute-start(f32[1,1024]{1,0:T(1,128)S(1)} %add.14), channel_id=1, source_target_pairs={{0,4},{1,5},{2,6},{3,7},{4,0},{5,1},{6,2},{7,3},{8,12},{9,13},{10,... | collective-permute-start | bytes 12296 | tf_op jit(solution)/shard_map/ppermute | solution.py:263
  55.3 2.8 %collective-permute-done.2 = f32[1,1024]{1,0:T(1,128)S(1)} collective-permute-done((f32[1,1024]{1,0:T(1,128)S(1)}, f32[1,1024]{1,0:T(1,128)S(1)}, u32[]{:S(2)}, u32[]{:S(2)}) %collective-permute-start.2) | collective-permute-done | bytes 4128 | tf_op jit(solution)/shard_map/ppermute | solution.py:263
  58.1 0.6 add.15
  58.7 0.6 slice.19
  59.3 5.7 %all-to-all-done.1.w_ref = bf16[32,64,128]{2,1,0:T(8,128)(2,1)} async-done(((bf16[32,64,128]{2,1,0:T(8,128)(2,1)}), bf16[32,64,128]{2,1,0:T(8,128)(2,1)}, u32[]{:S(2)}, u32[]{:S(2)}) %all-to-all-start.1) | async-done | bytes 524320 | tf_op jit(solution)/shard_map/all_to_all | solution.py:255
  65.0 0.0 copy-done.5
  65.0 0.0 copy-done.3
  65.0 0.0 copy-done.1
  65.0 0.0 copy-start.7
  65.0 1.2 %copy-done.7 = bf16[1024,512]{1,0:T(8,128)(2,1)S(1)} copy-done((bf16[1024,512]{1,0:T(8,128)(2,1)S(1)}, bf16[1024,512]{1,0:T(8,128)(2,1)}, u32[]{:S(2)}) %copy-start.7) | copy-done | bytes 1048600
  66.2 13.0 %block_grads.1 = (bf16[1024,512]{1,0:T(8,128)(2,1)}, bf16[1024,512]{1,0:T(8,128)(2,1)}, bf16[1024,512]{1,0:T(8,128)(2,1)}, bf16[1,4,128,128]{3,2,1,0:T(8,128)(2,1)}) custom-call(s32[1]{0:T(128)S(6)} %copy.15.start_ref, bf16[1024,512]{1,0:T(8,128)(2,1)S(1)} %copy-done.1, bf16[1024,512]{1,0:T(8,128)(2,1)S(1)} %copy-done.3, bf16[1024,512]{1,0:T(8,128)(2,1)S(1)} %copy-done.5, ...), custom_call_target="tpu_custom_call" | custom-call | flops 5368709120 | bytes 7340032 | tf_op jit(solution)/shard_map/block_grads/pallas_call | solution.py:217
  (3 shorter events, 0.0 us)
Async XLA Ops:
  0.6 0.7 copy-start.12
  0.6 0.7 copy-start.10
  1.3 1.2 %copy-start = (bf16[1024,512]{1,0:T(8,128)(2,1)S(1)}, bf16[1024,512]{1,0:T(8,128)(2,1)}, u32[]{:S(2)}) copy-start(bf16[1024,512]{1,0:T(8,128)(2,1)} %q_ref.3) | copy-start | bytes 3145732
  2.6 1.2 %copy-start.2 = (bf16[1024,512]{1,0:T(8,128)(2,1)S(1)}, bf16[1024,512]{1,0:T(8,128)(2,1)}, u32[]{:S(2)}) copy-start(bf16[1024,512]{1,0:T(8,128)(2,1)} %k_ref.3) | copy-start | bytes 3145732
  3.8 1.2 %copy-start.4 = (bf16[1024,512]{1,0:T(8,128)(2,1)S(1)}, bf16[1024,512]{1,0:T(8,128)(2,1)}, u32[]{:S(2)}) copy-start(bf16[1024,512]{1,0:T(8,128)(2,1)} %v_ref.3) | copy-start | bytes 3145732
  5.0 1.2 %copy-start.6 = (bf16[1024,512]{1,0:T(8,128)(2,1)S(1)}, bf16[1024,512]{1,0:T(8,128)(2,1)}, u32[]{:S(2)}) copy-start(bf16[1024,512]{1,0:T(8,128)(2,1)} %g_ref.3) | copy-start | bytes 3145732
  6.3 0.9 %copy-start.9 = (bf16[1,4,128,128]{3,2,1,0:T(8,128)(2,1)S(1)}, bf16[1,4,128,128]{3,2,1,0:T(8,128)(2,1)}, u32[]{:S(2)}) copy-start(bf16[1,4,128,128]{3,2,1,0:T(8,128)(2,1)} %c_ref.1) | copy-start | bytes 393220
  7.2 57.8 %copy-start.5 = (bf16[1024,512]{1,0:T(8,128)(2,1)S(1)}, bf16[1024,512]{1,0:T(8,128)(2,1)}, u32[]{:S(2)}) copy-start(bf16[1024,512]{1,0:T(8,128)(2,1)} %v_ref.3) | copy-start | bytes 3145732
  10.0 31.5 %copy-start.11 = (s32[32]{0:T(128)S(1)}, s32[32]{0:T(128)}, u32[]{:S(2)}) copy-start(s32[32]{0:T(128)} %owner_ref.1) | copy-start | bytes 388
  10.0 55.0 %copy-start.3 = (bf16[1024,512]{1,0:T(8,128)(2,1)S(1)}, bf16[1024,512]{1,0:T(8,128)(2,1)}, u32[]{:S(2)}) copy-start(bf16[1024,512]{1,0:T(8,128)(2,1)} %k_ref.3) | copy-start | bytes 3145732
  41.5 23.5 %copy-start.1 = (bf16[1024,512]{1,0:T(8,128)(2,1)S(1)}, bf16[1024,512]{1,0:T(8,128)(2,1)}, u32[]{:S(2)}) copy-start(bf16[1024,512]{1,0:T(8,128)(2,1)} %q_ref.3) | copy-start | bytes 3145732
  42.2 0.8 %copy-start.8 = (bf16[32,64,128]{2,1,0:T(8,128)(2,1)}, bf16[32,64,128]{2,1,0:T(8,128)(2,1)S(1)}, u32[]{:S(2)}) copy-start(bf16[32,64,128]{2,1,0:T(8,128)(2,1)S(1)} %get-tuple-element.27) | copy-start | bytes 1572868
  43.0 22.0 %all-to-all-start.1 = ((bf16[32,64,128]{2,1,0:T(8,128)(2,1)}), bf16[32,64,128]{2,1,0:T(8,128)(2,1)}, u32[]{:S(2)}, u32[]{:S(2)}) async-start(bf16[32,64,128]{2,1,0:T(8,128)(2,1)} %copy-done.8), calls=%async_computation.1 | async-start | bytes 1048576 | tf_op jit(solution)/shard_map/all_to_all | solution.py:255
  48.1 1.3 %collective-permute-start = (f32[1,1024]{1,0:T(1,128)S(1)}, f32[1,1024]{1,0:T(1,128)S(1)}, u32[]{:S(2)}, u32[]{:S(2)}) collective-permute-start(f32[1,1024]{1,0:T(1,128)S(1)} %get-tuple-element.33), channel_id=1, source_target_pairs={{0,1},{1,0},{2,3},{3,2},{4,5},{5,4},{6,7},{7,6},{8,9},{9,8},{10,11... | collective-permute-start | bytes 12296 | tf_op jit(solution)/shard_map/ppermute | solution.py:263
  49.4 3.6 %collective-permute-start.1 = (f32[1,1024]{1,0:T(1,128)S(1)}, f32[1,1024]{1,0:T(1,128)S(1)}, u32[]{:S(2)}, u32[]{:S(2)}) collective-permute-start(f32[1,1024]{1,0:T(1,128)S(1)} %add.13), channel_id=1, source_target_pairs={{0,2},{1,3},{2,0},{3,1},{4,6},{5,7},{6,4},{7,5},{8,10},{9,11},{10,... | collective-permute-start | bytes 12296 | tf_op jit(solution)/shard_map/ppermute | solution.py:263
  53.0 5.1 %collective-permute-start.2 = (f32[1,1024]{1,0:T(1,128)S(1)}, f32[1,1024]{1,0:T(1,128)S(1)}, u32[]{:S(2)}, u32[]{:S(2)}) collective-permute-start(f32[1,1024]{1,0:T(1,128)S(1)} %add.14), channel_id=1, source_target_pairs={{0,4},{1,5},{2,6},{3,7},{4,0},{5,1},{6,2},{7,3},{8,12},{9,13},{10,... | collective-permute-start | bytes 12296 | tf_op jit(solution)/shard_map/ppermute | solution.py:263
  65.0 1.2 %copy-start.7 = (bf16[1024,512]{1,0:T(8,128)(2,1)S(1)}, bf16[1024,512]{1,0:T(8,128)(2,1)}, u32[]{:S(2)}) copy-start(bf16[1024,512]{1,0:T(8,128)(2,1)} %g_ref.3) | copy-start | bytes 3145732

commit v2 on v1

v2 whole, which is shorter than its diff:
```python
import functools
import math

import jax
import jax.numpy as jnp
from jax import lax
from jax.experimental import pallas as pl
from jax.experimental.pallas import tpu as pltpu
from jax.sharding import PartitionSpec as P

D = 128
PIECE = 16
STRIP = 256
VMEM_BYTES = 63 << 20 | 128 << 10
F32 = jnp.float32
BF16 = jnp.bfloat16


def nt(a, b):
    return lax.dot_general(a, b, (((1,), (1,)), ((), ())), preferred_element_type=F32)


def nn(a, b):
    return lax.dot_general(a, b, (((1,), (0,)), ((), ())), preferred_element_type=F32)


def tn(a, b):
    return lax.dot_general(a, b, (((0,), (0,)), ((), ())), preferred_element_type=F32)


def row_masks(start, length):
    rows = lax.broadcasted_iota(jnp.int32, (length, D), 0)
    after = (rows >= start).astype(F32)
    before = 1.0 - after
    whole = jnp.where(start >= length, 1.0, 0.0).astype(F32)
    final = jnp.maximum(after, whole)
    return before.astype(BF16), after.astype(BF16), final.astype(BF16)


def whole(space):
    return pl.BlockSpec(memory_space=space)


def sums_kernel(
    start_ref, q_any, k_any, v_any, g_any, c_any, probe_ref, steer_ref,
    u_any, gate_ref, q_ref, k_ref, v_ref, g_ref, u_ref, in_sem, c_sem, out_sem,
):
    heads, length, _ = q_ref.shape
    pieces = D // PIECE
    start = start_ref[0]

    def fetches(h):
        pairs = ((k_any, k_ref), (v_any, v_ref), (q_any, q_ref), (g_any, g_ref))
        return [
            pltpu.make_async_copy(far.at[:, h * D : (h + 1) * D], near.at[h], in_sem.at[n, h])
            for n, (far, near) in enumerate(pairs)
        ]

    cached = [
        pltpu.make_async_copy(
            c_any.at[0, h, n * PIECE : (n + 1) * PIECE, :], u_any.at[h * pieces + n, 48:64, :], c_sem.at[h * pieces + n]
        )
        for h in range(heads)
        for n in range(pieces)
    ]
    for h in range(heads):
        for copy in fetches(h):
            copy.start()
    for copy in cached:
        copy.start()

    before, after, final = row_masks(start, length)
    probe = probe_ref[...]
    high = probe.astype(BF16)
    low = (probe - high.astype(F32)).astype(BF16)
    rows = lax.broadcasted_iota(jnp.int32, (8, D), 0)
    flag = jnp.where(start < length, 1.0, 0.0).astype(F32)
    tile = jnp.full((8, D), flag)
    gate = jnp.zeros((heads, length), F32)
    steer = steer_ref[...].astype(F32)
    sent = []
    for h in range(heads):
        for copy in fetches(h):
            copy.wait()
        g = g_ref[h]
        kv = tn(k_ref[h], v_ref[h] * final)
        both = tn(q_ref[h], jnp.concatenate([g * before, g * after], axis=1))
        here = slice(h * pieces, (h + 1) * pieces)
        u_ref[here, 0:16, :] = kv.astype(BF16).reshape(pieces, PIECE, D)
        u_ref[here, 16:32, :] = both[:, :D].astype(BF16).reshape(pieces, PIECE, D)
        u_ref[here, 32:48, :] = both[:, D:].astype(BF16).reshape(pieces, PIECE, D)
        copy = pltpu.make_async_copy(u_ref.at[here, 0:48, :], u_any.at[here, 0:48, :], out_sem.at[h])
        copy.start()
        sent.append(copy)
        steer_sum = nn(high, g) + nn(low, g)
        tile = jnp.where(rows == h, jnp.broadcast_to(steer_sum, (8, D)), tile)
        vector = jnp.where(rows[:heads] == h, steer, 0.0).astype(BF16)
        gate = gate + nt(vector, g)
    gate_ref[...] = jnp.sum(gate, axis=0, keepdims=True)
    u_ref[:, 64:72, :] = jnp.broadcast_to(tile.astype(BF16)[None], (u_ref.shape[0], 8, D))
    copy = pltpu.make_async_copy(u_ref.at[:, 64:72, :], u_any.at[:, 64:72, :], out_sem.at[heads])
    copy.start()
    sent.append(copy)
    for copy in cached + sent:
        copy.wait()


def block_sums(queries, key_rows, value_rows, out_grad, cache_states, session_start, probe_gate, steer_vector):
    length, width = queries.shape
    heads = width // D
    total = heads * D // PIECE
    near = pltpu.VMEM((heads, length, D), BF16)
    hbm, vmem = whole(pltpu.HBM), whole(pltpu.VMEM)
    return pl.pallas_call(
        sums_kernel,
        in_specs=[whole(pltpu.SMEM), hbm, hbm, hbm, hbm, hbm, vmem, vmem],
        out_specs=[hbm, vmem],
        out_shape=[
            jax.ShapeDtypeStruct((total, 72, D), BF16),
            jax.ShapeDtypeStruct((1, length), F32),
        ],
        scratch_shapes=[
            near,
            near,
            near,
            near,
            pltpu.VMEM((total, 72, D), BF16),
            pltpu.SemaphoreType.DMA((4, heads)),
            pltpu.SemaphoreType.DMA((total,)),
            pltpu.SemaphoreType.DMA((heads + 1,)),
        ],
        compiler_params=pltpu.CompilerParams(vmem_limit_bytes=VMEM_BYTES),
        cost_estimate=pl.CostEstimate(
            flops=8 * heads * length * D * D, bytes_accessed=8 * length * width, transcendentals=0
        ),
        name="block_sums",
    )(
        session_start,
        queries,
        key_rows,
        value_rows,
        out_grad,
        cache_states,
        probe_gate.reshape(1, length),
        steer_vector,
    )


def scan_kernel(owner_ref, v_ref, w_ref, steer_ref):
    blocks = v_ref.shape[0]

    def extra(b):
        return v_ref[b, 64:72, :].astype(F32)

    def flag_of(b):
        row = extra(b)[4:5]
        return jnp.broadcast_to(row, (PIECE, D)) > 0.5

    state = jnp.zeros((PIECE, D), F32)
    steer = jnp.zeros((8, D), F32)
    for b in range(blocks):
        cached = v_ref[owner_ref[b], 48:64, :]
        w_ref[b, 32:48, :] = cached
        w_ref[b, 0:16, :] = state.astype(BF16)
        added = v_ref[b, 0:16, :].astype(F32)
        state = added + jnp.where(flag_of(b), cached.astype(F32), state)
        steer = steer + extra(b)
    state = jnp.zeros((PIECE, D), F32)
    for b in reversed(range(blocks)):
        flag = flag_of(b)
        w_ref[b, 16:32, :] = state.astype(BF16)
        begun = (v_ref[b, 32:48, :].astype(F32) + state) * (1.0 / D)
        w_ref[owner_ref[b], 48:64, :] = jnp.where(flag, begun, 0.0).astype(BF16)
        state = v_ref[b, 16:32, :].astype(F32) + jnp.where(flag, 0.0, state)
    tokens = blocks * 1024
    steer_ref[...] = steer[0 : steer_ref.shape[0]] * (1.0 / math.sqrt(tokens))


def scan_blocks(owner, pieces, heads):
    blocks = pieces.shape[0]
    vmem = whole(pltpu.VMEM)
    return pl.pallas_call(
        scan_kernel,
        in_specs=[whole(pltpu.SMEM), vmem],
        out_specs=[vmem, vmem],
        out_shape=[
            jax.ShapeDtypeStruct((blocks, 64, D), BF16),
            jax.ShapeDtypeStruct((heads, D), F32),
        ],
        compiler_params=pltpu.CompilerParams(vmem_limit_bytes=8 << 20),
        name="scan_blocks",
    )(owner, pieces)


def local_kernel(
    start_ref, q_any, k_any, v_any, g_any, pq_any, pk_any, pv_any,
    q_ref, k_ref, v_ref, g_ref, pq_ref, pk_ref, pv_ref, in_sem, out_sem,
):
    heads, length, _ = q_ref.shape
    start = start_ref[0]

    def fetches(h):
        pairs = ((g_any, g_ref), (v_any, v_ref), (k_any, k_ref), (q_any, q_ref))
        columns = pl.ds(pl.multiple_of(h * D, D), D)
        return [
            pltpu.make_async_copy(far.at[:, columns], near.at[h], in_sem.at[n, h])
            for n, (far, near) in enumerate(pairs)
        ]

    def returns(h):
        pairs = ((pq_ref, pq_any), (pk_ref, pk_any), (pv_ref, pv_any))
        return [
            pltpu.make_async_copy(near.at[h], far.at[h], out_sem.at[n, h])
            for n, (near, far) in enumerate(pairs)
        ]

    for h in range(heads):
        for copy in fetches(h):
            copy.start()

    @pl.loop(0, heads)
    def _(h):
        for copy in fetches(h):
            copy.wait()
        for i in range(length // STRIP):
            lo, hi = i * STRIP, (i + 1) * STRIP
            s = lo + lax.broadcasted_iota(jnp.int32, (STRIP, hi), 0)
            t = lax.broadcasted_iota(jnp.int32, (STRIP, hi), 1)
            keep = (t <= s) & (t >= jnp.where(s >= start, start, 0))
            y = jnp.where(keep, nt(g_ref[h, lo:hi, :], v_ref[h, 0:hi, :]), 0.0).astype(BF16)
            pq_ref[h, lo:hi, :] = nn(y, k_ref[h, 0:hi, :])
        for j in range(length // STRIP):
            lo, hi = j * STRIP, (j + 1) * STRIP
            rest = length - lo
            t = lo + lax.broadcasted_iota(jnp.int32, (STRIP, rest), 0)
            s = lo + lax.broadcasted_iota(jnp.int32, (STRIP, rest), 1)
            keep = (t <= s) & (s < jnp.where(t < start, start, length))
            yt = jnp.where(keep, nt(v_ref[h, lo:hi, :], g_ref[h, lo:length, :]), 0.0).astype(BF16)
            pk_ref[h, lo:hi, :] = nn(yt, q_ref[h, lo:length, :])
            xt = jnp.where(keep, nt(k_ref[h, lo:hi, :], q_ref[h, lo:length, :]), 0.0).astype(BF16)
            pv_ref[h, lo:hi, :] = nn(xt, g_ref[h, lo:length, :])
        for copy in returns(h):
            copy.start()

    for h in range(heads):
        for copy in returns(h):
            copy.wait()


def local_grads(session_start, queries, key_rows, value_rows, out_grad):
    length, width = queries.shape
    heads = width // D
    hbm = whole(pltpu.HBM)
    near = pltpu.VMEM((heads, length, D), BF16)
    sums = pltpu.VMEM((heads, length, D), F32)
    part = jax.ShapeDtypeStruct((heads, length, D), F32)
    return pl.pallas_call(
        local_kernel,
        in_specs=[whole(pltpu.SMEM), hbm, hbm, hbm, hbm],
        out_specs=[hbm, hbm, hbm],
        out_shape=[part, part, part],
        scratch_shapes=[near] * 4
        + [sums] * 3
        + [pltpu.SemaphoreType.DMA((4, heads)), pltpu.SemaphoreType.DMA((3, heads))],
        compiler_params=pltpu.CompilerParams(vmem_limit_bytes=VMEM_BYTES),
        cost_estimate=pl.CostEstimate(
            flops=16 * heads * length * length * D, bytes_accessed=20 * heads * length * D, transcendentals=0
        ),
        name="local_grads",
    )(session_start, queries, key_rows, value_rows, out_grad)


def state_kernel(
    start_ref, k_any, v_any, g_any, pq_any, pk_any, pv_any, w_ref,
    dq_any, dk_any, dv_any, dc_any,
    k_ref, v_ref, g_ref, pq_ref, pk_ref, pv_ref, dq_ref, dk_ref, dv_ref, in_sem, c_sem, out_sem,
):
    heads, length, _ = k_ref.shape
    pieces = D // PIECE
    start = start_ref[0]

    def fetches(h):
        columns = slice(h * D, (h + 1) * D)
        pairs = (
            (g_any.at[:, columns], g_ref.at[h]),
            (pq_any.at[h], pq_ref.at[h]),
            (v_any.at[:, columns], v_ref.at[h]),
            (pk_any.at[h], pk_ref.at[h]),
            (k_any.at[:, columns], k_ref.at[h]),
            (pv_any.at[h], pv_ref.at[h]),
        )
        return [pltpu.make_async_copy(far, near, in_sem.at[n, h]) for n, (far, near) in enumerate(pairs)]

    for h in range(heads):
        for copy in fetches(h):
            copy.start()
    copies = [
        pltpu.make_async_copy(
            w_ref.at[h * pieces + n, 48:64, :], dc_any.at[0, h, n * PIECE : (n + 1) * PIECE, :], c_sem.at[h * pieces + n]
        )
        for h in range(heads)
        for n in range(pieces)
    ]
    for copy in copies:
        copy.start()
    before, after, final = row_masks(start, length)
    scale = 1.0 / D
    for h in range(heads):
        for copy in fetches(h):
            copy.wait()
        here = slice(h * pieces, (h + 1) * pieces)
        enter = w_ref[here, 0:16, :].reshape(D, D)
        leave = w_ref[here, 16:32, :].reshape(D, D)
        cached = w_ref[here, 32:48, :].reshape(D, D)
        g = g_ref[h]
        inter = jnp.concatenate([g * before, g * after], axis=1)
        dq = pq_ref[h] + nt(inter, jnp.concatenate([enter, cached], axis=1))
        dq_ref[h] = (dq * scale).astype(BF16)
        dk = pk_ref[h] + nt(v_ref[h] * final, leave)
        dk_ref[h] = (dk * scale).astype(BF16)
        dv = pv_ref[h] + nn(k_ref[h] * final, leave)
        dv_ref[h] = (dv * scale).astype(BF16)
        for n, (near, far) in enumerate(((dq_ref, dq_any), (dk_ref, dk_any), (dv_ref, dv_any))):
            copy = pltpu.make_async_copy(near.at[h], far.at[:, h * D : (h + 1) * D], out_sem.at[n, h])
            copy.start()
            copies.append(copy)
    for copy in copies:
        copy.wait()


def state_grads(session_start, key_rows, value_rows, out_grad, parts, states):
    heads, length, _ = parts[0].shape
    total = heads * D // PIECE
    hbm = whole(pltpu.HBM)
    near = pltpu.VMEM((heads, length, D), BF16)
    sums = pltpu.VMEM((heads, length, D), F32)
    wide = jax.ShapeDtypeStruct((length, heads * D), BF16)
    return pl.pallas_call(
        state_kernel,
        in_specs=[whole(pltpu.SMEM)] + [hbm] * 6 + [whole(pltpu.VMEM)],
        out_specs=[hbm] * 4,
        out_shape=[wide, wide, wide, jax.ShapeDtypeStruct((1, heads, D, D), BF16)],
        scratch_shapes=[
            near,
            near,
            near,
            sums,
            sums,
            sums,
            near,
            near,
            near,
            pltpu.SemaphoreType.DMA((6, heads)),
            pltpu.SemaphoreType.DMA((total,)),
            pltpu.SemaphoreType.DMA((3, heads)),
        ],
        compiler_params=pltpu.CompilerParams(vmem_limit_bytes=VMEM_BYTES),
        cost_estimate=pl.CostEstimate(
            flops=8 * heads * length * D * D, bytes_accessed=20 * heads * length * D, transcendentals=0
        ),
        name="state_grads",
    )(session_start, key_rows, value_rows, out_grad, *parts, states)


def shards(
    queries,
    key_rows,
    value_rows,
    out_grad,
    cache_states,
    session_start,
    cache_owner,
    probe_gate,
    steer_vector,
):
    heads = steer_vector.shape[0]
    sent, gate = block_sums(
        queries, key_rows, value_rows, out_grad, cache_states, session_start, probe_gate, steer_vector
    )
    pieces = lax.all_to_all(sent, "seq", 0, 0, tiled=True)
    parts = local_grads(session_start, queries, key_rows, value_rows, out_grad)
    pieces, parts = lax.optimization_barrier((pieces, parts))
    scanned, grad_steer = scan_blocks(cache_owner, pieces, heads)
    states = lax.all_to_all(scanned, "seq", 0, 0, tiled=True)
    grad_queries, grad_keys, grad_values, grad_cache = state_grads(
        session_start, key_rows, value_rows, out_grad, parts, states
    )
    count = lax.axis_size("head")
    step = 1
    while step < count:
        gate = gate + lax.ppermute(gate, "head", [(i, i ^ step) for i in range(count)])
        step *= 2
    return (grad_queries, grad_keys, grad_values, grad_cache, grad_steer, gate.reshape(-1))


def solution(mesh):
    in_specs = (
        P("seq", "head"),
        P("seq", "head"),
        P("seq", "head"),
        P("seq", "head"),
        P("seq", "head", None, None),
        P("seq"),
        P(),
        P("seq"),
        P("head", None),
    )
    out_specs = (
        P("seq", "head"),
        P("seq", "head"),
        P("seq", "head"),
        P("seq", "head", None, None),
        P("head", None),
        P("seq"),
    )
    return jax.shard_map(shards, mesh=mesh, in_specs=in_specs, out_specs=out_specs, check_vma=False)
```

time: 79.7 us -> 70.3 us (0.88)
  blocking collectives: 31.4 us -> 0 us
  Pallas kernels: 16.5 us -> 28.8 us
  starting transfers between devices: 7.97 us -> 19 us
  local copies, waits for them, and re-layouts: 8.41 us -> 0.81 us
  waiting for transfers between devices: 12.8 us -> 19.5 us
    all_to_all x1 -> x0, blocking collectives: 31.4 us -> none  [shards(): pieces = lax.all_to_all(sent, 'seq', 0, 0, tiled=True)]
    pallas_call x3 -> x4, Pallas kernels: 16.5 us -> 28.8 us  [the longest x1 13 us: local_grads(): pl.pallas_call(local_kernel, in_specs=[whole(pltpu.SMEM), hbm, hbm, hbm,...]
    all_to_all x0 -> x1, starting transfers between devices: none -> 11.3 us  [shards(): pieces = lax.all_to_all(sent, 'seq', 0, 0, tiled=True)]
    unnamed x26 -> x6, local copies, waits for them, and re-layouts: 7.83 us -> 0.81 us
    all_to_all x0 -> x1, waiting for transfers between devices: none -> 5.95 us  [shards(): pieces = lax.all_to_all(sent, 'seq', 0, 0, tiled=True)]
  transfers between devices with their start and end apart: 4 -> 5, of which waited for: 4 -> 5; matrix products, arithmetic and copies ran while one was open for 1% -> 1% of each run, Pallas kernels for 0% -> 19%
where the time goes in v2:
time: 70.3 us; the launch traced here: 70 us
  Pallas kernels  28.8 us (41%)
  waiting for transfers between devices  19.5 us (28%)
  starting transfers between devices  19 us (27%)
  between operations  1.35 us (2%)
  local copies, waits for them, and re-layouts  0.81 us (1%)
    pallas_call x1, Pallas kernels, local_grads(): pl.pallas_call(local_kernel, in_specs=[whole(pltpu.SMEM), hbm, hbm, hbm,...  13 us
    all_to_all x1, starting transfers between devices, shards(): pieces = lax.all_to_all(sent, 'seq', 0, 0, tiled=True)  11.3 us
    pallas_call x1, Pallas kernels, state_grads(): pl.pallas_call(state_kernel, in_specs=[whole(pltpu.SMEM)] + [hbm] * 6 + [...  7.39 us
    ppermute x3, waiting for transfers between devices, shards(): lax.ppermute(gate, 'head', [(i, i ^ step) for i in range(count)])  7.13 us
    pallas_call x1, Pallas kernels, block_sums(): pl.pallas_call(sums_kernel, in_specs=[whole(pltpu.SMEM), hbm, hbm, hbm, h...  6.87 us
    all_to_all x1, waiting for transfers between devices, shards(): states = lax.all_to_all(scanned, 'seq', 0, 0, tiled=True)  6.4 us
    all_to_all x1, waiting for transfers between devices, shards(): pieces = lax.all_to_all(sent, 'seq', 0, 0, tiled=True)  5.95 us
    all_to_all x1, starting transfers between devices, shards(): states = lax.all_to_all(scanned, 'seq', 0, 0, tiled=True)  4.8 us
  transfers between devices with their start and end apart: 5, of which 5 were waited for; matrix products, arithmetic and copies ran while one was open for 1% of the time, Pallas kernels for 19%

profile of v2, /device:TPU:8, one launch (start us, length us, event | category | flops | bytes accessed | tf_op | source)
XLA Modules:
  0.0 70.0 jit_solution(17966132564150065656)
XLA Ops:
  1.3 6.9 %block_sums.1 = (bf16[32,72,128]{2,1,0:T(8,128)(2,1)}, f32[1,1024]{1,0:T(1,128)}) custom-call(s32[1]{0:T(128)S(6)} %copy.15.start_ref, bf16[1024,512]{1,0:T(8,128)(2,1)} %q_any.3, bf16[1024,512]{1,0:T(8,128)(2,1)} %k_any.5, bf16[1024,512]{1,0:T(8,128)(2,1)} %v_any.5, bf16[1024,512]{1,0:T(8,128)(2,1)} %g_any.5, bf16[1,4,128,128]{3,2,1,0:T(8,128)(2,1)} %c_any.1, ...), custom_call_target="tpu_custom_call" | custom-call | flops 536870912 | bytes 4194304 | tf_op jit(solution)/shard_map/block_sums/pallas_call | solution.py:114
  8.2 11.3 %all-to-all-start = ((bf16[32,72,128]{2,1,0:T(8,128)(2,1)}), bf16[32,72,128]{2,1,0:T(8,128)(2,1)S(1)}, u32[]{:S(2)}, u32[]{:S(2)}) async-start(bf16[32,72,128]{2,1,0:T(8,128)(2,1)} %get-tuple-element.21), calls=%async_computation | async-start | bytes 1179648 | tf_op jit(solution)/shard_map/all_to_all | solution.py:380
  19.5 0.0 copy-start
  19.5 0.0 copy-start.2
  19.5 13.0 %local_grads.1 = (f32[4,1024,128]{2,1,0:T(8,128)}, f32[4,1024,128]{2,1,0:T(8,128)}, f32[4,1024,128]{2,1,0:T(8,128)}) custom-call(s32[1]{0:T(128)S(6)} %copy.15.start_ref, bf16[1024,512]{1,0:T(8,128)(2,1)} %q_any.3, bf16[1024,512]{1,0:T(8,128)(2,1)} %k_any.5, bf16[1024,512]{1,0:T(8,128)(2,1)} %v_any.5, bf16[1024,512]{1,0:T(8,128)(2,1)} %g_any.5), custom_call_target="tpu_custom_call" | custom-call | flops 8589934592 | bytes 10485760 | tf_op jit(solution)/shard_map/local_grads/pallas_call | solution.py:257
  32.5 6.0 %all-to-all-done.v_ref = bf16[32,72,128]{2,1,0:T(8,128)(2,1)S(1)} async-done(((bf16[32,72,128]{2,1,0:T(8,128)(2,1)}), bf16[32,72,128]{2,1,0:T(8,128)(2,1)S(1)}, u32[]{:S(2)}, u32[]{:S(2)}) %all-to-all-start) | async-done | bytes 589856 | tf_op jit(solution)/shard_map/all_to_all | solution.py:380
  38.5 0.0 copy-done
  38.5 1.5 %scan_blocks.1 = (bf16[32,64,128]{2,1,0:T(8,128)(2,1)}, f32[4,128]{1,0:T(4,128)}) custom-call(s32[32]{0:T(128)S(1)} %copy-done, bf16[32,72,128]{2,1,0:T(8,128)(2,1)S(1)} %all-to-all-done.v_ref), custom_call_target="tpu_custom_call" | custom-call | tf_op jit(solution)/shard_map/scan_blocks/pallas_call | solution.py:182
  40.0 4.8 %all-to-all-start.1 = ((bf16[32,64,128]{2,1,0:T(8,128)(2,1)}), bf16[32,64,128]{2,1,0:T(8,128)(2,1)S(1)}, u32[]{:S(2)}, u32[]{:S(2)}) async-start(bf16[32,64,128]{2,1,0:T(8,128)(2,1)} %get-tuple-element.29), calls=%async_computation.1 | async-start | bytes 1048576 | tf_op jit(solution)/shard_map/all_to_all | solution.py:384
  44.8 0.0 copy-done.2
  44.8 0.1 collective-permute-start
  44.9 1.2 %collective-permute-done = f32[1,1024]{1,0:T(1,128)S(1)} collective-permute-done((f32[1,1024]{1,0:T(1,128)S(1)}, f32[1,1024]{1,0:T(1,128)S(1)}, u32[]{:S(2)}, u32[]{:S(2)}) %collective-permute-start) | collective-permute-done | bytes 4128 | tf_op jit(solution)/shard_map/ppermute | solution.py:391
  46.1 0.4 collective-permute-start.1
  46.5 3.2 %collective-permute-done.1 = f32[1,1024]{1,0:T(1,128)S(1)} collective-permute-done((f32[1,1024]{1,0:T(1,128)S(1)}, f32[1,1024]{1,0:T(1,128)S(1)}, u32[]{:S(2)}, u32[]{:S(2)}) %collective-permute-start.1) | collective-permute-done | bytes 4128 | tf_op jit(solution)/shard_map/ppermute | solution.py:391
  49.7 2.3 %collective-permute-start.2 = (f32[1,1024]{1,0:T(1,128)S(1)}, f32[1,1024]{1,0:T(1,128)S(1)}, u32[]{:S(2)}, u32[]{:S(2)}) collective-permute-start(f32[1,1024]{1,0:T(1,128)S(1)} %add.10), channel_id=1, source_target_pairs={{0,4},{1,5},{2,6},{3,7},{4,0},{5,1},{6,2},{7,3},{8,12},{9,13},{10,... | collective-permute-start | bytes 12296 | tf_op jit(solution)/shard_map/ppermute | solution.py:391
  52.0 2.8 %collective-permute-done.2 = f32[1,1024]{1,0:T(1,128)S(1)} collective-permute-done((f32[1,1024]{1,0:T(1,128)S(1)}, f32[1,1024]{1,0:T(1,128)S(1)}, u32[]{:S(2)}, u32[]{:S(2)}) %collective-permute-start.2) | collective-permute-done | bytes 4128 | tf_op jit(solution)/shard_map/ppermute | solution.py:391
  54.8 0.6 add.11
  55.4 6.4 %all-to-all-done.1.w_ref = bf16[32,64,128]{2,1,0:T(8,128)(2,1)S(1)} async-done(((bf16[32,64,128]{2,1,0:T(8,128)(2,1)}), bf16[32,64,128]{2,1,0:T(8,128)(2,1)S(1)}, u32[]{:S(2)}, u32[]{:S(2)}) %all-to-all-start.1) | async-done | bytes 524320 | tf_op jit(solution)/shard_map/all_to_all | solution.py:384
  61.8 0.0 copy-start.1
  61.8 0.8 %copy-done.1 = bf16[32,64,128]{2,1,0:T(8,128)(2,1)} copy-done((bf16[32,64,128]{2,1,0:T(8,128)(2,1)}, bf16[32,64,128]{2,1,0:T(8,128)(2,1)S(1)}, u32[]{:S(2)}) %copy-start.1) | copy-done | bytes 524312
  62.6 7.4 %state_grads.1 = (bf16[1024,512]{1,0:T(8,128)(2,1)}, bf16[1024,512]{1,0:T(8,128)(2,1)}, bf16[1024,512]{1,0:T(8,128)(2,1)}, bf16[1,4,128,128]{3,2,1,0:T(8,128)(2,1)}) custom-call(s32[1]{0:T(128)S(6)} %copy.15.start_ref, bf16[1024,512]{1,0:T(8,128)(2,1)} %k_any.5, bf16[1024,512]{1,0:T(8,128)(2,1)} %v_any.5, bf16[1024,512]{1,0:T(8,128)(2,1)} %g_any.5, ...), custom_call_target="tpu_custom_call" | custom-call | flops 536870912 | bytes 10485760 | tf_op jit(solution)/shard_map/state_grads/pallas_call | solution.py:338
  (2 shorter events, 0.0 us)
Async XLA Ops:
  8.2 30.3 %all-to-all-start = ((bf16[32,72,128]{2,1,0:T(8,128)(2,1)}), bf16[32,72,128]{2,1,0:T(8,128)(2,1)S(1)}, u32[]{:S(2)}, u32[]{:S(2)}) async-start(bf16[32,72,128]{2,1,0:T(8,128)(2,1)} %get-tuple-element.21), calls=%async_computation | async-start | bytes 1179648 | tf_op jit(solution)/shard_map/all_to_all | solution.py:380
  19.5 19.0 %copy-start = (s32[32]{0:T(128)S(1)}, s32[32]{0:T(128)}, u32[]{:S(2)}) copy-start(s32[32]{0:T(128)} %owner_ref.1) | copy-start | bytes 388
  19.5 25.3 %copy-start.2 = (f32[1,1024]{1,0:T(1,128)S(1)}, f32[1,1024]{1,0:T(1,128)}, u32[]{:S(2)}) copy-start(f32[1,1024]{1,0:T(1,128)} %get-tuple-element.35) | copy-start | bytes 12292
  40.0 21.8 %all-to-all-start.1 = ((bf16[32,64,128]{2,1,0:T(8,128)(2,1)}), bf16[32,64,128]{2,1,0:T(8,128)(2,1)S(1)}, u32[]{:S(2)}, u32[]{:S(2)}) async-start(bf16[32,64,128]{2,1,0:T(8,128)(2,1)} %get-tuple-element.29), calls=%async_computation.1 | async-start | bytes 1048576 | tf_op jit(solution)/shard_map/all_to_all | solution.py:384
  44.8 1.3 %collective-permute-start = (f32[1,1024]{1,0:T(1,128)S(1)}, f32[1,1024]{1,0:T(1,128)S(1)}, u32[]{:S(2)}, u32[]{:S(2)}) collective-permute-start(f32[1,1024]{1,0:T(1,128)S(1)} %copy-done.2), channel_id=1, source_target_pairs={{0,1},{1,0},{2,3},{3,2},{4,5},{5,4},{6,7},{7,6},{8,9},{9,8},{10,11... | collective-permute-start | bytes 12296 | tf_op jit(solution)/shard_map/ppermute | solution.py:391
  46.1 3.6 %collective-permute-start.1 = (f32[1,1024]{1,0:T(1,128)S(1)}, f32[1,1024]{1,0:T(1,128)S(1)}, u32[]{:S(2)}, u32[]{:S(2)}) collective-permute-start(f32[1,1024]{1,0:T(1,128)S(1)} %add.9), channel_id=1, source_target_pairs={{0,2},{1,3},{2,0},{3,1},{4,6},{5,7},{6,4},{7,5},{8,10},{9,11},{10,... | collective-permute-start | bytes 12296 | tf_op jit(solution)/shard_map/ppermute | solution.py:391
  49.7 5.1 %collective-permute-start.2 = (f32[1,1024]{1,0:T(1,128)S(1)}, f32[1,1024]{1,0:T(1,128)S(1)}, u32[]{:S(2)}, u32[]{:S(2)}) collective-permute-start(f32[1,1024]{1,0:T(1,128)S(1)} %add.10), channel_id=1, source_target_pairs={{0,4},{1,5},{2,6},{3,7},{4,0},{5,1},{6,2},{7,3},{8,12},{9,13},{10,... | collective-permute-start | bytes 12296 | tf_op jit(solution)/shard_map/ppermute | solution.py:391
  61.8 0.8 %copy-start.1 = (bf16[32,64,128]{2,1,0:T(8,128)(2,1)}, bf16[32,64,128]{2,1,0:T(8,128)(2,1)S(1)}, u32[]{:S(2)}) copy-start(bf16[32,64,128]{2,1,0:T(8,128)(2,1)S(1)} %all-to-all-done.1.w_ref) | copy-start | bytes 1572868

commit v3 on v2

--- a/solution.py
+++ b/solution.py
@@ -11,7 +11,9 @@
 D = 128
 PIECE = 16
 STRIP = 256
-VMEM_BYTES = 63 << 20 | 128 << 10
+VMEM_BYTES = 61 << 20
+STATE_BYTES = 48 << 20
+AHEAD = 2
 F32 = jnp.float32
 BF16 = jnp.bfloat16
 
@@ -56,18 +58,11 @@
             for n, (far, near) in enumerate(pairs)
         ]
 
-    cached = [
-        pltpu.make_async_copy(
-            c_any.at[0, h, n * PIECE : (n + 1) * PIECE, :], u_any.at[h * pieces + n, 48:64, :], c_sem.at[h * pieces + n]
-        )
-        for h in range(heads)
-        for n in range(pieces)
-    ]
-    for h in range(heads):
+    for h in range(AHEAD):
         for copy in fetches(h):
             copy.start()
-    for copy in cached:
-        copy.start()
+    cached = pltpu.make_async_copy(c_any, u_any.at[:, 48:64, :], c_sem)
+    cached.start()
 
     before, after, final = row_masks(start, length)
     probe = probe_ref[...]
@@ -82,6 +77,9 @@
     for h in range(heads):
         for copy in fetches(h):
             copy.wait()
+        if h + AHEAD < heads:
+            for copy in fetches(h + AHEAD):
+                copy.start()
         g = g_ref[h]
         kv = tn(k_ref[h], v_ref[h] * final)
         both = tn(q_ref[h], jnp.concatenate([g * before, g * after], axis=1))
@@ -101,7 +99,7 @@
     copy = pltpu.make_async_copy(u_ref.at[:, 64:72, :], u_any.at[:, 64:72, :], out_sem.at[heads])
     copy.start()
     sent.append(copy)
-    for copy in cached + sent:
+    for copy in [cached] + sent:
         copy.wait()
 
 
@@ -126,7 +124,7 @@
             near,
             pltpu.VMEM((total, 72, D), BF16),
             pltpu.SemaphoreType.DMA((4, heads)),
-            pltpu.SemaphoreType.DMA((total,)),
+            pltpu.SemaphoreType.DMA(()),
             pltpu.SemaphoreType.DMA((heads + 1,)),
         ],
         compiler_params=pltpu.CompilerParams(vmem_limit_bytes=VMEM_BYTES),
@@ -140,13 +138,13 @@
         key_rows,
         value_rows,
         out_grad,
-        cache_states,
+        cache_states.reshape(total, PIECE, D),
         probe_gate.reshape(1, length),
         steer_vector,
     )
 
 
-def scan_kernel(owner_ref, v_ref, w_ref, steer_ref):
+def scan_kernel(owner_ref, v_ref, w_any, steer_ref, w_ref, sem):
     blocks = v_ref.shape[0]
 
     def extra(b):
@@ -160,41 +158,47 @@
     steer = jnp.zeros((8, D), F32)
     for b in range(blocks):
         cached = v_ref[owner_ref[b], 48:64, :]
-        w_ref[b, 32:48, :] = cached
         w_ref[b, 0:16, :] = state.astype(BF16)
+        w_ref[b, 16:32, :] = cached
         added = v_ref[b, 0:16, :].astype(F32)
         state = added + jnp.where(flag_of(b), cached.astype(F32), state)
         steer = steer + extra(b)
+    first = pltpu.make_async_copy(w_ref.at[:, 0:32, :], w_any.at[:, 0:32, :], sem.at[0])
+    first.start()
     state = jnp.zeros((PIECE, D), F32)
     for b in reversed(range(blocks)):
         flag = flag_of(b)
-        w_ref[b, 16:32, :] = state.astype(BF16)
+        w_ref[b, 32:48, :] = state.astype(BF16)
         begun = (v_ref[b, 32:48, :].astype(F32) + state) * (1.0 / D)
         w_ref[owner_ref[b], 48:64, :] = jnp.where(flag, begun, 0.0).astype(BF16)
         state = v_ref[b, 16:32, :].astype(F32) + jnp.where(flag, 0.0, state)
+    second = pltpu.make_async_copy(w_ref.at[:, 32:64, :], w_any.at[:, 32:64, :], sem.at[1])
+    second.start()
     tokens = blocks * 1024
     steer_ref[...] = steer[0 : steer_ref.shape[0]] * (1.0 / math.sqrt(tokens))
+    first.wait()
+    second.wait()
 
 
 def scan_blocks(owner, pieces, heads):
     blocks = pieces.shape[0]
-    vmem = whole(pltpu.VMEM)
+    hbm, vmem = whole(pltpu.HBM), whole(pltpu.VMEM)
     return pl.pallas_call(
         scan_kernel,
         in_specs=[whole(pltpu.SMEM), vmem],
-        out_specs=[vmem, vmem],
+        out_specs=[hbm, vmem],
         out_shape=[
             jax.ShapeDtypeStruct((blocks, 64, D), BF16),
             jax.ShapeDtypeStruct((heads, D), F32),
         ],
-        compiler_params=pltpu.CompilerParams(vmem_limit_bytes=8 << 20),
+        scratch_shapes=[pltpu.VMEM((blocks, 64, D), BF16), pltpu.SemaphoreType.DMA((2,))],
+        compiler_params=pltpu.CompilerParams(vmem_limit_bytes=VMEM_BYTES),
         name="scan_blocks",
     )(owner, pieces)
 
 
 def local_kernel(
-    start_ref, q_any, k_any, v_any, g_any, pq_any, pk_any, pv_any,
-    q_ref, k_ref, v_ref, g_ref, pq_ref, pk_ref, pv_ref, in_sem, out_sem,
+    start_ref, q_any, k_any, v_any, g_any, part_any, q_ref, k_ref, v_ref, g_ref, part_ref, in_sem, out_sem
 ):
     heads, length, _ = q_ref.shape
     start = start_ref[0]
@@ -207,14 +211,10 @@
             for n, (far, near) in enumerate(pairs)
         ]
 
-    def returns(h):
-        pairs = ((pq_ref, pq_any), (pk_ref, pk_any), (pv_ref, pv_any))
-        return [
-            pltpu.make_async_copy(near.at[h], far.at[h], out_sem.at[n, h])
-            for n, (near, far) in enumerate(pairs)
-        ]
-
-    for h in range(heads):
+    def result(h):
+        return pltpu.make_async_copy(part_ref.at[:, h], part_any.at[:, h], out_sem.at[h])
+
+    for h in range(AHEAD):
         for copy in fetches(h):
             copy.start()
 
@@ -222,13 +222,19 @@
     def _(h):
         for copy in fetches(h):
             copy.wait()
+
+        @pl.when(h + AHEAD < heads)
+        def _():
+            for copy in fetches(h + AHEAD):
+                copy.start()
+
         for i in range(length // STRIP):
             lo, hi = i * STRIP, (i + 1) * STRIP
             s = lo + lax.broadcasted_iota(jnp.int32, (STRIP, hi), 0)
             t = lax.broadcasted_iota(jnp.int32, (STRIP, hi), 1)
             keep = (t <= s) & (t >= jnp.where(s >= start, start, 0))
             y = jnp.where(keep, nt(g_ref[h, lo:hi, :], v_ref[h, 0:hi, :]), 0.0).astype(BF16)
-            pq_ref[h, lo:hi, :] = nn(y, k_ref[h, 0:hi, :])
+            part_ref[0, h, lo:hi, :] = nn(y, k_ref[h, 0:hi, :]).astype(BF16)
         for j in range(length // STRIP):
             lo, hi = j * STRIP, (j + 1) * STRIP
             rest = length - lo
@@ -236,15 +242,13 @@
             s = lo + lax.broadcasted_iota(jnp.int32, (STRIP, rest), 1)
             keep = (t <= s) & (s < jnp.where(t < start, start, length))
             yt = jnp.where(keep, nt(v_ref[h, lo:hi, :], g_ref[h, lo:length, :]), 0.0).astype(BF16)
-            pk_ref[h, lo:hi, :] = nn(yt, q_ref[h, lo:length, :])
+            part_ref[1, h, lo:hi, :] = nn(yt, q_ref[h, lo:length, :]).astype(BF16)
             xt = jnp.where(keep, nt(k_ref[h, lo:hi, :], q_ref[h, lo:length, :]), 0.0).astype(BF16)
-            pv_ref[h, lo:hi, :] = nn(xt, g_ref[h, lo:length, :])
-        for copy in returns(h):
-            copy.start()
+            part_ref[2, h, lo:hi, :] = nn(xt, g_ref[h, lo:length, :]).astype(BF16)
+        result(h).start()
 
     for h in range(heads):
-        for copy in returns(h):
-            copy.wait()
+        result(h).wait()
 
 
 def local_grads(session_start, queries, key_rows, value_rows, out_grad):
@@ -252,16 +256,17 @@
     heads = width // D
     hbm = whole(pltpu.HBM)
     near = pltpu.VMEM((heads, length, D), BF16)
-    sums = pltpu.VMEM((heads, length, D), F32)
-    part = jax.ShapeDtypeStruct((heads, length, D), F32)
     return pl.pallas_call(
         local_kernel,
         in_specs=[whole(pltpu.SMEM), hbm, hbm, hbm, hbm],
-        out_specs=[hbm, hbm, hbm],
-        out_shape=[part, part, part],
+        out_specs=hbm,
+        out_shape=jax.ShapeDtypeStruct((3, heads, length, D), BF16),
         scratch_shapes=[near] * 4
-        + [sums] * 3
-        + [pltpu.SemaphoreType.DMA((4, heads)), pltpu.SemaphoreType.DMA((3, heads))],
+        + [
+            pltpu.VMEM((3, heads, length, D), BF16),
+            pltpu.SemaphoreType.DMA((4, heads)),
+            pltpu.SemaphoreType.DMA((heads,)),
+        ],
         compiler_params=pltpu.CompilerParams(vmem_limit_bytes=VMEM_BYTES),
         cost_estimate=pl.CostEstimate(
             flops=16 * heads * length * length * D, bytes_accessed=20 * heads * length * D, transcendentals=0
@@ -271,57 +276,39 @@
 
 
 def state_kernel(
-    start_ref, k_any, v_any, g_any, pq_any, pk_any, pv_any, w_ref,
-    dq_any, dk_any, dv_any, dc_any,
-    k_ref, v_ref, g_ref, pq_ref, pk_ref, pv_ref, dq_ref, dk_ref, dv_ref, in_sem, c_sem, out_sem,
+    start_ref, k_ref, v_ref, g_ref, part_any, w_ref,
+    dq_any, dk_any, dv_any, dc_any, part_ref, out_ref, in_sem, c_sem, out_sem,
 ):
-    heads, length, _ = k_ref.shape
+    _, heads, length, _ = part_ref.shape
     pieces = D // PIECE
     start = start_ref[0]
 
-    def fetches(h):
-        columns = slice(h * D, (h + 1) * D)
-        pairs = (
-            (g_any.at[:, columns], g_ref.at[h]),
-            (pq_any.at[h], pq_ref.at[h]),
-            (v_any.at[:, columns], v_ref.at[h]),
-            (pk_any.at[h], pk_ref.at[h]),
-            (k_any.at[:, columns], k_ref.at[h]),
-            (pv_any.at[h], pv_ref.at[h]),
-        )
-        return [pltpu.make_async_copy(far, near, in_sem.at[n, h]) for n, (far, near) in enumerate(pairs)]
+    def fetch(h):
+        return pltpu.make_async_copy(part_any.at[:, h], part_ref.at[:, h], in_sem.at[h])
 
     for h in range(heads):
-        for copy in fetches(h):
-            copy.start()
-    copies = [
-        pltpu.make_async_copy(
-            w_ref.at[h * pieces + n, 48:64, :], dc_any.at[0, h, n * PIECE : (n + 1) * PIECE, :], c_sem.at[h * pieces + n]
-        )
-        for h in range(heads)
-        for n in range(pieces)
-    ]
-    for copy in copies:
-        copy.start()
+        fetch(h).start()
+    copies = [pltpu.make_async_copy(w_ref.at[:, 48:64, :], dc_any, c_sem)]
+    copies[0].start()
     before, after, final = row_masks(start, length)
     scale = 1.0 / D
     for h in range(heads):
-        for copy in fetches(h):
-            copy.wait()
+        fetch(h).wait()
+        columns = slice(h * D, (h + 1) * D)
         here = slice(h * pieces, (h + 1) * pieces)
         enter = w_ref[here, 0:16, :].reshape(D, D)
-        leave = w_ref[here, 16:32, :].reshape(D, D)
-        cached = w_ref[here, 32:48, :].reshape(D, D)
-        g = g_ref[h]
+        cached = w_ref[here, 16:32, :].reshape(D, D)
+        leave = w_ref[here, 32:48, :].reshape(D, D)
+        g = g_ref[:, columns]
         inter = jnp.concatenate([g * before, g * after], axis=1)
-        dq = pq_ref[h] + nt(inter, jnp.concatenate([enter, cached], axis=1))
-        dq_ref[h] = (dq * scale).astype(BF16)
-        dk = pk_ref[h] + nt(v_ref[h] * final, leave)
-        dk_ref[h] = (dk * scale).astype(BF16)
-        dv = pv_ref[h] + nn(k_ref[h] * final, leave)
-        dv_ref[h] = (dv * scale).astype(BF16)
-        for n, (near, far) in enumerate(((dq_ref, dq_any), (dk_ref, dk_any), (dv_ref, dv_any))):
-            copy = pltpu.make_async_copy(near.at[h], far.at[:, h * D : (h + 1) * D], out_sem.at[n, h])
+        dq = part_ref[0, h].astype(F32) + nt(inter, jnp.concatenate([enter, cached], axis=1))
+        out_ref[0, h] = (dq * scale).astype(BF16)
+        dk = part_ref[1, h].astype(F32) + nt(v_ref[:, columns] * final, leave)
+        out_ref[1, h] = (dk * scale).astype(BF16)
+        dv = part_ref[2, h].astype(F32) + nn(k_ref[:, columns] * final, leave)
+        out_ref[2, h] = (dv * scale).astype(BF16)
+        for n, far in enumerate((dq_any, dk_any, dv_any)):
+            copy = pltpu.make_async_copy(out_ref.at[n, h], far.at[:, columns], out_sem.at[n, h])
             copy.start()
             copies.append(copy)
     for copy in copies:
@@ -329,37 +316,30 @@
 
 
 def state_grads(session_start, key_rows, value_rows, out_grad, parts, states):
-    heads, length, _ = parts[0].shape
+    _, heads, length, _ = parts.shape
     total = heads * D // PIECE
-    hbm = whole(pltpu.HBM)
-    near = pltpu.VMEM((heads, length, D), BF16)
-    sums = pltpu.VMEM((heads, length, D), F32)
+    hbm, vmem = whole(pltpu.HBM), whole(pltpu.VMEM)
+    near = pltpu.VMEM((3, heads, length, D), BF16)
     wide = jax.ShapeDtypeStruct((length, heads * D), BF16)
-    return pl.pallas_call(
+    *grads, grad_cache = pl.pallas_call(
         state_kernel,
-        in_specs=[whole(pltpu.SMEM)] + [hbm] * 6 + [whole(pltpu.VMEM)],
+        in_specs=[whole(pltpu.SMEM), vmem, vmem, vmem, hbm, vmem],
         out_specs=[hbm] * 4,
-        out_shape=[wide, wide, wide, jax.ShapeDtypeStruct((1, heads, D, D), BF16)],
+        out_shape=[wide, wide, wide, jax.ShapeDtypeStruct((total, PIECE, D), BF16)],
         scratch_shapes=[
             near,
             near,
-            near,
-            sums,
-            sums,
-            sums,
-            near,
-            near,
-            near,
-            pltpu.SemaphoreType.DMA((6, heads)),
-            pltpu.SemaphoreType.DMA((total,)),
+            pltpu.SemaphoreType.DMA((heads,)),
+            pltpu.SemaphoreType.DMA(()),
             pltpu.SemaphoreType.DMA((3, heads)),
         ],
-        compiler_params=pltpu.CompilerParams(vmem_limit_bytes=VMEM_BYTES),
+        compiler_params=pltpu.CompilerParams(vmem_limit_bytes=STATE_BYTES),
         cost_estimate=pl.CostEstimate(
             flops=8 * heads * length * D * D, bytes_accessed=20 * heads * length * D, transcendentals=0
         ),
         name="state_grads",
-    )(session_start, key_rows, value_rows, out_grad, *parts, states)
+    )(session_start, key_rows, value_rows, out_grad, parts, states)
+    return *grads, grad_cache.reshape(1, heads, D, D)
 
 
 def shards(

time: 70.3 us -> 69.1 us (0.983)
  Pallas kernels: 28.8 us -> 26.3 us
  local copies, waits for them, and re-layouts: 0.81 us -> 2.06 us
    pallas_call x1, Pallas kernels: 7.39 us -> 4.03 us  [state_grads(): pl.pallas_call(state_kernel, in_specs=[whole(pltpu.SMEM), vmem, vmem, vme...]
    unnamed x6 -> x10, local copies, waits for them, and re-layouts: 0.81 us -> 2.06 us
    pallas_call x1, Pallas kernels: 1.49 us -> 2.52 us  [scan_blocks(): pl.pallas_call(scan_kernel, in_specs=[whole(pltpu.SMEM), vmem], out_specs...]
where the time goes in v3:
time: 69.1 us; the launch traced here: 68.6 us
  Pallas kernels  26.3 us (38%)
  waiting for transfers between devices  19.4 us (28%)
  starting transfers between devices  19 us (27%)
  local copies, waits for them, and re-layouts  2.06 us (3%)
  between operations  1.37 us (2%)
    pallas_call x1, Pallas kernels, local_grads(): pl.pallas_call(local_kernel, in_specs=[whole(pltpu.SMEM), hbm, hbm, hbm,...  13.1 us
    all_to_all x1, starting transfers between devices, shards(): pieces = lax.all_to_all(sent, 'seq', 0, 0, tiled=True)  11.3 us
    ppermute x3, waiting for transfers between devices, shards(): lax.ppermute(gate, 'head', [(i, i ^ step) for i in range(count)])  7.13 us
    pallas_call x1, Pallas kernels, block_sums(): pl.pallas_call(sums_kernel, in_specs=[whole(pltpu.SMEM), hbm, hbm, hbm, h...  6.58 us
    all_to_all x1, waiting for transfers between devices, shards(): states = lax.all_to_all(scanned, 'seq', 0, 0, tiled=True)  6.4 us
    all_to_all x1, waiting for transfers between devices, shards(): pieces = lax.all_to_all(sent, 'seq', 0, 0, tiled=True)  5.84 us
    all_to_all x1, starting transfers between devices, shards(): states = lax.all_to_all(scanned, 'seq', 0, 0, tiled=True)  4.81 us
    pallas_call x1, Pallas kernels, state_grads(): pl.pallas_call(state_kernel, in_specs=[whole(pltpu.SMEM), vmem, vmem, vme...  4.03 us
  transfers between devices with their start and end apart: 5, of which 5 were waited for; matrix products, arithmetic and copies ran while one was open for 1% of the time, Pallas kernels for 19%

profile of v3, /device:TPU:8, one launch (start us, length us, event | category | flops | bytes accessed | tf_op | source)
XLA Modules:
  0.0 68.6 jit_solution(17236772012665206992)
XLA Ops:
  1.3 6.6 %block_sums.1 = (bf16[32,72,128]{2,1,0:T(8,128)(2,1)}, f32[1,1024]{1,0:T(1,128)}) custom-call(s32[1]{0:T(128)S(6)} %copy.15.start_ref, bf16[1024,512]{1,0:T(8,128)(2,1)} %q_any.3, bf16[1024,512]{1,0:T(8,128)(2,1)} %k_ref.1, bf16[1024,512]{1,0:T(8,128)(2,1)} %v_ref.1, bf16[1024,512]{1,0:T(8,128)(2,1)} %g_ref.1, bf16[32,16,128]{2,1,0:T(8,128)(2,1)} %bitcast.4, ...), custom_call_target="tpu_custom_call" | custom-call | flops 536870912 | bytes 4194304 | tf_op jit(solution)/shard_map/block_sums/pallas_call | solution.py:112
  7.9 11.3 %all-to-all-start = ((bf16[32,72,128]{2,1,0:T(8,128)(2,1)}), bf16[32,72,128]{2,1,0:T(8,128)(2,1)S(1)}, u32[]{:S(2)}, u32[]{:S(2)}) async-start(bf16[32,72,128]{2,1,0:T(8,128)(2,1)} %get-tuple-element.16), calls=%async_computation | async-start | bytes 1179648 | tf_op jit(solution)/shard_map/all_to_all | solution.py:360
  19.2 0.0 copy-start.4
  19.2 0.0 copy-start
  19.2 0.0 copy-start.1
  19.2 13.1 %local_grads.1.part_any = bf16[3,4,1024,128]{3,2,1,0:T(8,128)(2,1)} custom-call(s32[1]{0:T(128)S(6)} %copy.15.start_ref, bf16[1024,512]{1,0:T(8,128)(2,1)} %q_any.3, bf16[1024,512]{1,0:T(8,128)(2,1)} %k_ref.1, bf16[1024,512]{1,0:T(8,128)(2,1)} %v_ref.1, bf16[1024,512]{1,0:T(8,128)(2,1)} %g_ref.1), custom_call_target="tpu_custom_call" | custom-call | flops 8589934592 | bytes 10485760 | tf_op jit(solution)/shard_map/local_grads/pallas_call | solution.py:259
  32.4 5.8 %all-to-all-done.v_ref = bf16[32,72,128]{2,1,0:T(8,128)(2,1)S(1)} async-done(((bf16[32,72,128]{2,1,0:T(8,128)(2,1)}), bf16[32,72,128]{2,1,0:T(8,128)(2,1)S(1)}, u32[]{:S(2)}, u32[]{:S(2)}) %all-to-all-start) | async-done | bytes 589856 | tf_op jit(solution)/shard_map/all_to_all | solution.py:360
  38.2 0.0 copy-start.3
  38.2 0.8 %copy-done.3 = bf16[32,72,128]{2,1,0:T(8,128)(2,1)} copy-done((bf16[32,72,128]{2,1,0:T(8,128)(2,1)}, bf16[32,72,128]{2,1,0:T(8,128)(2,1)S(1)}, u32[]{:S(2)}) %copy-start.3) | copy-done | bytes 589848
  39.0 2.5 %scan_blocks.1 = (bf16[32,64,128]{2,1,0:T(8,128)(2,1)}, f32[4,128]{1,0:T(4,128)}) custom-call(s32[32]{0:T(128)} %owner_ref.1, bf16[32,72,128]{2,1,0:T(8,128)(2,1)} %copy-done.3), custom_call_target="tpu_custom_call" | custom-call | tf_op jit(solution)/shard_map/scan_blocks/pallas_call | solution.py:186
  41.5 4.8 %all-to-all-start.1 = ((bf16[32,64,128]{2,1,0:T(8,128)(2,1)}), bf16[32,64,128]{2,1,0:T(8,128)(2,1)S(1)}, u32[]{:S(2)}, u32[]{:S(2)}) async-start(bf16[32,64,128]{2,1,0:T(8,128)(2,1)} %get-tuple-element.19), calls=%async_computation.1 | async-start | bytes 1048576 | tf_op jit(solution)/shard_map/all_to_all | solution.py:364
  46.4 0.0 copy-done.4
  46.4 0.1 collective-permute-start
  46.5 1.2 %collective-permute-done = f32[1,1024]{1,0:T(1,128)S(1)} collective-permute-done((f32[1,1024]{1,0:T(1,128)S(1)}, f32[1,1024]{1,0:T(1,128)S(1)}, u32[]{:S(2)}, u32[]{:S(2)}) %collective-permute-start) | collective-permute-done | bytes 4128 | tf_op jit(solution)/shard_map/ppermute | solution.py:371
  47.6 0.4 collective-permute-start.1
  48.1 3.2 %collective-permute-done.1 = f32[1,1024]{1,0:T(1,128)S(1)} collective-permute-done((f32[1,1024]{1,0:T(1,128)S(1)}, f32[1,1024]{1,0:T(1,128)S(1)}, u32[]{:S(2)}, u32[]{:S(2)}) %collective-permute-start.1) | collective-permute-done | bytes 4128 | tf_op jit(solution)/shard_map/ppermute | solution.py:371
  51.2 2.3 %collective-permute-start.2 = (f32[1,1024]{1,0:T(1,128)S(1)}, f32[1,1024]{1,0:T(1,128)S(1)}, u32[]{:S(2)}, u32[]{:S(2)}) collective-permute-start(f32[1,1024]{1,0:T(1,128)S(1)} %add.10), channel_id=1, source_target_pairs={{0,4},{1,5},{2,6},{3,7},{4,0},{5,1},{6,2},{7,3},{8,12},{9,13},{10,... | collective-permute-start | bytes 12296 | tf_op jit(solution)/shard_map/ppermute | solution.py:371
  53.5 2.8 %collective-permute-done.2 = f32[1,1024]{1,0:T(1,128)S(1)} collective-permute-done((f32[1,1024]{1,0:T(1,128)S(1)}, f32[1,1024]{1,0:T(1,128)S(1)}, u32[]{:S(2)}, u32[]{:S(2)}) %collective-permute-start.2) | collective-permute-done | bytes 4128 | tf_op jit(solution)/shard_map/ppermute | solution.py:371
  56.4 0.6 add.11
  57.0 6.4 %all-to-all-done.1.w_ref = bf16[32,64,128]{2,1,0:T(8,128)(2,1)S(1)} async-done(((bf16[32,64,128]{2,1,0:T(8,128)(2,1)}), bf16[32,64,128]{2,1,0:T(8,128)(2,1)S(1)}, u32[]{:S(2)}, u32[]{:S(2)}) %all-to-all-start.1) | async-done | bytes 524320 | tf_op jit(solution)/shard_map/all_to_all | solution.py:364
  63.4 0.0 copy-done
  63.4 0.0 copy-done.1
  63.4 0.0 copy-start.2
  63.4 1.2 %copy-done.2 = bf16[1024,512]{1,0:T(8,128)(2,1)S(1)} copy-done((bf16[1024,512]{1,0:T(8,128)(2,1)S(1)}, bf16[1024,512]{1,0:T(8,128)(2,1)}, u32[]{:S(2)}) %copy-start.2) | copy-done | bytes 1048600
  64.6 4.0 %state_grads.1 = (bf16[1024,512]{1,0:T(8,128)(2,1)}, bf16[1024,512]{1,0:T(8,128)(2,1)}, bf16[1024,512]{1,0:T(8,128)(2,1)}, bf16[32,16,128]{2,1,0:T(8,128)(2,1)}) custom-call(s32[1]{0:T(128)S(6)} %copy.15.start_ref, bf16[1024,512]{1,0:T(8,128)(2,1)S(1)} %copy-done, bf16[1024,512]{1,0:T(8,128)(2,1)S(1)} %copy-done.1, bf16[1024,512]{1,0:T(8,128)(2,1)S(1)} %copy-done.2, ...), custom_call_target="tpu_custom_call" | custom-call | flops 536870912 | bytes 10485760 | tf_op jit(solution)/shard_map/state_grads/pallas_call | solution.py:324
  (2 shorter events, 0.0 us)
Async XLA Ops:
  7.9 30.3 %all-to-all-start = ((bf16[32,72,128]{2,1,0:T(8,128)(2,1)}), bf16[32,72,128]{2,1,0:T(8,128)(2,1)S(1)}, u32[]{:S(2)}, u32[]{:S(2)}) async-start(bf16[32,72,128]{2,1,0:T(8,128)(2,1)} %get-tuple-element.16), calls=%async_computation | async-start | bytes 1179648 | tf_op jit(solution)/shard_map/all_to_all | solution.py:360
  19.2 27.2 %copy-start.4 = (f32[1,1024]{1,0:T(1,128)S(1)}, f32[1,1024]{1,0:T(1,128)}, u32[]{:S(2)}) copy-start(f32[1,1024]{1,0:T(1,128)} %get-tuple-element.25) | copy-start | bytes 12292
  19.2 44.2 %copy-start = (bf16[1024,512]{1,0:T(8,128)(2,1)S(1)}, bf16[1024,512]{1,0:T(8,128)(2,1)}, u32[]{:S(2)}) copy-start(bf16[1024,512]{1,0:T(8,128)(2,1)} %k_ref.1) | copy-start | bytes 3145732
  19.2 44.1 %copy-start.1 = (bf16[1024,512]{1,0:T(8,128)(2,1)S(1)}, bf16[1024,512]{1,0:T(8,128)(2,1)}, u32[]{:S(2)}) copy-start(bf16[1024,512]{1,0:T(8,128)(2,1)} %v_ref.1) | copy-start | bytes 3145732
  38.2 0.8 %copy-start.3 = (bf16[32,72,128]{2,1,0:T(8,128)(2,1)}, bf16[32,72,128]{2,1,0:T(8,128)(2,1)S(1)}, u32[]{:S(2)}) copy-start(bf16[32,72,128]{2,1,0:T(8,128)(2,1)S(1)} %all-to-all-done.v_ref) | copy-start | bytes 1769476
  41.5 21.8 %all-to-all-start.1 = ((bf16[32,64,128]{2,1,0:T(8,128)(2,1)}), bf16[32,64,128]{2,1,0:T(8,128)(2,1)S(1)}, u32[]{:S(2)}, u32[]{:S(2)}) async-start(bf16[32,64,128]{2,1,0:T(8,128)(2,1)} %get-tuple-element.19), calls=%async_computation.1 | async-start | bytes 1048576 | tf_op jit(solution)/shard_map/all_to_all | solution.py:364
  46.4 1.3 %collective-permute-start = (f32[1,1024]{1,0:T(1,128)S(1)}, f32[1,1024]{1,0:T(1,128)S(1)}, u32[]{:S(2)}, u32[]{:S(2)}) collective-permute-start(f32[1,1024]{1,0:T(1,128)S(1)} %copy-done.4), channel_id=1, source_target_pairs={{0,1},{1,0},{2,3},{3,2},{4,5},{5,4},{6,7},{7,6},{8,9},{9,8},{10,11... | collective-permute-start | bytes 12296 | tf_op jit(solution)/shard_map/ppermute | solution.py:371
  47.6 3.6 %collective-permute-start.1 = (f32[1,1024]{1,0:T(1,128)S(1)}, f32[1,1024]{1,0:T(1,128)S(1)}, u32[]{:S(2)}, u32[]{:S(2)}) collective-permute-start(f32[1,1024]{1,0:T(1,128)S(1)} %add.9), channel_id=1, source_target_pairs={{0,2},{1,3},{2,0},{3,1},{4,6},{5,7},{6,4},{7,5},{8,10},{9,11},{10,... | collective-permute-start | bytes 12296 | tf_op jit(solution)/shard_map/ppermute | solution.py:371
  51.2 5.1 %collective-permute-start.2 = (f32[1,1024]{1,0:T(1,128)S(1)}, f32[1,1024]{1,0:T(1,128)S(1)}, u32[]{:S(2)}, u32[]{:S(2)}) collective-permute-start(f32[1,1024]{1,0:T(1,128)S(1)} %add.10), channel_id=1, source_target_pairs={{0,4},{1,5},{2,6},{3,7},{4,0},{5,1},{6,2},{7,3},{8,12},{9,13},{10,... | collective-permute-start | bytes 12296 | tf_op jit(solution)/shard_map/ppermute | solution.py:371
  63.4 1.2 %copy-start.2 = (bf16[1024,512]{1,0:T(8,128)(2,1)S(1)}, bf16[1024,512]{1,0:T(8,128)(2,1)}, u32[]{:S(2)}) copy-start(bf16[1024,512]{1,0:T(8,128)(2,1)} %g_ref.1) | copy-start | bytes 3145732

commit v4 on v3

--- a/solution.py
+++ b/solution.py
@@ -11,7 +11,7 @@
 D = 128
 PIECE = 16
 STRIP = 256
-VMEM_BYTES = 61 << 20
+VMEM_BYTES = 60 << 20
 STATE_BYTES = 48 << 20
 AHEAD = 2
 F32 = jnp.float32
@@ -44,12 +44,11 @@
 
 
 def sums_kernel(
-    start_ref, q_any, k_any, v_any, g_any, c_any, probe_ref, steer_ref,
-    u_any, gate_ref, q_ref, k_ref, v_ref, g_ref, u_ref, in_sem, c_sem, out_sem,
+    start_any, q_any, k_any, v_any, g_any, c_any, probe_any, steer_any, u_any, gate_ref,
+    start_ref, q_ref, k_ref, v_ref, g_ref, probe_ref, steer_ref, u_ref, in_sem, few_sem, out_sem,
 ):
     heads, length, _ = q_ref.shape
     pieces = D // PIECE
-    start = start_ref[0]
 
     def fetches(h):
         pairs = ((k_any, k_ref), (v_any, v_ref), (q_any, q_ref), (g_any, g_ref))
@@ -58,21 +57,31 @@
             for n, (far, near) in enumerate(pairs)
         ]
 
+    few = [
+        pltpu.make_async_copy(start_any, start_ref, few_sem.at[0]),
+        pltpu.make_async_copy(probe_any, probe_ref, few_sem.at[1]),
+        pltpu.make_async_copy(steer_any, steer_ref, few_sem.at[2]),
+        pltpu.make_async_copy(c_any, u_ref.at[:, 48:64, :], few_sem.at[3]),
+    ]
+    few[0].start()
     for h in range(AHEAD):
         for copy in fetches(h):
             copy.start()
-    cached = pltpu.make_async_copy(c_any, u_any.at[:, 48:64, :], c_sem)
-    cached.start()
-
+    for copy in few[1:]:
+        copy.start()
+    few[0].wait()
+    start = start_ref[0]
     before, after, final = row_masks(start, length)
+    for copy in few[1:]:
+        copy.wait()
     probe = probe_ref[...]
     high = probe.astype(BF16)
     low = (probe - high.astype(F32)).astype(BF16)
+    steer = steer_ref[...].astype(F32)
     rows = lax.broadcasted_iota(jnp.int32, (8, D), 0)
     flag = jnp.where(start < length, 1.0, 0.0).astype(F32)
     tile = jnp.full((8, D), flag)
     gate = jnp.zeros((heads, length), F32)
-    steer = steer_ref[...].astype(F32)
     sent = []
     for h in range(heads):
         for copy in fetches(h):
@@ -87,19 +96,19 @@
         u_ref[here, 0:16, :] = kv.astype(BF16).reshape(pieces, PIECE, D)
         u_ref[here, 16:32, :] = both[:, :D].astype(BF16).reshape(pieces, PIECE, D)
         u_ref[here, 32:48, :] = both[:, D:].astype(BF16).reshape(pieces, PIECE, D)
-        copy = pltpu.make_async_copy(u_ref.at[here, 0:48, :], u_any.at[here, 0:48, :], out_sem.at[h])
+        copy = pltpu.make_async_copy(u_ref.at[here, 0:64, :], u_any.at[here, 0:64, :], out_sem.at[h])
         copy.start()
         sent.append(copy)
         steer_sum = nn(high, g) + nn(low, g)
         tile = jnp.where(rows == h, jnp.broadcast_to(steer_sum, (8, D)), tile)
         vector = jnp.where(rows[:heads] == h, steer, 0.0).astype(BF16)
         gate = gate + nt(vector, g)
-    gate_ref[...] = jnp.sum(gate, axis=0, keepdims=True)
     u_ref[:, 64:72, :] = jnp.broadcast_to(tile.astype(BF16)[None], (u_ref.shape[0], 8, D))
     copy = pltpu.make_async_copy(u_ref.at[:, 64:72, :], u_any.at[:, 64:72, :], out_sem.at[heads])
     copy.start()
     sent.append(copy)
-    for copy in [cached] + sent:
+    gate_ref[...] = jnp.sum(gate, axis=0, keepdims=True)
+    for copy in sent:
         copy.wait()
 
 
@@ -111,20 +120,23 @@
     hbm, vmem = whole(pltpu.HBM), whole(pltpu.VMEM)
     return pl.pallas_call(
         sums_kernel,
-        in_specs=[whole(pltpu.SMEM), hbm, hbm, hbm, hbm, hbm, vmem, vmem],
+        in_specs=[hbm] * 8,
         out_specs=[hbm, vmem],
         out_shape=[
             jax.ShapeDtypeStruct((total, 72, D), BF16),
             jax.ShapeDtypeStruct((1, length), F32),
         ],
         scratch_shapes=[
-            near,
-            near,
-            near,
-            near,
+            pltpu.SMEM(session_start.shape, jnp.int32),
+            near,
+            near,
+            near,
+            near,
+            pltpu.VMEM((1, length), F32),
+            pltpu.VMEM(steer_vector.shape, BF16),
             pltpu.VMEM((total, 72, D), BF16),
             pltpu.SemaphoreType.DMA((4, heads)),
-            pltpu.SemaphoreType.DMA(()),
+            pltpu.SemaphoreType.DMA((4,)),
             pltpu.SemaphoreType.DMA((heads + 1,)),
         ],
         compiler_params=pltpu.CompilerParams(vmem_limit_bytes=VMEM_BYTES),
@@ -144,8 +156,13 @@
     )
 
 
-def scan_kernel(owner_ref, v_ref, w_any, steer_ref, w_ref, sem):
+def scan_kernel(owner_any, v_any, w_any, steer_ref, owner_ref, v_ref, w_ref, in_sem, out_sem):
     blocks = v_ref.shape[0]
+    fetched = [pltpu.make_async_copy(owner_any, owner_ref, in_sem.at[0])]
+    for n, rows in enumerate((slice(48, 72), slice(0, 16), slice(16, 48))):
+        fetched.append(pltpu.make_async_copy(v_any.at[:, rows, :], v_ref.at[:, rows, :], in_sem.at[n + 1]))
+    for copy in fetched:
+        copy.start()
 
     def extra(b):
         return v_ref[b, 64:72, :].astype(F32)
@@ -156,6 +173,8 @@
 
     state = jnp.zeros((PIECE, D), F32)
     steer = jnp.zeros((8, D), F32)
+    for copy in fetched[:3]:
+        copy.wait()
     for b in range(blocks):
         cached = v_ref[owner_ref[b], 48:64, :]
         w_ref[b, 0:16, :] = state.astype(BF16)
@@ -163,8 +182,9 @@
         added = v_ref[b, 0:16, :].astype(F32)
         state = added + jnp.where(flag_of(b), cached.astype(F32), state)
         steer = steer + extra(b)
-    first = pltpu.make_async_copy(w_ref.at[:, 0:32, :], w_any.at[:, 0:32, :], sem.at[0])
+    first = pltpu.make_async_copy(w_ref.at[:, 0:32, :], w_any.at[:, 0:32, :], out_sem.at[0])
     first.start()
+    fetched[3].wait()
     state = jnp.zeros((PIECE, D), F32)
     for b in reversed(range(blocks)):
         flag = flag_of(b)
@@ -172,7 +192,7 @@
         begun = (v_ref[b, 32:48, :].astype(F32) + state) * (1.0 / D)
         w_ref[owner_ref[b], 48:64, :] = jnp.where(flag, begun, 0.0).astype(BF16)
         state = v_ref[b, 16:32, :].astype(F32) + jnp.where(flag, 0.0, state)
-    second = pltpu.make_async_copy(w_ref.at[:, 32:64, :], w_any.at[:, 32:64, :], sem.at[1])
+    second = pltpu.make_async_copy(w_ref.at[:, 32:64, :], w_any.at[:, 32:64, :], out_sem.at[1])
     second.start()
     tokens = blocks * 1024
     steer_ref[...] = steer[0 : steer_ref.shape[0]] * (1.0 / math.sqrt(tokens))
@@ -185,23 +205,31 @@
     hbm, vmem = whole(pltpu.HBM), whole(pltpu.VMEM)
     return pl.pallas_call(
         scan_kernel,
-        in_specs=[whole(pltpu.SMEM), vmem],
+        in_specs=[hbm, hbm],
         out_specs=[hbm, vmem],
         out_shape=[
             jax.ShapeDtypeStruct((blocks, 64, D), BF16),
             jax.ShapeDtypeStruct((heads, D), F32),
         ],
-        scratch_shapes=[pltpu.VMEM((blocks, 64, D), BF16), pltpu.SemaphoreType.DMA((2,))],
+        scratch_shapes=[
+            pltpu.SMEM(owner.shape, jnp.int32),
+            pltpu.VMEM(pieces.shape, BF16),
+            pltpu.VMEM((blocks, 64, D), BF16),
+            pltpu.SemaphoreType.DMA((4,)),
+            pltpu.SemaphoreType.DMA((2,)),
+        ],
         compiler_params=pltpu.CompilerParams(vmem_limit_bytes=VMEM_BYTES),
         name="scan_blocks",
     )(owner, pieces)
 
 
 def local_kernel(
-    start_ref, q_any, k_any, v_any, g_any, part_any, q_ref, k_ref, v_ref, g_ref, part_ref, in_sem, out_sem
+    start_any, q_any, k_any, v_any, g_any, part_any,
+    start_ref, q_ref, k_ref, v_ref, g_ref, part_ref, start_sem, in_sem, out_sem,
 ):
     heads, length, _ = q_ref.shape
-    start = start_ref[0]
+    started = pltpu.make_async_copy(start_any, start_ref, start_sem)
+    started.start()
 
     def fetches(h):
         pairs = ((g_any, g_ref), (v_any, v_ref), (k_any, k_ref), (q_any, q_ref))
@@ -217,6 +245,9 @@
     for h in range(AHEAD):
         for copy in fetches(h):
             copy.start()
+
+    started.wait()
+    start = start_ref[0]
 
     @pl.loop(0, heads)
     def _(h):
@@ -258,12 +289,14 @@
     near = pltpu.VMEM((heads, length, D), BF16)
     return pl.pallas_call(
         local_kernel,
-        in_specs=[whole(pltpu.SMEM), hbm, hbm, hbm, hbm],
+        in_specs=[hbm] * 5,
         out_specs=hbm,
         out_shape=jax.ShapeDtypeStruct((3, heads, length, D), BF16),
-        scratch_shapes=[near] * 4
+        scratch_shapes=[pltpu.SMEM(session_start.shape, jnp.int32)]
+        + [near] * 4
         + [
             pltpu.VMEM((3, heads, length, D), BF16),
+            pltpu.SemaphoreType.DMA(()),
             pltpu.SemaphoreType.DMA((4, heads)),
             pltpu.SemaphoreType.DMA((heads,)),
         ],
@@ -276,24 +309,39 @@
 
 
 def state_kernel(
-    start_ref, k_ref, v_ref, g_ref, part_any, w_ref,
-    dq_any, dk_any, dv_any, dc_any, part_ref, out_ref, in_sem, c_sem, out_sem,
+    start_any, k_ref, v_ref, g_ref, part_any, w_any,
+    dq_any, dk_any, dv_any, dc_any,
+    start_ref, part_ref, w_ref, out_ref, start_sem, in_sem, w_sem, c_sem, out_sem,
 ):
     _, heads, length, _ = part_ref.shape
     pieces = D // PIECE
-    start = start_ref[0]
 
     def fetch(h):
         return pltpu.make_async_copy(part_any.at[:, h], part_ref.at[:, h], in_sem.at[h])
 
+    def states(h):
+        here = slice(h * pieces, (h + 1) * pieces)
+        return pltpu.make_async_copy(w_any.at[here], w_ref.at[here], w_sem.at[h])
+
+    def cache(h):
+        here = slice(h * pieces, (h + 1) * pieces)
+        return pltpu.make_async_copy(w_ref.at[here, 48:64, :], dc_any.at[here], c_sem.at[h])
+
+    started = pltpu.make_async_copy(start_any, start_ref, start_sem)
+    started.start()
     for h in range(heads):
+        states(h).start()
         fetch(h).start()
-    copies = [pltpu.make_async_copy(w_ref.at[:, 48:64, :], dc_any, c_sem)]
-    copies[0].start()
+    copies = []
+    started.wait()
+    start = start_ref[0]
     before, after, final = row_masks(start, length)
     scale = 1.0 / D
     for h in range(heads):
         fetch(h).wait()
+        states(h).wait()
+        cache(h).start()
+        copies.append(cache(h))
         columns = slice(h * D, (h + 1) * D)
         here = slice(h * pieces, (h + 1) * pieces)
         enter = w_ref[here, 0:16, :].reshape(D, D)
@@ -323,14 +371,18 @@
     wide = jax.ShapeDtypeStruct((length, heads * D), BF16)
     *grads, grad_cache = pl.pallas_call(
         state_kernel,
-        in_specs=[whole(pltpu.SMEM), vmem, vmem, vmem, hbm, vmem],
+        in_specs=[hbm, vmem, vmem, vmem, hbm, hbm],
         out_specs=[hbm] * 4,
         out_shape=[wide, wide, wide, jax.ShapeDtypeStruct((total, PIECE, D), BF16)],
         scratch_shapes=[
-            near,
-            near,
+            pltpu.SMEM(session_start.shape, jnp.int32),
+            near,
+            pltpu.VMEM(states.shape, BF16),
+            near,
+            pltpu.SemaphoreType.DMA(()),
             pltpu.SemaphoreType.DMA((heads,)),
-            pltpu.SemaphoreType.DMA(()),
+            pltpu.SemaphoreType.DMA((heads,)),
+            pltpu.SemaphoreType.DMA((heads,)),
             pltpu.SemaphoreType.DMA((3, heads)),
         ],
         compiler_params=pltpu.CompilerParams(vmem_limit_bytes=STATE_BYTES),

time: 69.1 us -> 66 us (0.955)
  local copies, waits for them, and re-layouts: 2.06 us -> 0.03 us
  Pallas kernels: 26.3 us -> 25.1 us
    unnamed x10 -> x8, local copies, waits for them, and re-layouts: 2.06 us -> 0.03 us
    pallas_call x4, Pallas kernels: 26.3 us -> 25.1 us  [the longest x1 13.1 us: local_grads(): pl.pallas_call(local_kernel, in_specs=[hbm] * 5, out_specs=hbm, out_shape...]
  transfers between devices with their start and end apart: 5 -> 5, of which waited for: 5 -> 5; matrix products, arithmetic and copies ran while one was open for 1% -> 1% of each run, Pallas kernels for 19% -> 20%
where the time goes in v4:
time: 66 us; the launch traced here: 65.7 us
  Pallas kernels  25.1 us (38%)
  waiting for transfers between devices  19.3 us (29%)
  starting transfers between devices  19.2 us (29%)
  between operations  1.38 us (2%)
    pallas_call x1, Pallas kernels, local_grads(): pl.pallas_call(local_kernel, in_specs=[hbm] * 5, out_specs=hbm, out_shape...  13.1 us
    all_to_all x1, starting transfers between devices, shards(): pieces = lax.all_to_all(sent, 'seq', 0, 0, tiled=True)  11.4 us
    ppermute x3, waiting for transfers between devices, shards(): lax.ppermute(gate, 'head', [(i, i ^ step) for i in range(count)])  7.13 us
    all_to_all x1, waiting for transfers between devices, shards(): states = lax.all_to_all(scanned, 'seq', 0, 0, tiled=True)  6.38 us
    all_to_all x1, waiting for transfers between devices, shards(): pieces = lax.all_to_all(sent, 'seq', 0, 0, tiled=True)  5.82 us
    pallas_call x1, Pallas kernels, block_sums(): pl.pallas_call(sums_kernel, in_specs=[hbm] * 8, out_specs=[hbm, vmem], ou...  5.3 us
    all_to_all x1, starting transfers between devices, shards(): states = lax.all_to_all(scanned, 'seq', 0, 0, tiled=True)  4.94 us
    pallas_call x1, Pallas kernels, state_grads(): pl.pallas_call(state_kernel, in_specs=[hbm, vmem, vmem, vmem, hbm, hbm],...  4.15 us
  transfers between devices with their start and end apart: 5, of which 5 were waited for; matrix products, arithmetic and copies ran while one was open for 1% of the time, Pallas kernels for 20%

profile of v4, /device:TPU:8, one launch (start us, length us, event | category | flops | bytes accessed | tf_op | source)
XLA Modules:
  0.0 65.7 jit_solution(15031312100927005475)
XLA Ops:
  1.3 5.3 %block_sums.1 = (bf16[32,72,128]{2,1,0:T(8,128)(2,1)}, f32[1,1024]{1,0:T(1,128)}) custom-call(s32[1]{0:T(128)S(6)} %copy.15.start_any, bf16[1024,512]{1,0:T(8,128)(2,1)} %q_any.3, bf16[1024,512]{1,0:T(8,128)(2,1)} %k_ref.1, bf16[1024,512]{1,0:T(8,128)(2,1)} %v_ref.1, bf16[1024,512]{1,0:T(8,128)(2,1)} %g_ref.1, bf16[32,16,128]{2,1,0:T(8,128)(2,1)} %bitcast.4, ...), custom_call_target="tpu_custom_call" | custom-call | flops 536870912 | bytes 4194304 | tf_op jit(solution)/shard_map/block_sums/pallas_call | solution.py:121
  6.6 11.4 %all-to-all-start = ((bf16[32,72,128]{2,1,0:T(8,128)(2,1)}), bf16[32,72,128]{2,1,0:T(8,128)(2,1)}, u32[]{:S(2)}, u32[]{:S(2)}) async-start(bf16[32,72,128]{2,1,0:T(8,128)(2,1)} %get-tuple-element.16), calls=%async_computation | async-start | bytes 1179648 | tf_op jit(solution)/shard_map/all_to_all | solution.py:412
  18.0 0.0 copy-start.3
  18.0 0.0 copy-start
  18.1 0.0 copy-start.1
  18.1 0.0 copy-start.2
  18.1 13.1 %local_grads.1.part_any = bf16[3,4,1024,128]{3,2,1,0:T(8,128)(2,1)} custom-call(s32[1]{0:T(128)S(6)} %copy.15.start_any, bf16[1024,512]{1,0:T(8,128)(2,1)} %q_any.3, bf16[1024,512]{1,0:T(8,128)(2,1)} %k_ref.1, bf16[1024,512]{1,0:T(8,128)(2,1)} %v_ref.1, bf16[1024,512]{1,0:T(8,128)(2,1)} %g_ref.1), custom_call_target="tpu_custom_call" | custom-call | flops 8589934592 | bytes 10485760 | tf_op jit(solution)/shard_map/local_grads/pallas_call | solution.py:290
  31.2 5.8 %all-to-all-done.v_any = bf16[32,72,128]{2,1,0:T(8,128)(2,1)} async-done(((bf16[32,72,128]{2,1,0:T(8,128)(2,1)}), bf16[32,72,128]{2,1,0:T(8,128)(2,1)}, u32[]{:S(2)}, u32[]{:S(2)}) %all-to-all-start) | async-done | bytes 589856 | tf_op jit(solution)/shard_map/all_to_all | solution.py:412
  37.0 2.6 %scan_blocks.1 = (bf16[32,64,128]{2,1,0:T(8,128)(2,1)}, f32[4,128]{1,0:T(4,128)}) custom-call(s32[32]{0:T(128)} %owner_any.1, bf16[32,72,128]{2,1,0:T(8,128)(2,1)} %all-to-all-done.v_any), custom_call_target="tpu_custom_call" | custom-call | tf_op jit(solution)/shard_map/scan_blocks/pallas_call | solution.py:206
  39.6 4.9 %all-to-all-start.1 = ((bf16[32,64,128]{2,1,0:T(8,128)(2,1)}), bf16[32,64,128]{2,1,0:T(8,128)(2,1)}, u32[]{:S(2)}, u32[]{:S(2)}) async-start(bf16[32,64,128]{2,1,0:T(8,128)(2,1)} %get-tuple-element.19), calls=%async_computation.1 | async-start | bytes 1048576 | tf_op jit(solution)/shard_map/all_to_all | solution.py:416
  44.5 0.0 copy-done.3
  44.5 0.1 collective-permute-start
  44.6 1.2 %collective-permute-done = f32[1,1024]{1,0:T(1,128)S(1)} collective-permute-done((f32[1,1024]{1,0:T(1,128)S(1)}, f32[1,1024]{1,0:T(1,128)S(1)}, u32[]{:S(2)}, u32[]{:S(2)}) %collective-permute-start) | collective-permute-done | bytes 4128 | tf_op jit(solution)/shard_map/ppermute | solution.py:423
  45.8 0.4 collective-permute-start.1
  46.3 3.2 %collective-permute-done.1 = f32[1,1024]{1,0:T(1,128)S(1)} collective-permute-done((f32[1,1024]{1,0:T(1,128)S(1)}, f32[1,1024]{1,0:T(1,128)S(1)}, u32[]{:S(2)}, u32[]{:S(2)}) %collective-permute-start.1) | collective-permute-done | bytes 4128 | tf_op jit(solution)/shard_map/ppermute | solution.py:423
  49.4 2.3 %collective-permute-start.2 = (f32[1,1024]{1,0:T(1,128)S(1)}, f32[1,1024]{1,0:T(1,128)S(1)}, u32[]{:S(2)}, u32[]{:S(2)}) collective-permute-start(f32[1,1024]{1,0:T(1,128)S(1)} %add.10), channel_id=1, source_target_pairs={{0,4},{1,5},{2,6},{3,7},{4,0},{5,1},{6,2},{7,3},{8,12},{9,13},{10,... | collective-permute-start | bytes 12296 | tf_op jit(solution)/shard_map/ppermute | solution.py:423
  51.7 2.8 %collective-permute-done.2 = f32[1,1024]{1,0:T(1,128)S(1)} collective-permute-done((f32[1,1024]{1,0:T(1,128)S(1)}, f32[1,1024]{1,0:T(1,128)S(1)}, u32[]{:S(2)}, u32[]{:S(2)}) %collective-permute-start.2) | collective-permute-done | bytes 4128 | tf_op jit(solution)/shard_map/ppermute | solution.py:423
  54.5 0.6 add.11
  55.1 6.4 %all-to-all-done.1.w_any = bf16[32,64,128]{2,1,0:T(8,128)(2,1)} async-done(((bf16[32,64,128]{2,1,0:T(8,128)(2,1)}), bf16[32,64,128]{2,1,0:T(8,128)(2,1)}, u32[]{:S(2)}, u32[]{:S(2)}) %all-to-all-start.1) | async-done | bytes 524320 | tf_op jit(solution)/shard_map/all_to_all | solution.py:416
  61.5 0.0 copy-done
  61.5 0.0 copy-done.1
  61.5 0.0 copy-done.2
  61.5 4.1 %state_grads.1 = (bf16[1024,512]{1,0:T(8,128)(2,1)}, bf16[1024,512]{1,0:T(8,128)(2,1)}, bf16[1024,512]{1,0:T(8,128)(2,1)}, bf16[32,16,128]{2,1,0:T(8,128)(2,1)}) custom-call(s32[1]{0:T(128)S(6)} %copy.15.start_any, bf16[1024,512]{1,0:T(8,128)(2,1)S(1)} %copy-done, bf16[1024,512]{1,0:T(8,128)(2,1)S(1)} %copy-done.1, bf16[1024,512]{1,0:T(8,128)(2,1)S(1)} %copy-done.2, ...), custom_call_target="tpu_custom_call" | custom-call | flops 536870912 | bytes 10485760 | tf_op jit(solution)/shard_map/state_grads/pallas_call | solution.py:372
  (2 shorter events, 0.0 us)
Async XLA Ops:
  6.6 30.4 %all-to-all-start = ((bf16[32,72,128]{2,1,0:T(8,128)(2,1)}), bf16[32,72,128]{2,1,0:T(8,128)(2,1)}, u32[]{:S(2)}, u32[]{:S(2)}) async-start(bf16[32,72,128]{2,1,0:T(8,128)(2,1)} %get-tuple-element.16), calls=%async_computation | async-start | bytes 1179648 | tf_op jit(solution)/shard_map/all_to_all | solution.py:412
  18.0 26.5 %copy-start.3 = (f32[1,1024]{1,0:T(1,128)S(1)}, f32[1,1024]{1,0:T(1,128)}, u32[]{:S(2)}) copy-start(f32[1,1024]{1,0:T(1,128)} %get-tuple-element.25) | copy-start | bytes 12292
  18.0 43.5 %copy-start = (bf16[1024,512]{1,0:T(8,128)(2,1)S(1)}, bf16[1024,512]{1,0:T(8,128)(2,1)}, u32[]{:S(2)}) copy-start(bf16[1024,512]{1,0:T(8,128)(2,1)} %k_ref.1) | copy-start | bytes 3145732
  18.1 43.5 %copy-start.1 = (bf16[1024,512]{1,0:T(8,128)(2,1)S(1)}, bf16[1024,512]{1,0:T(8,128)(2,1)}, u32[]{:S(2)}) copy-start(bf16[1024,512]{1,0:T(8,128)(2,1)} %v_ref.1) | copy-start | bytes 3145732
  18.1 43.4 %copy-start.2 = (bf16[1024,512]{1,0:T(8,128)(2,1)S(1)}, bf16[1024,512]{1,0:T(8,128)(2,1)}, u32[]{:S(2)}) copy-start(bf16[1024,512]{1,0:T(8,128)(2,1)} %g_ref.1) | copy-start | bytes 3145732
  39.6 21.9 %all-to-all-start.1 = ((bf16[32,64,128]{2,1,0:T(8,128)(2,1)}), bf16[32,64,128]{2,1,0:T(8,128)(2,1)}, u32[]{:S(2)}, u32[]{:S(2)}) async-start(bf16[32,64,128]{2,1,0:T(8,128)(2,1)} %get-tuple-element.19), calls=%async_computation.1 | async-start | bytes 1048576 | tf_op jit(solution)/shard_map/all_to_all | solution.py:416
  44.5 1.3 %collective-permute-start = (f32[1,1024]{1,0:T(1,128)S(1)}, f32[1,1024]{1,0:T(1,128)S(1)}, u32[]{:S(2)}, u32[]{:S(2)}) collective-permute-start(f32[1,1024]{1,0:T(1,128)S(1)} %copy-done.3), channel_id=1, source_target_pairs={{0,1},{1,0},{2,3},{3,2},{4,5},{5,4},{6,7},{7,6},{8,9},{9,8},{10,11... | collective-permute-start | bytes 12296 | tf_op jit(solution)/shard_map/ppermute | solution.py:423
  45.8 3.6 %collective-permute-start.1 = (f32[1,1024]{1,0:T(1,128)S(1)}, f32[1,1024]{1,0:T(1,128)S(1)}, u32[]{:S(2)}, u32[]{:S(2)}) collective-permute-start(f32[1,1024]{1,0:T(1,128)S(1)} %add.9), channel_id=1, source_target_pairs={{0,2},{1,3},{2,0},{3,1},{4,6},{5,7},{6,4},{7,5},{8,10},{9,11},{10,... | collective-permute-start | bytes 12296 | tf_op jit(solution)/shard_map/ppermute | solution.py:423
  49.4 5.1 %collective-permute-start.2 = (f32[1,1024]{1,0:T(1,128)S(1)}, f32[1,1024]{1,0:T(1,128)S(1)}, u32[]{:S(2)}, u32[]{:S(2)}) collective-permute-start(f32[1,1024]{1,0:T(1,128)S(1)} %add.10), channel_id=1, source_target_pairs={{0,4},{1,5},{2,6},{3,7},{4,0},{5,1},{6,2},{7,3},{8,12},{9,13},{10,... | collective-permute-start | bytes 12296 | tf_op jit(solution)/shard_map/ppermute | solution.py:423

commit v5 on v4

--- a/solution.py
+++ b/solution.py
@@ -30,6 +30,10 @@
     return lax.dot_general(a, b, (((0,), (0,)), ((), ())), preferred_element_type=F32)
 
 
+def group_place(b, count):
+    return lax.rem(7 * count // 4 - 1 - b, count) if isinstance(b, jax.Array) else (7 * count // 4 - 1 - b) % count
+
+
 def row_masks(start, length):
     rows = lax.broadcasted_iota(jnp.int32, (length, D), 0)
     after = (rows >= start).astype(F32)
@@ -61,19 +65,18 @@
         pltpu.make_async_copy(start_any, start_ref, few_sem.at[0]),
         pltpu.make_async_copy(probe_any, probe_ref, few_sem.at[1]),
         pltpu.make_async_copy(steer_any, steer_ref, few_sem.at[2]),
-        pltpu.make_async_copy(c_any, u_ref.at[:, 48:64, :], few_sem.at[3]),
     ]
-    few[0].start()
+    cached = pltpu.make_async_copy(c_any, u_ref.at[:, 16:32, :], few_sem.at[3])
+    for copy in few:
+        copy.start()
     for h in range(AHEAD):
         for copy in fetches(h):
             copy.start()
-    for copy in few[1:]:
-        copy.start()
-    few[0].wait()
+    cached.start()
+    for copy in few:
+        copy.wait()
     start = start_ref[0]
     before, after, final = row_masks(start, length)
-    for copy in few[1:]:
-        copy.wait()
     probe = probe_ref[...]
     high = probe.astype(BF16)
     low = (probe - high.astype(F32)).astype(BF16)
@@ -93,9 +96,11 @@
         kv = tn(k_ref[h], v_ref[h] * final)
         both = tn(q_ref[h], jnp.concatenate([g * before, g * after], axis=1))
         here = slice(h * pieces, (h + 1) * pieces)
-        u_ref[here, 0:16, :] = kv.astype(BF16).reshape(pieces, PIECE, D)
-        u_ref[here, 16:32, :] = both[:, :D].astype(BF16).reshape(pieces, PIECE, D)
-        u_ref[here, 32:48, :] = both[:, D:].astype(BF16).reshape(pieces, PIECE, D)
+        u_ref[here, 0:16, :] = both[:, D:].astype(BF16).reshape(pieces, PIECE, D)
+        u_ref[here, 32:48, :] = kv.astype(BF16).reshape(pieces, PIECE, D)
+        u_ref[here, 48:64, :] = both[:, :D].astype(BF16).reshape(pieces, PIECE, D)
+        if h == 0:
+            cached.wait()
         copy = pltpu.make_async_copy(u_ref.at[here, 0:64, :], u_any.at[here, 0:64, :], out_sem.at[h])
         copy.start()
         sent.append(copy)
@@ -159,13 +164,13 @@
 def scan_kernel(owner_any, v_any, w_any, steer_ref, owner_ref, v_ref, w_ref, in_sem, out_sem):
     blocks = v_ref.shape[0]
     fetched = [pltpu.make_async_copy(owner_any, owner_ref, in_sem.at[0])]
-    for n, rows in enumerate((slice(48, 72), slice(0, 16), slice(16, 48))):
+    for n, rows in enumerate((slice(16, 48), slice(64, 72), slice(0, 16), slice(48, 64))):
         fetched.append(pltpu.make_async_copy(v_any.at[:, rows, :], v_ref.at[:, rows, :], in_sem.at[n + 1]))
     for copy in fetched:
         copy.start()
 
     def extra(b):
-        return v_ref[b, 64:72, :].astype(F32)
+        return v_ref[group_place(b, blocks), 64:72, :].astype(F32)
 
     def flag_of(b):
         row = extra(b)[4:5]
@@ -176,22 +181,26 @@
     for copy in fetched[:3]:
         copy.wait()
     for b in range(blocks):
-        cached = v_ref[owner_ref[b], 48:64, :]
-        w_ref[b, 0:16, :] = state.astype(BF16)
-        w_ref[b, 16:32, :] = cached
-        added = v_ref[b, 0:16, :].astype(F32)
+        here = group_place(b, blocks)
+        cached = v_ref[group_place(owner_ref[b], blocks), 16:32, :]
+        w_ref[here, 0:16, :] = state.astype(BF16)
+        w_ref[here, 16:32, :] = cached
+        added = v_ref[here, 32:48, :].astype(F32)
         state = added + jnp.where(flag_of(b), cached.astype(F32), state)
         steer = steer + extra(b)
     first = pltpu.make_async_copy(w_ref.at[:, 0:32, :], w_any.at[:, 0:32, :], out_sem.at[0])
     first.start()
-    fetched[3].wait()
+    for copy in fetched[3:]:
+        copy.wait()
     state = jnp.zeros((PIECE, D), F32)
     for b in reversed(range(blocks)):
+        here = group_place(b, blocks)
         flag = flag_of(b)
-        w_ref[b, 32:48, :] = state.astype(BF16)
-        begun = (v_ref[b, 32:48, :].astype(F32) + state) * (1.0 / D)
-        w_ref[owner_ref[b], 48:64, :] = jnp.where(flag, begun, 0.0).astype(BF16)
-        state = v_ref[b, 16:32, :].astype(F32) + jnp.where(flag, 0.0, state)
+        w_ref[here, 32:48, :] = state.astype(BF16)
+        begun = (v_ref[here, 0:16, :].astype(F32) + state) * (1.0 / D)
+        slot = group_place(owner_ref[b], blocks)
+        w_ref[slot, 48:64, :] = jnp.where(flag, begun, 0.0).astype(BF16)
+        state = v_ref[here, 48:64, :].astype(F32) + jnp.where(flag, 0.0, state)
     second = pltpu.make_async_copy(w_ref.at[:, 32:64, :], w_any.at[:, 32:64, :], out_sem.at[1])
     second.start()
     tokens = blocks * 1024
@@ -215,7 +224,7 @@
             pltpu.SMEM(owner.shape, jnp.int32),
             pltpu.VMEM(pieces.shape, BF16),
             pltpu.VMEM((blocks, 64, D), BF16),
-            pltpu.SemaphoreType.DMA((4,)),
+            pltpu.SemaphoreType.DMA((5,)),
             pltpu.SemaphoreType.DMA((2,)),
         ],
         compiler_params=pltpu.CompilerParams(vmem_limit_bytes=VMEM_BYTES),
@@ -329,7 +338,7 @@
 
     started = pltpu.make_async_copy(start_any, start_ref, start_sem)
     started.start()
-    for h in range(heads):
+    for h in range(AHEAD):
         states(h).start()
         fetch(h).start()
     copies = []
@@ -340,6 +349,9 @@
     for h in range(heads):
         fetch(h).wait()
         states(h).wait()
+        if h + AHEAD < heads:
+            states(h + AHEAD).start()
+            fetch(h + AHEAD).start()
         cache(h).start()
         copies.append(cache(h))
         columns = slice(h * D, (h + 1) * D)
@@ -409,11 +421,13 @@
     sent, gate = block_sums(
         queries, key_rows, value_rows, out_grad, cache_states, session_start, probe_gate, steer_vector
     )
-    pieces = lax.all_to_all(sent, "seq", 0, 0, tiled=True)
+    blocks = lax.axis_size("seq")
+    group = [sorted(range(blocks), key=lambda b: group_place(b, blocks))]
+    pieces = lax.all_to_all(sent, "seq", 0, 0, tiled=True, axis_index_groups=group)
     parts = local_grads(session_start, queries, key_rows, value_rows, out_grad)
     pieces, parts = lax.optimization_barrier((pieces, parts))
     scanned, grad_steer = scan_blocks(cache_owner, pieces, heads)
-    states = lax.all_to_all(scanned, "seq", 0, 0, tiled=True)
+    states = lax.all_to_all(scanned, "seq", 0, 0, tiled=True, axis_index_groups=group)
     grad_queries, grad_keys, grad_values, grad_cache = state_grads(
         session_start, key_rows, value_rows, out_grad, parts, states
     )

time: 66 us -> 63.8 us (0.967)
  waiting for transfers between devices: 19.3 us -> 9.37 us
  starting transfers between devices: 19.2 us -> 26.1 us
  Pallas kernels: 25.1 us -> 25.9 us
    all_to_all x2, waiting for transfers between devices: 12.2 us -> 2.25 us  [the longest x1 1.13 us: shards(): lax.all_to_all(scanned, 'seq', 0, 0, tiled=True, axis_index_groups=group)]
    all_to_all x2, starting transfers between devices: 16.4 us -> 23.2 us  [the longest x1 13.3 us: shards(): lax.all_to_all(sent, 'seq', 0, 0, tiled=True, axis_index_groups=group)]
    pallas_call x1, Pallas kernels: 4.15 us -> 5.02 us  [state_grads(): pl.pallas_call(state_kernel, in_specs=[hbm, vmem, vmem, vmem, hbm, hbm],...]
  transfers between devices with their start and end apart: 5 -> 5, of which waited for: 5 -> 5; matrix products, arithmetic and copies ran while one was open for 1% -> 1% of each run, Pallas kernels for 20% -> 21%
where the time goes in v5:
time: 63.8 us; the launch traced here: 63.4 us
  starting transfers between devices  26.1 us (41%)
  Pallas kernels  25.9 us (41%)
  waiting for transfers between devices  9.37 us (15%)
  between operations  1.38 us (2%)
    all_to_all x1, starting transfers between devices, shards(): lax.all_to_all(sent, 'seq', 0, 0, tiled=True, axis_index_groups=group)  13.3 us
    pallas_call x1, Pallas kernels, local_grads(): pl.pallas_call(local_kernel, in_specs=[hbm] * 5, out_specs=hbm, out_shape...  13.1 us
    all_to_all x1, starting transfers between devices, shards(): lax.all_to_all(scanned, 'seq', 0, 0, tiled=True, axis_index_groups=group)  9.93 us
    ppermute x3, waiting for transfers between devices, shards(): lax.ppermute(gate, 'head', [(i, i ^ step) for i in range(count)])  7.12 us
    pallas_call x1, Pallas kernels, block_sums(): pl.pallas_call(sums_kernel, in_specs=[hbm] * 8, out_specs=[hbm, vmem], ou...  5.25 us
    pallas_call x1, Pallas kernels, state_grads(): pl.pallas_call(state_kernel, in_specs=[hbm, vmem, vmem, vmem, hbm, hbm],...  5.02 us
    ppermute x3, starting transfers between devices, shards(): lax.ppermute(gate, 'head', [(i, i ^ step) for i in range(count)])  2.84 us
    pallas_call x1, Pallas kernels, scan_blocks(): pl.pallas_call(scan_kernel, in_specs=[hbm, hbm], out_specs=[hbm, vmem], o...  2.52 us
  transfers between devices with their start and end apart: 5, of which 5 were waited for; matrix products, arithmetic and copies ran while one was open for 1% of the time, Pallas kernels for 21%

profile of v5, /device:TPU:8, one launch (start us, length us, event | category | flops | bytes accessed | tf_op | source)
XLA Modules:
  0.0 63.4 jit_solution(5650339320741772785)
XLA Ops:
  1.3 5.3 %block_sums.1 = (bf16[32,72,128]{2,1,0:T(8,128)(2,1)}, f32[1,1024]{1,0:T(1,128)}) custom-call(s32[1]{0:T(128)S(6)} %copy.15.start_any, bf16[1024,512]{1,0:T(8,128)(2,1)} %q_any.3, bf16[1024,512]{1,0:T(8,128)(2,1)} %k_ref.1, bf16[1024,512]{1,0:T(8,128)(2,1)} %v_ref.1, bf16[1024,512]{1,0:T(8,128)(2,1)} %g_ref.1, bf16[32,16,128]{2,1,0:T(8,128)(2,1)} %bitcast.4, ...), custom_call_target="tpu_custom_call" | custom-call | flops 536870912 | bytes 4194304 | tf_op jit(solution)/shard_map/block_sums/pallas_call | solution.py:126
  6.5 13.3 %all-to-all-start = ((bf16[32,72,128]{2,1,0:T(8,128)(2,1)}), bf16[32,72,128]{2,1,0:T(8,128)(2,1)}, u32[]{:S(2)}, u32[]{:S(2)}) async-start(bf16[32,72,128]{2,1,0:T(8,128)(2,1)} %get-tuple-element.16), calls=%async_computation | async-start | bytes 1179648 | tf_op jit(solution)/shard_map/all_to_all | solution.py:426
  19.8 0.0 copy-start.3
  19.9 0.0 copy-start
  19.9 0.0 copy-start.1
  19.9 0.0 copy-start.2
  19.9 13.1 %local_grads.1.part_any = bf16[3,4,1024,128]{3,2,1,0:T(8,128)(2,1)} custom-call(s32[1]{0:T(128)S(6)} %copy.15.start_any, bf16[1024,512]{1,0:T(8,128)(2,1)} %q_any.3, bf16[1024,512]{1,0:T(8,128)(2,1)} %k_ref.1, bf16[1024,512]{1,0:T(8,128)(2,1)} %v_ref.1, bf16[1024,512]{1,0:T(8,128)(2,1)} %g_ref.1), custom_call_target="tpu_custom_call" | custom-call | flops 8589934592 | bytes 10485760 | tf_op jit(solution)/shard_map/local_grads/pallas_call | solution.py:299
  33.0 1.1 %all-to-all-done.v_any = bf16[32,72,128]{2,1,0:T(8,128)(2,1)} async-done(((bf16[32,72,128]{2,1,0:T(8,128)(2,1)}), bf16[32,72,128]{2,1,0:T(8,128)(2,1)}, u32[]{:S(2)}, u32[]{:S(2)}) %all-to-all-start) | async-done | bytes 589856 | tf_op jit(solution)/shard_map/all_to_all | solution.py:426
  34.1 2.5 %scan_blocks.1 = (bf16[32,64,128]{2,1,0:T(8,128)(2,1)}, f32[4,128]{1,0:T(4,128)}) custom-call(s32[32]{0:T(128)} %owner_any.1, bf16[32,72,128]{2,1,0:T(8,128)(2,1)} %all-to-all-done.v_any), custom_call_target="tpu_custom_call" | custom-call | tf_op jit(solution)/shard_map/scan_blocks/pallas_call | solution.py:215
  36.7 9.9 %all-to-all-start.1 = ((bf16[32,64,128]{2,1,0:T(8,128)(2,1)}), bf16[32,64,128]{2,1,0:T(8,128)(2,1)}, u32[]{:S(2)}, u32[]{:S(2)}) async-start(bf16[32,64,128]{2,1,0:T(8,128)(2,1)} %get-tuple-element.19), calls=%async_computation.1 | async-start | bytes 1048576 | tf_op jit(solution)/shard_map/all_to_all | solution.py:430
  46.6 0.0 copy-done.3
  46.6 0.1 collective-permute-start
  46.7 1.2 %collective-permute-done = f32[1,1024]{1,0:T(1,128)S(1)} collective-permute-done((f32[1,1024]{1,0:T(1,128)S(1)}, f32[1,1024]{1,0:T(1,128)S(1)}, u32[]{:S(2)}, u32[]{:S(2)}) %collective-permute-start) | collective-permute-done | bytes 4128 | tf_op jit(solution)/shard_map/ppermute | solution.py:437
  47.9 0.5 collective-permute-start.1
  48.3 3.2 %collective-permute-done.1 = f32[1,1024]{1,0:T(1,128)S(1)} collective-permute-done((f32[1,1024]{1,0:T(1,128)S(1)}, f32[1,1024]{1,0:T(1,128)S(1)}, u32[]{:S(2)}, u32[]{:S(2)}) %collective-permute-start.1) | collective-permute-done | bytes 4128 | tf_op jit(solution)/shard_map/ppermute | solution.py:437
  51.5 2.3 %collective-permute-start.2 = (f32[1,1024]{1,0:T(1,128)S(1)}, f32[1,1024]{1,0:T(1,128)S(1)}, u32[]{:S(2)}, u32[]{:S(2)}) collective-permute-start(f32[1,1024]{1,0:T(1,128)S(1)} %add.10), channel_id=1, source_target_pairs={{0,4},{1,5},{2,6},{3,7},{4,0},{5,1},{6,2},{7,3},{8,12},{9,13},{10,... | collective-permute-start | bytes 12296 | tf_op jit(solution)/shard_map/ppermute | solution.py:437
  53.8 2.8 %collective-permute-done.2 = f32[1,1024]{1,0:T(1,128)S(1)} collective-permute-done((f32[1,1024]{1,0:T(1,128)S(1)}, f32[1,1024]{1,0:T(1,128)S(1)}, u32[]{:S(2)}, u32[]{:S(2)}) %collective-permute-start.2) | collective-permute-done | bytes 4128 | tf_op jit(solution)/shard_map/ppermute | solution.py:437
  56.6 0.6 add.11
  57.2 1.1 %all-to-all-done.1.w_any = bf16[32,64,128]{2,1,0:T(8,128)(2,1)} async-done(((bf16[32,64,128]{2,1,0:T(8,128)(2,1)}), bf16[32,64,128]{2,1,0:T(8,128)(2,1)}, u32[]{:S(2)}, u32[]{:S(2)}) %all-to-all-start.1) | async-done | bytes 524320 | tf_op jit(solution)/shard_map/all_to_all | solution.py:430
  58.3 0.0 copy-done
  58.3 0.0 copy-done.1
  58.3 0.0 copy-done.2
  58.3 5.0 %state_grads.1 = (bf16[1024,512]{1,0:T(8,128)(2,1)}, bf16[1024,512]{1,0:T(8,128)(2,1)}, bf16[1024,512]{1,0:T(8,128)(2,1)}, bf16[32,16,128]{2,1,0:T(8,128)(2,1)}) custom-call(s32[1]{0:T(128)S(6)} %copy.15.start_any, bf16[1024,512]{1,0:T(8,128)(2,1)S(1)} %copy-done, bf16[1024,512]{1,0:T(8,128)(2,1)S(1)} %copy-done.1, bf16[1024,512]{1,0:T(8,128)(2,1)S(1)} %copy-done.2, ...), custom_call_target="tpu_custom_call" | custom-call | flops 536870912 | bytes 10485760 | tf_op jit(solution)/shard_map/state_grads/pallas_call | solution.py:384
  (2 shorter events, 0.0 us)
Async XLA Ops:
  6.5 27.6 %all-to-all-start = ((bf16[32,72,128]{2,1,0:T(8,128)(2,1)}), bf16[32,72,128]{2,1,0:T(8,128)(2,1)}, u32[]{:S(2)}, u32[]{:S(2)}) async-start(bf16[32,72,128]{2,1,0:T(8,128)(2,1)} %get-tuple-element.16), calls=%async_computation | async-start | bytes 1179648 | tf_op jit(solution)/shard_map/all_to_all | solution.py:426
  19.8 26.8 %copy-start.3 = (f32[1,1024]{1,0:T(1,128)S(1)}, f32[1,1024]{1,0:T(1,128)}, u32[]{:S(2)}) copy-start(f32[1,1024]{1,0:T(1,128)} %get-tuple-element.25) | copy-start | bytes 12292
  19.9 38.5 %copy-start = (bf16[1024,512]{1,0:T(8,128)(2,1)S(1)}, bf16[1024,512]{1,0:T(8,128)(2,1)}, u32[]{:S(2)}) copy-start(bf16[1024,512]{1,0:T(8,128)(2,1)} %k_ref.1) | copy-start | bytes 3145732
  19.9 38.5 %copy-start.1 = (bf16[1024,512]{1,0:T(8,128)(2,1)S(1)}, bf16[1024,512]{1,0:T(8,128)(2,1)}, u32[]{:S(2)}) copy-start(bf16[1024,512]{1,0:T(8,128)(2,1)} %v_ref.1) | copy-start | bytes 3145732
  19.9 38.5 %copy-start.2 = (bf16[1024,512]{1,0:T(8,128)(2,1)S(1)}, bf16[1024,512]{1,0:T(8,128)(2,1)}, u32[]{:S(2)}) copy-start(bf16[1024,512]{1,0:T(8,128)(2,1)} %g_ref.1) | copy-start | bytes 3145732
  36.7 21.7 %all-to-all-start.1 = ((bf16[32,64,128]{2,1,0:T(8,128)(2,1)}), bf16[32,64,128]{2,1,0:T(8,128)(2,1)}, u32[]{:S(2)}, u32[]{:S(2)}) async-start(bf16[32,64,128]{2,1,0:T(8,128)(2,1)} %get-tuple-element.19), calls=%async_computation.1 | async-start | bytes 1048576 | tf_op jit(solution)/shard_map/all_to_all | solution.py:430
  46.6 1.3 %collective-permute-start = (f32[1,1024]{1,0:T(1,128)S(1)}, f32[1,1024]{1,0:T(1,128)S(1)}, u32[]{:S(2)}, u32[]{:S(2)}) collective-permute-start(f32[1,1024]{1,0:T(1,128)S(1)} %copy-done.3), channel_id=1, source_target_pairs={{0,1},{1,0},{2,3},{3,2},{4,5},{5,4},{6,7},{7,6},{8,9},{9,8},{10,11... | collective-permute-start | bytes 12296 | tf_op jit(solution)/shard_map/ppermute | solution.py:437
  47.9 3.6 %collective-permute-start.1 = (f32[1,1024]{1,0:T(1,128)S(1)}, f32[1,1024]{1,0:T(1,128)S(1)}, u32[]{:S(2)}, u32[]{:S(2)}) collective-permute-start(f32[1,1024]{1,0:T(1,128)S(1)} %add.9), channel_id=1, source_target_pairs={{0,2},{1,3},{2,0},{3,1},{4,6},{5,7},{6,4},{7,5},{8,10},{9,11},{10,... | collective-permute-start | bytes 12296 | tf_op jit(solution)/shard_map/ppermute | solution.py:437
  51.5 5.1 %collective-permute-start.2 = (f32[1,1024]{1,0:T(1,128)S(1)}, f32[1,1024]{1,0:T(1,128)S(1)}, u32[]{:S(2)}, u32[]{:S(2)}) collective-permute-start(f32[1,1024]{1,0:T(1,128)S(1)} %add.10), channel_id=1, source_target_pairs={{0,4},{1,5},{2,6},{3,7},{4,0},{5,1},{6,2},{7,3},{8,12},{9,13},{10,... | collective-permute-start | bytes 12296 | tf_op jit(solution)/shard_map/ppermute | solution.py:437

commit v6 on v5

--- a/solution.py
+++ b/solution.py
@@ -66,7 +66,7 @@
         pltpu.make_async_copy(probe_any, probe_ref, few_sem.at[1]),
         pltpu.make_async_copy(steer_any, steer_ref, few_sem.at[2]),
     ]
-    cached = pltpu.make_async_copy(c_any, u_ref.at[:, 16:32, :], few_sem.at[3])
+    cached = pltpu.make_async_copy(c_any, u_ref.at[:, 32:48, :], few_sem.at[3])
     for copy in few:
         copy.start()
     for h in range(AHEAD):
@@ -96,9 +96,9 @@
         kv = tn(k_ref[h], v_ref[h] * final)
         both = tn(q_ref[h], jnp.concatenate([g * before, g * after], axis=1))
         here = slice(h * pieces, (h + 1) * pieces)
-        u_ref[here, 0:16, :] = both[:, D:].astype(BF16).reshape(pieces, PIECE, D)
-        u_ref[here, 32:48, :] = kv.astype(BF16).reshape(pieces, PIECE, D)
-        u_ref[here, 48:64, :] = both[:, :D].astype(BF16).reshape(pieces, PIECE, D)
+        u_ref[here, 16:32, :] = both[:, D:].astype(BF16).reshape(pieces, PIECE, D)
+        u_ref[here, 48:64, :] = kv.astype(BF16).reshape(pieces, PIECE, D)
+        u_ref[here, 0:16, :] = both[:, :D].astype(BF16).reshape(pieces, PIECE, D)
         if h == 0:
             cached.wait()
         copy = pltpu.make_async_copy(u_ref.at[here, 0:64, :], u_any.at[here, 0:64, :], out_sem.at[h])
@@ -164,7 +164,7 @@
 def scan_kernel(owner_any, v_any, w_any, steer_ref, owner_ref, v_ref, w_ref, in_sem, out_sem):
     blocks = v_ref.shape[0]
     fetched = [pltpu.make_async_copy(owner_any, owner_ref, in_sem.at[0])]
-    for n, rows in enumerate((slice(16, 48), slice(64, 72), slice(0, 16), slice(48, 64))):
+    for n, rows in enumerate((slice(16, 72), slice(0, 16))):
         fetched.append(pltpu.make_async_copy(v_any.at[:, rows, :], v_ref.at[:, rows, :], in_sem.at[n + 1]))
     for copy in fetched:
         copy.start()
@@ -178,29 +178,29 @@
 
     state = jnp.zeros((PIECE, D), F32)
     steer = jnp.zeros((8, D), F32)
-    for copy in fetched[:3]:
+    for copy in fetched[:2]:
         copy.wait()
     for b in range(blocks):
         here = group_place(b, blocks)
-        cached = v_ref[group_place(owner_ref[b], blocks), 16:32, :]
+        cached = v_ref[group_place(owner_ref[b], blocks), 32:48, :]
         w_ref[here, 0:16, :] = state.astype(BF16)
         w_ref[here, 16:32, :] = cached
-        added = v_ref[here, 32:48, :].astype(F32)
+        added = v_ref[here, 48:64, :].astype(F32)
         state = added + jnp.where(flag_of(b), cached.astype(F32), state)
         steer = steer + extra(b)
     first = pltpu.make_async_copy(w_ref.at[:, 0:32, :], w_any.at[:, 0:32, :], out_sem.at[0])
     first.start()
-    for copy in fetched[3:]:
+    for copy in fetched[2:]:
         copy.wait()
     state = jnp.zeros((PIECE, D), F32)
     for b in reversed(range(blocks)):
         here = group_place(b, blocks)
         flag = flag_of(b)
         w_ref[here, 32:48, :] = state.astype(BF16)
-        begun = (v_ref[here, 0:16, :].astype(F32) + state) * (1.0 / D)
+        begun = (v_ref[here, 16:32, :].astype(F32) + state) * (1.0 / D)
         slot = group_place(owner_ref[b], blocks)
         w_ref[slot, 48:64, :] = jnp.where(flag, begun, 0.0).astype(BF16)
-        state = v_ref[here, 48:64, :].astype(F32) + jnp.where(flag, 0.0, state)
+        state = v_ref[here, 0:16, :].astype(F32) + jnp.where(flag, 0.0, state)
     second = pltpu.make_async_copy(w_ref.at[:, 32:64, :], w_any.at[:, 32:64, :], out_sem.at[1])
     second.start()
     tokens = blocks * 1024
@@ -224,7 +224,7 @@
             pltpu.SMEM(owner.shape, jnp.int32),
             pltpu.VMEM(pieces.shape, BF16),
             pltpu.VMEM((blocks, 64, D), BF16),
-            pltpu.SemaphoreType.DMA((5,)),
+            pltpu.SemaphoreType.DMA((3,)),
             pltpu.SemaphoreType.DMA((2,)),
         ],
         compiler_params=pltpu.CompilerParams(vmem_limit_bytes=VMEM_BYTES),
@@ -234,7 +234,7 @@
 
 def local_kernel(
     start_any, q_any, k_any, v_any, g_any, part_any,
-    start_ref, q_ref, k_ref, v_ref, g_ref, part_ref, start_sem, in_sem, out_sem,
+    start_ref, q_ref, k_ref, v_ref, g_ref, sum_ref, part_ref, start_sem, in_sem, out_sem,
 ):
     heads, length, _ = q_ref.shape
     started = pltpu.make_async_copy(start_any, start_ref, start_sem)
@@ -273,18 +273,20 @@
             s = lo + lax.broadcasted_iota(jnp.int32, (STRIP, hi), 0)
             t = lax.broadcasted_iota(jnp.int32, (STRIP, hi), 1)
             keep = (t <= s) & (t >= jnp.where(s >= start, start, 0))
-            y = jnp.where(keep, nt(g_ref[h, lo:hi, :], v_ref[h, 0:hi, :]), 0.0).astype(BF16)
+            g = g_ref[h, lo:hi, :]
+            q = q_ref[h, lo:hi, :]
+            y = jnp.where(keep, nt(g, v_ref[h, 0:hi, :]), 0.0).astype(BF16)
             part_ref[0, h, lo:hi, :] = nn(y, k_ref[h, 0:hi, :]).astype(BF16)
-        for j in range(length // STRIP):
-            lo, hi = j * STRIP, (j + 1) * STRIP
-            rest = length - lo
-            t = lo + lax.broadcasted_iota(jnp.int32, (STRIP, rest), 0)
-            s = lo + lax.broadcasted_iota(jnp.int32, (STRIP, rest), 1)
-            keep = (t <= s) & (s < jnp.where(t < start, start, length))
-            yt = jnp.where(keep, nt(v_ref[h, lo:hi, :], g_ref[h, lo:length, :]), 0.0).astype(BF16)
-            part_ref[1, h, lo:hi, :] = nn(yt, q_ref[h, lo:length, :]).astype(BF16)
-            xt = jnp.where(keep, nt(k_ref[h, lo:hi, :], q_ref[h, lo:length, :]), 0.0).astype(BF16)
-            part_ref[2, h, lo:hi, :] = nn(xt, g_ref[h, lo:length, :]).astype(BF16)
+            x = jnp.where(keep, nt(q, k_ref[h, 0:hi, :]), 0.0).astype(BF16)
+            dk = tn(y, q)
+            dv = tn(x, g)
+            sum_ref[0, lo:hi, :] = dk[lo:]
+            sum_ref[1, lo:hi, :] = dv[lo:]
+            if i > 0:
+                sum_ref[0, 0:lo, :] += dk[:lo]
+                sum_ref[1, 0:lo, :] += dv[:lo]
+        part_ref[1, h] = sum_ref[0].astype(BF16)
+        part_ref[2, h] = sum_ref[1].astype(BF16)
         result(h).start()
 
     for h in range(heads):
@@ -304,6 +306,7 @@
         scratch_shapes=[pltpu.SMEM(session_start.shape, jnp.int32)]
         + [near] * 4
         + [
+            pltpu.VMEM((2, length, D), F32),
             pltpu.VMEM((3, heads, length, D), BF16),
             pltpu.SemaphoreType.DMA(()),
             pltpu.SemaphoreType.DMA((4, heads)),
@@ -338,7 +341,7 @@
 
     started = pltpu.make_async_copy(start_any, start_ref, start_sem)
     started.start()
-    for h in range(AHEAD):
+    for h in range(heads):
         states(h).start()
         fetch(h).start()
     copies = []
@@ -349,9 +352,6 @@
     for h in range(heads):
         fetch(h).wait()
         states(h).wait()
-        if h + AHEAD < heads:
-            states(h + AHEAD).start()
-            fetch(h + AHEAD).start()
         cache(h).start()
         copies.append(cache(h))
         columns = slice(h * D, (h + 1) * D)

time: 63.8 us -> 62.9 us (0.986)
  Pallas kernels: 25.9 us -> 25.1 us
    pallas_call x1, Pallas kernels: 5.02 us -> 4.16 us  [state_grads(): pl.pallas_call(state_kernel, in_specs=[hbm, vmem, vmem, vmem, hbm, hbm],...]
where the time goes in v6:
time: 62.9 us; the launch traced here: 62.5 us
  starting transfers between devices  26.1 us (41%)
  Pallas kernels  25.1 us (40%)
  waiting for transfers between devices  9.39 us (15%)
  between operations  1.38 us (2%)
    all_to_all x1, starting transfers between devices, shards(): lax.all_to_all(sent, 'seq', 0, 0, tiled=True, axis_index_groups=group)  13.3 us
    pallas_call x1, Pallas kernels, local_grads(): pl.pallas_call(local_kernel, in_specs=[hbm] * 5, out_specs=hbm, out_shape...  13.1 us
    all_to_all x1, starting transfers between devices, shards(): lax.all_to_all(scanned, 'seq', 0, 0, tiled=True, axis_index_groups=group)  9.93 us
    ppermute x3, waiting for transfers between devices, shards(): lax.ppermute(gate, 'head', [(i, i ^ step) for i in range(count)])  7.12 us
    pallas_call x1, Pallas kernels, block_sums(): pl.pallas_call(sums_kernel, in_specs=[hbm] * 8, out_specs=[hbm, vmem], ou...  5.25 us
    pallas_call x1, Pallas kernels, state_grads(): pl.pallas_call(state_kernel, in_specs=[hbm, vmem, vmem, vmem, hbm, hbm],...  4.16 us
    ppermute x3, starting transfers between devices, shards(): lax.ppermute(gate, 'head', [(i, i ^ step) for i in range(count)])  2.84 us
    pallas_call x1, Pallas kernels, scan_blocks(): pl.pallas_call(scan_kernel, in_specs=[hbm, hbm], out_specs=[hbm, vmem], o...  2.54 us
  transfers between devices with their start and end apart: 5, of which 5 were waited for; matrix products, arithmetic and copies ran while one was open for 1% of the time, Pallas kernels for 21%

profile of v6, /device:TPU:8, one launch (start us, length us, event | category | flops | bytes accessed | tf_op | source)
XLA Modules:
  0.0 62.5 jit_solution(11305920504661930619)
XLA Ops:
  1.3 5.3 %block_sums.1 = (bf16[32,72,128]{2,1,0:T(8,128)(2,1)}, f32[1,1024]{1,0:T(1,128)}) custom-call(s32[1]{0:T(128)S(6)} %copy.15.start_any, bf16[1024,512]{1,0:T(8,128)(2,1)} %q_any.3, bf16[1024,512]{1,0:T(8,128)(2,1)} %k_ref.1, bf16[1024,512]{1,0:T(8,128)(2,1)} %v_ref.1, bf16[1024,512]{1,0:T(8,128)(2,1)} %g_ref.1, bf16[32,16,128]{2,1,0:T(8,128)(2,1)} %bitcast.4, ...), custom_call_target="tpu_custom_call" | custom-call | flops 536870912 | bytes 4194304 | tf_op jit(solution)/shard_map/block_sums/pallas_call | solution.py:126
  6.5 13.3 %all-to-all-start = ((bf16[32,72,128]{2,1,0:T(8,128)(2,1)}), bf16[32,72,128]{2,1,0:T(8,128)(2,1)}, u32[]{:S(2)}, u32[]{:S(2)}) async-start(bf16[32,72,128]{2,1,0:T(8,128)(2,1)} %get-tuple-element.16), calls=%async_computation | async-start | bytes 1179648 | tf_op jit(solution)/shard_map/all_to_all | solution.py:426
  19.8 0.0 copy-start.3
  19.9 0.0 copy-start
  19.9 0.0 copy-start.1
  19.9 0.0 copy-start.2
  19.9 13.1 %local_grads.1.part_any = bf16[3,4,1024,128]{3,2,1,0:T(8,128)(2,1)} custom-call(s32[1]{0:T(128)S(6)} %copy.15.start_any, bf16[1024,512]{1,0:T(8,128)(2,1)} %q_any.3, bf16[1024,512]{1,0:T(8,128)(2,1)} %k_ref.1, bf16[1024,512]{1,0:T(8,128)(2,1)} %v_ref.1, bf16[1024,512]{1,0:T(8,128)(2,1)} %g_ref.1), custom_call_target="tpu_custom_call" | custom-call | flops 8589934592 | bytes 10485760 | tf_op jit(solution)/shard_map/local_grads/pallas_call | solution.py:301
  33.0 1.1 %all-to-all-done.v_any = bf16[32,72,128]{2,1,0:T(8,128)(2,1)} async-done(((bf16[32,72,128]{2,1,0:T(8,128)(2,1)}), bf16[32,72,128]{2,1,0:T(8,128)(2,1)}, u32[]{:S(2)}, u32[]{:S(2)}) %all-to-all-start) | async-done | bytes 589856 | tf_op jit(solution)/shard_map/all_to_all | solution.py:426
  34.1 2.5 %scan_blocks.1 = (bf16[32,64,128]{2,1,0:T(8,128)(2,1)}, f32[4,128]{1,0:T(4,128)}) custom-call(s32[32]{0:T(128)} %owner_any.1, bf16[32,72,128]{2,1,0:T(8,128)(2,1)} %all-to-all-done.v_any), custom_call_target="tpu_custom_call" | custom-call | tf_op jit(solution)/shard_map/scan_blocks/pallas_call | solution.py:215
  36.7 9.9 %all-to-all-start.1 = ((bf16[32,64,128]{2,1,0:T(8,128)(2,1)}), bf16[32,64,128]{2,1,0:T(8,128)(2,1)}, u32[]{:S(2)}, u32[]{:S(2)}) async-start(bf16[32,64,128]{2,1,0:T(8,128)(2,1)} %get-tuple-element.19), calls=%async_computation.1 | async-start | bytes 1048576 | tf_op jit(solution)/shard_map/all_to_all | solution.py:430
  46.6 0.0 copy-done.3
  46.6 0.1 collective-permute-start
  46.7 1.2 %collective-permute-done = f32[1,1024]{1,0:T(1,128)S(1)} collective-permute-done((f32[1,1024]{1,0:T(1,128)S(1)}, f32[1,1024]{1,0:T(1,128)S(1)}, u32[]{:S(2)}, u32[]{:S(2)}) %collective-permute-start) | collective-permute-done | bytes 4128 | tf_op jit(solution)/shard_map/ppermute | solution.py:437
  47.9 0.5 collective-permute-start.1
  48.4 3.2 %collective-permute-done.1 = f32[1,1024]{1,0:T(1,128)S(1)} collective-permute-done((f32[1,1024]{1,0:T(1,128)S(1)}, f32[1,1024]{1,0:T(1,128)S(1)}, u32[]{:S(2)}, u32[]{:S(2)}) %collective-permute-start.1) | collective-permute-done | bytes 4128 | tf_op jit(solution)/shard_map/ppermute | solution.py:437
  51.5 2.3 %collective-permute-start.2 = (f32[1,1024]{1,0:T(1,128)S(1)}, f32[1,1024]{1,0:T(1,128)S(1)}, u32[]{:S(2)}, u32[]{:S(2)}) collective-permute-start(f32[1,1024]{1,0:T(1,128)S(1)} %add.10), channel_id=1, source_target_pairs={{0,4},{1,5},{2,6},{3,7},{4,0},{5,1},{6,2},{7,3},{8,12},{9,13},{10,... | collective-permute-start | bytes 12296 | tf_op jit(solution)/shard_map/ppermute | solution.py:437
  53.8 2.8 %collective-permute-done.2 = f32[1,1024]{1,0:T(1,128)S(1)} collective-permute-done((f32[1,1024]{1,0:T(1,128)S(1)}, f32[1,1024]{1,0:T(1,128)S(1)}, u32[]{:S(2)}, u32[]{:S(2)}) %collective-permute-start.2) | collective-permute-done | bytes 4128 | tf_op jit(solution)/shard_map/ppermute | solution.py:437
  56.6 0.6 add.11
  57.2 1.1 %all-to-all-done.1.w_any = bf16[32,64,128]{2,1,0:T(8,128)(2,1)} async-done(((bf16[32,64,128]{2,1,0:T(8,128)(2,1)}), bf16[32,64,128]{2,1,0:T(8,128)(2,1)}, u32[]{:S(2)}, u32[]{:S(2)}) %all-to-all-start.1) | async-done | bytes 524320 | tf_op jit(solution)/shard_map/all_to_all | solution.py:430
  58.4 0.0 copy-done
  58.4 0.0 copy-done.1
  58.4 0.0 copy-done.2
  58.4 4.2 %state_grads.1 = (bf16[1024,512]{1,0:T(8,128)(2,1)}, bf16[1024,512]{1,0:T(8,128)(2,1)}, bf16[1024,512]{1,0:T(8,128)(2,1)}, bf16[32,16,128]{2,1,0:T(8,128)(2,1)}) custom-call(s32[1]{0:T(128)S(6)} %copy.15.start_any, bf16[1024,512]{1,0:T(8,128)(2,1)S(1)} %copy-done, bf16[1024,512]{1,0:T(8,128)(2,1)S(1)} %copy-done.1, bf16[1024,512]{1,0:T(8,128)(2,1)S(1)} %copy-done.2, ...), custom_call_target="tpu_custom_call" | custom-call | flops 536870912 | bytes 10485760 | tf_op jit(solution)/shard_map/state_grads/pallas_call | solution.py:384
  (2 shorter events, 0.0 us)
Async XLA Ops:
  6.5 27.6 %all-to-all-start = ((bf16[32,72,128]{2,1,0:T(8,128)(2,1)}), bf16[32,72,128]{2,1,0:T(8,128)(2,1)}, u32[]{:S(2)}, u32[]{:S(2)}) async-start(bf16[32,72,128]{2,1,0:T(8,128)(2,1)} %get-tuple-element.16), calls=%async_computation | async-start | bytes 1179648 | tf_op jit(solution)/shard_map/all_to_all | solution.py:426
  19.8 26.8 %copy-start.3 = (f32[1,1024]{1,0:T(1,128)S(1)}, f32[1,1024]{1,0:T(1,128)}, u32[]{:S(2)}) copy-start(f32[1,1024]{1,0:T(1,128)} %get-tuple-element.25) | copy-start | bytes 12292
  19.9 38.5 %copy-start = (bf16[1024,512]{1,0:T(8,128)(2,1)S(1)}, bf16[1024,512]{1,0:T(8,128)(2,1)}, u32[]{:S(2)}) copy-start(bf16[1024,512]{1,0:T(8,128)(2,1)} %k_ref.1) | copy-start | bytes 3145732
  19.9 38.5 %copy-start.1 = (bf16[1024,512]{1,0:T(8,128)(2,1)S(1)}, bf16[1024,512]{1,0:T(8,128)(2,1)}, u32[]{:S(2)}) copy-start(bf16[1024,512]{1,0:T(8,128)(2,1)} %v_ref.1) | copy-start | bytes 3145732
  19.9 38.5 %copy-start.2 = (bf16[1024,512]{1,0:T(8,128)(2,1)S(1)}, bf16[1024,512]{1,0:T(8,128)(2,1)}, u32[]{:S(2)}) copy-start(bf16[1024,512]{1,0:T(8,128)(2,1)} %g_ref.1) | copy-start | bytes 3145732
  36.7 21.7 %all-to-all-start.1 = ((bf16[32,64,128]{2,1,0:T(8,128)(2,1)}), bf16[32,64,128]{2,1,0:T(8,128)(2,1)}, u32[]{:S(2)}, u32[]{:S(2)}) async-start(bf16[32,64,128]{2,1,0:T(8,128)(2,1)} %get-tuple-element.19), calls=%async_computation.1 | async-start | bytes 1048576 | tf_op jit(solution)/shard_map/all_to_all | solution.py:430
  46.6 1.3 %collective-permute-start = (f32[1,1024]{1,0:T(1,128)S(1)}, f32[1,1024]{1,0:T(1,128)S(1)}, u32[]{:S(2)}, u32[]{:S(2)}) collective-permute-start(f32[1,1024]{1,0:T(1,128)S(1)} %copy-done.3), channel_id=1, source_target_pairs={{0,1},{1,0},{2,3},{3,2},{4,5},{5,4},{6,7},{7,6},{8,9},{9,8},{10,11... | collective-permute-start | bytes 12296 | tf_op jit(solution)/shard_map/ppermute | solution.py:437
  47.9 3.6 %collective-permute-start.1 = (f32[1,1024]{1,0:T(1,128)S(1)}, f32[1,1024]{1,0:T(1,128)S(1)}, u32[]{:S(2)}, u32[]{:S(2)}) collective-permute-start(f32[1,1024]{1,0:T(1,128)S(1)} %add.9), channel_id=1, source_target_pairs={{0,2},{1,3},{2,0},{3,1},{4,6},{5,7},{6,4},{7,5},{8,10},{9,11},{10,... | collective-permute-start | bytes 12296 | tf_op jit(solution)/shard_map/ppermute | solution.py:437
  51.5 5.1 %collective-permute-start.2 = (f32[1,1024]{1,0:T(1,128)S(1)}, f32[1,1024]{1,0:T(1,128)S(1)}, u32[]{:S(2)}, u32[]{:S(2)}) collective-permute-start(f32[1,1024]{1,0:T(1,128)S(1)} %add.10), channel_id=1, source_target_pairs={{0,4},{1,5},{2,6},{3,7},{4,0},{5,1},{6,2},{7,3},{8,12},{9,13},{10,... | collective-permute-start | bytes 12296 | tf_op jit(solution)/shard_map/ppermute | solution.py:437

commit v7 on v6

--- a/solution.py
+++ b/solution.py
@@ -14,6 +14,7 @@
 VMEM_BYTES = 60 << 20
 STATE_BYTES = 48 << 20
 AHEAD = 2
+NONE = 1e30
 F32 = jnp.float32
 BF16 = jnp.bfloat16
 
@@ -82,8 +83,7 @@
     low = (probe - high.astype(F32)).astype(BF16)
     steer = steer_ref[...].astype(F32)
     rows = lax.broadcasted_iota(jnp.int32, (8, D), 0)
-    flag = jnp.where(start < length, 1.0, 0.0).astype(F32)
-    tile = jnp.full((8, D), flag)
+    tile = jnp.zeros((8, D), F32)
     gate = jnp.zeros((heads, length), F32)
     sent = []
     for h in range(heads):
@@ -96,7 +96,8 @@
         kv = tn(k_ref[h], v_ref[h] * final)
         both = tn(q_ref[h], jnp.concatenate([g * before, g * after], axis=1))
         here = slice(h * pieces, (h + 1) * pieces)
-        u_ref[here, 16:32, :] = both[:, D:].astype(BF16).reshape(pieces, PIECE, D)
+        begun = jnp.where(start < length, both[:, D:], NONE)
+        u_ref[here, 16:32, :] = begun.astype(BF16).reshape(pieces, PIECE, D)
         u_ref[here, 48:64, :] = kv.astype(BF16).reshape(pieces, PIECE, D)
         u_ref[here, 0:16, :] = both[:, :D].astype(BF16).reshape(pieces, PIECE, D)
         if h == 0:
@@ -169,12 +170,9 @@
     for copy in fetched:
         copy.start()
 
-    def extra(b):
-        return v_ref[group_place(b, blocks), 64:72, :].astype(F32)
-
-    def flag_of(b):
-        row = extra(b)[4:5]
-        return jnp.broadcast_to(row, (PIECE, D)) > 0.5
+    def begun_of(b):
+        begun = v_ref[group_place(b, blocks), 16:32, :].astype(F32)
+        return begun, begun < 0.5 * NONE
 
     state = jnp.zeros((PIECE, D), F32)
     steer = jnp.zeros((8, D), F32)
@@ -186,8 +184,8 @@
         w_ref[here, 0:16, :] = state.astype(BF16)
         w_ref[here, 16:32, :] = cached
         added = v_ref[here, 48:64, :].astype(F32)
-        state = added + jnp.where(flag_of(b), cached.astype(F32), state)
-        steer = steer + extra(b)
+        state = added + jnp.where(begun_of(b)[1], cached.astype(F32), state)
+        steer = steer + v_ref[here, 64:72, :].astype(F32)
     first = pltpu.make_async_copy(w_ref.at[:, 0:32, :], w_any.at[:, 0:32, :], out_sem.at[0])
     first.start()
     for copy in fetched[2:]:
@@ -195,11 +193,11 @@
     state = jnp.zeros((PIECE, D), F32)
     for b in reversed(range(blocks)):
         here = group_place(b, blocks)
-        flag = flag_of(b)
+        begun, flag = begun_of(b)
         w_ref[here, 32:48, :] = state.astype(BF16)
-        begun = (v_ref[here, 16:32, :].astype(F32) + state) * (1.0 / D)
+        full = (begun + state) * (1.0 / D)
         slot = group_place(owner_ref[b], blocks)
-        w_ref[slot, 48:64, :] = jnp.where(flag, begun, 0.0).astype(BF16)
+        w_ref[slot, 48:64, :] = jnp.where(flag, full, 0.0).astype(BF16)
         state = v_ref[here, 0:16, :].astype(F32) + jnp.where(flag, 0.0, state)
     second = pltpu.make_async_copy(w_ref.at[:, 32:64, :], w_any.at[:, 32:64, :], out_sem.at[1])
     second.start()

time: 62.9 us -> 62.9 us (level)
  no operation moved by 1% of the time
where the time goes in v7:
time: 62.9 us; the launch traced here: 62.5 us
  starting transfers between devices  26.1 us (41%)
  Pallas kernels  25 us (40%)
  waiting for transfers between devices  9.39 us (15%)
  between operations  1.38 us (2%)
    all_to_all x1, starting transfers between devices, shards(): lax.all_to_all(sent, 'seq', 0, 0, tiled=True, axis_index_groups=group)  13.3 us
    pallas_call x1, Pallas kernels, local_grads(): pl.pallas_call(local_kernel, in_specs=[hbm] * 5, out_specs=hbm, out_shape...  13.1 us
    all_to_all x1, starting transfers between devices, shards(): lax.all_to_all(scanned, 'seq', 0, 0, tiled=True, axis_index_groups=group)  9.93 us
    ppermute x3, waiting for transfers between devices, shards(): lax.ppermute(gate, 'head', [(i, i ^ step) for i in range(count)])  7.13 us
    pallas_call x1, Pallas kernels, block_sums(): pl.pallas_call(sums_kernel, in_specs=[hbm] * 8, out_specs=[hbm, vmem], ou...  5.25 us
    pallas_call x1, Pallas kernels, state_grads(): pl.pallas_call(state_kernel, in_specs=[hbm, vmem, vmem, vmem, hbm, hbm],...  4.15 us
    ppermute x3, starting transfers between devices, shards(): lax.ppermute(gate, 'head', [(i, i ^ step) for i in range(count)])  2.83 us
    pallas_call x1, Pallas kernels, scan_blocks(): pl.pallas_call(scan_kernel, in_specs=[hbm, hbm], out_specs=[hbm, vmem], o...  2.53 us
  transfers between devices with their start and end apart: 5, of which 5 were waited for; matrix products, arithmetic and copies ran while one was open for 1% of the time, Pallas kernels for 21%

profile of v7, /device:TPU:8, one launch (start us, length us, event | category | flops | bytes accessed | tf_op | source)
XLA Modules:
  0.0 62.5 jit_solution(12528183655589559258)
XLA Ops:
  1.3 5.3 %block_sums.1 = (bf16[32,72,128]{2,1,0:T(8,128)(2,1)}, f32[1,1024]{1,0:T(1,128)}) custom-call(s32[1]{0:T(128)S(6)} %copy.15.start_any, bf16[1024,512]{1,0:T(8,128)(2,1)} %q_any.3, bf16[1024,512]{1,0:T(8,128)(2,1)} %k_ref.1, bf16[1024,512]{1,0:T(8,128)(2,1)} %v_ref.1, bf16[1024,512]{1,0:T(8,128)(2,1)} %g_ref.1, bf16[32,16,128]{2,1,0:T(8,128)(2,1)} %bitcast.4, ...), custom_call_target="tpu_custom_call" | custom-call | flops 536870912 | bytes 4194304 | tf_op jit(solution)/shard_map/block_sums/pallas_call | solution.py:127
  6.5 13.3 %all-to-all-start = ((bf16[32,72,128]{2,1,0:T(8,128)(2,1)}), bf16[32,72,128]{2,1,0:T(8,128)(2,1)}, u32[]{:S(2)}, u32[]{:S(2)}) async-start(bf16[32,72,128]{2,1,0:T(8,128)(2,1)} %get-tuple-element.16), calls=%async_computation | async-start | bytes 1179648 | tf_op jit(solution)/shard_map/all_to_all | solution.py:424
  19.9 0.0 copy-start.3
  19.9 0.0 copy-start
  19.9 0.0 copy-start.1
  19.9 0.0 copy-start.2
  19.9 13.1 %local_grads.1.part_any = bf16[3,4,1024,128]{3,2,1,0:T(8,128)(2,1)} custom-call(s32[1]{0:T(128)S(6)} %copy.15.start_any, bf16[1024,512]{1,0:T(8,128)(2,1)} %q_any.3, bf16[1024,512]{1,0:T(8,128)(2,1)} %k_ref.1, bf16[1024,512]{1,0:T(8,128)(2,1)} %v_ref.1, bf16[1024,512]{1,0:T(8,128)(2,1)} %g_ref.1), custom_call_target="tpu_custom_call" | custom-call | flops 8589934592 | bytes 10485760 | tf_op jit(solution)/shard_map/local_grads/pallas_call | solution.py:299
  33.0 1.1 %all-to-all-done.v_any = bf16[32,72,128]{2,1,0:T(8,128)(2,1)} async-done(((bf16[32,72,128]{2,1,0:T(8,128)(2,1)}), bf16[32,72,128]{2,1,0:T(8,128)(2,1)}, u32[]{:S(2)}, u32[]{:S(2)}) %all-to-all-start) | async-done | bytes 589856 | tf_op jit(solution)/shard_map/all_to_all | solution.py:424
  34.2 2.5 %scan_blocks.1 = (bf16[32,64,128]{2,1,0:T(8,128)(2,1)}, f32[4,128]{1,0:T(4,128)}) custom-call(s32[32]{0:T(128)} %owner_any.1, bf16[32,72,128]{2,1,0:T(8,128)(2,1)} %all-to-all-done.v_any), custom_call_target="tpu_custom_call" | custom-call | tf_op jit(solution)/shard_map/scan_blocks/pallas_call | solution.py:213
  36.7 9.9 %all-to-all-start.1 = ((bf16[32,64,128]{2,1,0:T(8,128)(2,1)}), bf16[32,64,128]{2,1,0:T(8,128)(2,1)}, u32[]{:S(2)}, u32[]{:S(2)}) async-start(bf16[32,64,128]{2,1,0:T(8,128)(2,1)} %get-tuple-element.19), calls=%async_computation.1 | async-start | bytes 1048576 | tf_op jit(solution)/shard_map/all_to_all | solution.py:428
  46.6 0.0 copy-done.3
  46.6 0.1 collective-permute-start
  46.7 1.2 %collective-permute-done = f32[1,1024]{1,0:T(1,128)S(1)} collective-permute-done((f32[1,1024]{1,0:T(1,128)S(1)}, f32[1,1024]{1,0:T(1,128)S(1)}, u32[]{:S(2)}, u32[]{:S(2)}) %collective-permute-start) | collective-permute-done | bytes 4128 | tf_op jit(solution)/shard_map/ppermute | solution.py:435
  47.9 0.4 collective-permute-start.1
  48.3 3.2 %collective-permute-done.1 = f32[1,1024]{1,0:T(1,128)S(1)} collective-permute-done((f32[1,1024]{1,0:T(1,128)S(1)}, f32[1,1024]{1,0:T(1,128)S(1)}, u32[]{:S(2)}, u32[]{:S(2)}) %collective-permute-start.1) | collective-permute-done | bytes 4128 | tf_op jit(solution)/shard_map/ppermute | solution.py:435
  51.5 2.3 %collective-permute-start.2 = (f32[1,1024]{1,0:T(1,128)S(1)}, f32[1,1024]{1,0:T(1,128)S(1)}, u32[]{:S(2)}, u32[]{:S(2)}) collective-permute-start(f32[1,1024]{1,0:T(1,128)S(1)} %add.10), channel_id=1, source_target_pairs={{0,4},{1,5},{2,6},{3,7},{4,0},{5,1},{6,2},{7,3},{8,12},{9,13},{10,... | collective-permute-start | bytes 12296 | tf_op jit(solution)/shard_map/ppermute | solution.py:435
  53.8 2.8 %collective-permute-done.2 = f32[1,1024]{1,0:T(1,128)S(1)} collective-permute-done((f32[1,1024]{1,0:T(1,128)S(1)}, f32[1,1024]{1,0:T(1,128)S(1)}, u32[]{:S(2)}, u32[]{:S(2)}) %collective-permute-start.2) | collective-permute-done | bytes 4128 | tf_op jit(solution)/shard_map/ppermute | solution.py:435
  56.6 0.6 add.11
  57.2 1.1 %all-to-all-done.1.w_any = bf16[32,64,128]{2,1,0:T(8,128)(2,1)} async-done(((bf16[32,64,128]{2,1,0:T(8,128)(2,1)}), bf16[32,64,128]{2,1,0:T(8,128)(2,1)}, u32[]{:S(2)}, u32[]{:S(2)}) %all-to-all-start.1) | async-done | bytes 524320 | tf_op jit(solution)/shard_map/all_to_all | solution.py:428
  58.3 0.0 copy-done
  58.3 0.0 copy-done.1
  58.3 0.0 copy-done.2
  58.4 4.2 %state_grads.1 = (bf16[1024,512]{1,0:T(8,128)(2,1)}, bf16[1024,512]{1,0:T(8,128)(2,1)}, bf16[1024,512]{1,0:T(8,128)(2,1)}, bf16[32,16,128]{2,1,0:T(8,128)(2,1)}) custom-call(s32[1]{0:T(128)S(6)} %copy.15.start_any, bf16[1024,512]{1,0:T(8,128)(2,1)S(1)} %copy-done, bf16[1024,512]{1,0:T(8,128)(2,1)S(1)} %copy-done.1, bf16[1024,512]{1,0:T(8,128)(2,1)S(1)} %copy-done.2, ...), custom_call_target="tpu_custom_call" | custom-call | flops 536870912 | bytes 10485760 | tf_op jit(solution)/shard_map/state_grads/pallas_call | solution.py:382
  (2 shorter events, 0.0 us)
Async XLA Ops:
  6.5 27.6 %all-to-all-start = ((bf16[32,72,128]{2,1,0:T(8,128)(2,1)}), bf16[32,72,128]{2,1,0:T(8,128)(2,1)}, u32[]{:S(2)}, u32[]{:S(2)}) async-start(bf16[32,72,128]{2,1,0:T(8,128)(2,1)} %get-tuple-element.16), calls=%async_computation | async-start | bytes 1179648 | tf_op jit(solution)/shard_map/all_to_all | solution.py:424
  19.9 26.8 %copy-start.3 = (f32[1,1024]{1,0:T(1,128)S(1)}, f32[1,1024]{1,0:T(1,128)}, u32[]{:S(2)}) copy-start(f32[1,1024]{1,0:T(1,128)} %get-tuple-element.25) | copy-start | bytes 12292
  19.9 38.5 %copy-start = (bf16[1024,512]{1,0:T(8,128)(2,1)S(1)}, bf16[1024,512]{1,0:T(8,128)(2,1)}, u32[]{:S(2)}) copy-start(bf16[1024,512]{1,0:T(8,128)(2,1)} %k_ref.1) | copy-start | bytes 3145732
  19.9 38.5 %copy-start.1 = (bf16[1024,512]{1,0:T(8,128)(2,1)S(1)}, bf16[1024,512]{1,0:T(8,128)(2,1)}, u32[]{:S(2)}) copy-start(bf16[1024,512]{1,0:T(8,128)(2,1)} %v_ref.1) | copy-start | bytes 3145732
  19.9 38.5 %copy-start.2 = (bf16[1024,512]{1,0:T(8,128)(2,1)S(1)}, bf16[1024,512]{1,0:T(8,128)(2,1)}, u32[]{:S(2)}) copy-start(bf16[1024,512]{1,0:T(8,128)(2,1)} %g_ref.1) | copy-start | bytes 3145732
  36.7 21.7 %all-to-all-start.1 = ((bf16[32,64,128]{2,1,0:T(8,128)(2,1)}), bf16[32,64,128]{2,1,0:T(8,128)(2,1)}, u32[]{:S(2)}, u32[]{:S(2)}) async-start(bf16[32,64,128]{2,1,0:T(8,128)(2,1)} %get-tuple-element.19), calls=%async_computation.1 | async-start | bytes 1048576 | tf_op jit(solution)/shard_map/all_to_all | solution.py:428
  46.6 1.3 %collective-permute-start = (f32[1,1024]{1,0:T(1,128)S(1)}, f32[1,1024]{1,0:T(1,128)S(1)}, u32[]{:S(2)}, u32[]{:S(2)}) collective-permute-start(f32[1,1024]{1,0:T(1,128)S(1)} %copy-done.3), channel_id=1, source_target_pairs={{0,1},{1,0},{2,3},{3,2},{4,5},{5,4},{6,7},{7,6},{8,9},{9,8},{10,11... | collective-permute-start | bytes 12296 | tf_op jit(solution)/shard_map/ppermute | solution.py:435
  47.9 3.6 %collective-permute-start.1 = (f32[1,1024]{1,0:T(1,128)S(1)}, f32[1,1024]{1,0:T(1,128)S(1)}, u32[]{:S(2)}, u32[]{:S(2)}) collective-permute-start(f32[1,1024]{1,0:T(1,128)S(1)} %add.9), channel_id=1, source_target_pairs={{0,2},{1,3},{2,0},{3,1},{4,6},{5,7},{6,4},{7,5},{8,10},{9,11},{10,... | collective-permute-start | bytes 12296 | tf_op jit(solution)/shard_map/ppermute | solution.py:435
  51.5 5.1 %collective-permute-start.2 = (f32[1,1024]{1,0:T(1,128)S(1)}, f32[1,1024]{1,0:T(1,128)S(1)}, u32[]{:S(2)}, u32[]{:S(2)}) collective-permute-start(f32[1,1024]{1,0:T(1,128)S(1)} %add.10), channel_id=1, source_target_pairs={{0,4},{1,5},{2,6},{3,7},{4,0},{5,1},{6,2},{7,3},{8,12},{9,13},{10,... | collective-permute-start | bytes 12296 | tf_op jit(solution)/shard_map/ppermute | solution.py:435
